TPU v7x, 32 devices: a whole 2x2x4 slice. The times are simulated.
32 devices in a mesh: blk: 32 (over z, y, x, core).
Axes of the slice: x: 2, y: 2, z: 4, core: 2. Of those that a mesh axis runs over, the one named last changes fastest.
Arguments:
- populations: float32 [1024, 19, 512], P('blk'), may hold values from 0 to 1, as said below
- coarse_faces: float32 [64, 2, 19, 64], P('blk'), may hold values from 0 to 1, as said below
- neighbors: int32 [1024, 6], P('blk'), may hold values from -1 to 1023, as said below
- interface: int32 [1024, 2], P('blk'), may hold values from -1 to 63, as said below
- solid: int32 [1024, 512], P('blk'), may hold values from 0 to 1, as said below
Outputs:
- advanced: float32 [1024, 19, 512], P('blk')
Inputs may be any that keep to these rules, and one draw needn't show every extreme that they name: `populations`: every entry is positive. `coarse_faces`: every entry is positive. `neighbors`: Symmetric: a is across face d of b exactly when b is across the opposite face of a. Blocks b with equal b // 32 share an owner. A block across a y or z face has the same owner; one across the +x (-x) face has the same owner or the next (previous) one. For each owner and each x direction at most 16 of its blocks have a neighbour with another owner, and some owner reaches 16 in each direction. The +y face of a block with interface[b, 0] >= 0 is -1 here. interface[b, 0] is owned by the next owner: interface[b, 0] // 2 == b // 32 + 1. interface[b, 1] is the quadrant, 0 to 3. Each pair of coarse block and quadrant appears at most once. `solid`: only cells with all three coordinates in 1..6 are wall cells.
All inputs are finite; a program needn't handle non-finite values.
Results may differ from a plain program's by a relative error of at most 0.0001.
Values sent between devices are 32-bit elements; how exact they have to be, the bound alone decides.
No kernel may reach another device: no remote copies, remote signals or barrier semaphores. Data moves between devices by JAX's collectives and lax.ppermute only.
A program may use at most 64 MiB of HBM per device.

v0:
```python
import jax
import jax.numpy as jnp
import numpy as np
from jax import lax
from jax.sharding import PartitionSpec as P


def shifted(shard, axis, by):
    peers = lax.axis_size(axis)
    pairs = [(i, i + by) for i in range(peers) if 0 <= i + by < peers]
    return lax.ppermute(shard, axis, pairs)


def velocity_list():
    return [
        [0, 0, 0],
        [1, 0, 0],
        [-1, 0, 0],
        [0, 1, 0],
        [0, -1, 0],
        [0, 0, 1],
        [0, 0, -1],
        [1, 1, 0],
        [-1, -1, 0],
        [1, -1, 0],
        [-1, 1, 0],
        [1, 0, 1],
        [-1, 0, -1],
        [1, 0, -1],
        [-1, 0, 1],
        [0, 1, 1],
        [0, -1, -1],
        [0, 1, -1],
        [0, -1, 1],
    ]


def opposite_list():
    return [0, 2, 1, 4, 3, 6, 5, 8, 7, 10, 9, 12, 11, 14, 13, 16, 15, 18, 17]


def build_relax():
    velocity_set = np.array(velocity_list())
    shear_rate = 1.0 / 0.6
    vel_x = velocity_set[:, 0] * 1.0
    vel_y = velocity_set[:, 1] * 1.0
    vel_z = velocity_set[:, 2] * 1.0
    speed_sq = vel_x * vel_x + vel_y * vel_y + vel_z * vel_z
    moment_rows = [
        np.ones(19),
        19.0 * speed_sq - 30.0,
        (21.0 * speed_sq * speed_sq - 53.0 * speed_sq + 24.0) / 2.0,
        vel_x,
        (5.0 * speed_sq - 9.0) * vel_x,
        vel_y,
        (5.0 * speed_sq - 9.0) * vel_y,
        vel_z,
        (5.0 * speed_sq - 9.0) * vel_z,
        3.0 * vel_x * vel_x - speed_sq,
        (3.0 * speed_sq - 5.0) * (3.0 * vel_x * vel_x - speed_sq),
        vel_y * vel_y - vel_z * vel_z,
        (3.0 * speed_sq - 5.0) * (vel_y * vel_y - vel_z * vel_z),
        vel_x * vel_y,
        vel_y * vel_z,
        vel_x * vel_z,
        (vel_y * vel_y - vel_z * vel_z) * vel_x,
        (vel_z * vel_z - vel_x * vel_x) * vel_y,
        (vel_x * vel_x - vel_y * vel_y) * vel_z,
    ]
    moments = np.stack(moment_rows)
    relax_rates = np.array(
        [
            0.0,
            1.19,
            1.4,
            0.0,
            1.2,
            0.0,
            1.2,
            0.0,
            1.2,
            shear_rate,
            1.4,
            shear_rate,
            1.4,
            shear_rate,
            shear_rate,
            shear_rate,
            1.98,
            1.98,
            1.98,
        ]
    )
    row_norms = np.sum(moments * moments, axis=1)
    return moments.T @ ((relax_rates / row_norms)[:, None] * moments)


def build_crossing():
    velocity_set = velocity_list()
    crossing_list = []
    for face_dir in range(6):
        axis_pos = face_dir // 2
        sign_val = 1 if face_dir % 2 == 0 else -1
        members = [
            lattice_dir
            for lattice_dir in range(19)
            if velocity_set[lattice_dir][axis_pos] == -sign_val
        ]
        crossing_list.append(members)
    return crossing_list


def build_layers():
    layer_list = []
    for face_dir in range(6):
        axis_pos = face_dir // 2
        level = 7 if face_dir % 2 == 0 else 0
        others = [other_axis for other_axis in range(3) if other_axis != axis_pos]
        cell_list = []
        for first_coord in range(8):
            for second_coord in range(8):
                coords = [0, 0, 0]
                coords[axis_pos] = level
                coords[others[0]] = first_coord
                coords[others[1]] = second_coord
                cell_list.append(64 * coords[0] + 8 * coords[1] + coords[2])
        layer_list.append(np.array(cell_list, dtype=np.int32))
    return layer_list


def build_sources():
    velocity_set = velocity_list()
    side_table = np.full((19, 512), -1, dtype=np.int32)
    ghost_table = np.zeros((19, 512), dtype=np.int32)
    for lattice_dir in range(19):
        for cell in range(512):
            coords = [cell // 64, cell // 8 % 8, cell % 8]
            source = [
                coords[axis_pos] - velocity_set[lattice_dir][axis_pos] for axis_pos in range(3)
            ]
            outside = [
                axis_pos for axis_pos in range(3) if source[axis_pos] < 0 or source[axis_pos] > 7
            ]
            if len(outside) == 1:
                axis_pos = outside[0]
                side_table[lattice_dir, cell] = 2 * axis_pos + (0 if source[axis_pos] > 7 else 1)
                others = [other_axis for other_axis in range(3) if other_axis != axis_pos]
                ghost_table[lattice_dir, cell] = 8 * source[others[0]] + source[others[1]]
            elif len(outside) > 1:
                side_table[lattice_dir, cell] = 6
    return (side_table, ghost_table)


def build_quadrants():
    quad_cells = np.zeros((4, 64), dtype=np.int32)
    for quad in range(4):
        for fine_i in range(8):
            for fine_k in range(8):
                quad_cells[quad, 8 * fine_i + fine_k] = (
                    8 * (4 * (quad // 2) + fine_i // 2) + 4 * (quad % 2) + fine_k // 2
                )
    return quad_cells


def build_offsets():
    velocity_set = velocity_list()
    return [
        int(
            64 * velocity_set[lattice_dir][0]
            + 8 * velocity_set[lattice_dir][1]
            + velocity_set[lattice_dir][2]
        )
        for lattice_dir in range(19)
    ]


def equilibrium(states):
    velocity_f32 = jnp.asarray(np.array(velocity_list()), dtype=jnp.float32)
    weight_f32 = jnp.asarray(
        np.array([1.0 / 3.0] + [1.0 / 18.0] * 6 + [1.0 / 36.0] * 12), dtype=jnp.float32
    )
    density = jnp.sum(states, axis=1)
    momentum = jnp.einsum("qa,mqn->man", velocity_f32, states, precision=lax.Precision.HIGHEST)
    velocity = momentum / density[:, None, :]
    project = jnp.einsum("qa,man->mqn", velocity_f32, velocity, precision=lax.Precision.HIGHEST)
    square = jnp.sum(velocity * velocity, axis=1)
    return (
        weight_f32[None, :, None]
        * density[:, None, :]
        * (1.0 + 3.0 * project + 4.5 * project * project - 1.5 * square[:, None, :])
    )


def collide(states):
    relax_matrix = jnp.asarray(build_relax(), dtype=jnp.float32)
    balance = equilibrium(states)
    return states - jnp.einsum(
        "pq,mqn->mpn", relax_matrix, states - balance, precision=lax.Precision.HIGHEST
    )


def layer_of(relaxed, face_dir):
    crossing_sets = build_crossing()
    layer_cells = build_layers()
    picked = jnp.take(relaxed, jnp.asarray(crossing_sets[face_dir], dtype=jnp.int32), axis=1)
    picked = jnp.take(picked, jnp.asarray(layer_cells[face_dir ^ 1], dtype=jnp.int32), axis=2)
    return picked.reshape(relaxed.shape[0], 320)


def interface_values(coarse_tiles):
    crossing_sets = build_crossing()
    coarse_ratio = 0.6 / 1.1
    total = coarse_tiles.shape[0]
    outputs = []
    for time_frac in (0.0, 0.5):
        blended = (1.0 - time_frac) * coarse_tiles[:, 0] + time_frac * coarse_tiles[:, 1]
        balance = equilibrium(blended)
        ghost_vals = balance + coarse_ratio * (blended - balance)
        chosen = jnp.take(ghost_vals, jnp.asarray(crossing_sets[2], dtype=jnp.int32), axis=1)
        outputs.append(chosen.reshape(total, 320))
    return jnp.stack(outputs, axis=1)


def spread_quadrant(picked, quadrant):
    quad_table = jnp.asarray(build_quadrants(), dtype=jnp.int32)
    total = picked.shape[0]
    ghost_view = picked.reshape(total, 2, 5, 64)
    cell_index = jnp.take(quad_table, quadrant, axis=0)
    cell_index = jnp.broadcast_to(cell_index[:, None, None, :], (total, 2, 5, 64))
    return jnp.take_along_axis(ghost_view, cell_index, axis=3).reshape(total, 2, 320)


def stream(relaxed, initial, ghosts, present, solid):
    crossing_sets = build_crossing()
    source_side, ghost_cell = build_sources()
    shift_offsets = build_offsets()
    opposite_dir = opposite_list()
    total = relaxed.shape[0]
    fluid = solid == 0
    ghost_view = ghosts.reshape(total, 6, 5, 64)
    pulled = []
    for lattice_dir in range(19):
        moved = jnp.roll(relaxed[:, lattice_dir], shift_offsets[lattice_dir], axis=1)
        usable = jnp.roll(fluid, shift_offsets[lattice_dir], axis=1)
        for face_dir in range(6):
            if lattice_dir in crossing_sets[face_dir]:
                slot_pos = crossing_sets[face_dir].index(lattice_dir)
                through = jnp.asarray(source_side[lattice_dir] == face_dir)[None, :]
                fetched = jnp.take(
                    ghost_view[:, face_dir, slot_pos], jnp.asarray(ghost_cell[lattice_dir]), axis=1
                )
                moved = jnp.where(through, fetched, moved)
                usable = jnp.where(through, present[:, face_dir : face_dir + 1], usable)
        edge_mask = jnp.asarray(source_side[lattice_dir] == 6)[None, :]
        usable = jnp.where(edge_mask, False, usable)
        pulled.append(jnp.where(usable, moved, relaxed[:, opposite_dir[lattice_dir]]))
    read = jnp.stack(pulled, axis=1)
    return jnp.where(fluid[:, None, :], read, initial)


def remote_faces(relaxed, neighbors, first_block, block_count):
    below_index = jnp.clip(neighbors[:, 1] - (first_block - block_count), 0, block_count - 1)
    above_index = jnp.clip(neighbors[:, 0] - (first_block + block_count), 0, block_count - 1)
    from_below = shifted(relaxed, "blk", 1)
    from_above = shifted(relaxed, "blk", -1)
    lower_ghost = jnp.take(layer_of(from_below, 1), below_index, axis=0)
    upper_ghost = jnp.take(layer_of(from_above, 0), above_index, axis=0)
    return (lower_ghost, upper_ghost)


def body(populations, coarse_faces, neighbors, interface, solid):
    block_count = populations.shape[0]
    coarse_count = coarse_faces.shape[0]
    position = lax.axis_index("blk")
    first_block = position * block_count
    received = shifted(coarse_faces, "blk", -1)
    coarse_vals = interface_values(received)
    coarse_local = jnp.clip(interface[:, 0] - (position + 1) * coarse_count, 0, coarse_count - 1)
    has_coarse = interface[:, 0] >= 0
    picked = jnp.take(coarse_vals, coarse_local, axis=0)
    fine_ghost = spread_quadrant(picked, interface[:, 1])
    face_ids = jnp.arange(6, dtype=jnp.int32)
    present = (neighbors >= 0) | (face_ids[None, :] == 2) & has_coarse[:, None]
    local_index = neighbors - first_block
    is_local = (local_index >= 0) & (local_index < block_count)
    local_clip = jnp.clip(local_index, 0, block_count - 1)
    current = populations
    for substep in range(2):
        relaxed = collide(current)
        layers = jnp.stack([layer_of(relaxed, face_dir) for face_dir in range(6)], axis=1)
        lower_ghost, upper_ghost = remote_faces(relaxed, neighbors, first_block, block_count)
        ghosts = []
        for face_dir in range(6):
            fetched = jnp.take(layers[:, face_dir], local_clip[:, face_dir], axis=0)
            if face_dir == 0:
                fetched = jnp.where(is_local[:, 0:1], fetched, upper_ghost)
            if face_dir == 1:
                fetched = jnp.where(is_local[:, 1:2], fetched, lower_ghost)
            if face_dir == 2:
                fetched = jnp.where(has_coarse[:, None], fine_ghost[:, substep], fetched)
            ghosts.append(fetched)
        current = stream(relaxed, populations, jnp.stack(ghosts, axis=1), present, solid)
    return current


def solution(mesh):
    placed = (
        P("blk", None, None),
        P("blk", None, None, None),
        P("blk", None),
        P("blk", None),
        P("blk", None),
    )
    return jax.shard_map(
        body, mesh=mesh, in_specs=placed, out_specs=P("blk", None, None), check_vma=False
    )
```

profile of v0, /device:TPU:23, one launch (start us, length us, event | category | flops | bytes accessed | tf_op | source)
XLA Modules:
  0.0 499.7 jit_solution(7644549550269582138)
XLA Ops:
  1.7 1.7 multiply_reduce_fusion.1
  5.9 2.3 fusion.4
  9.2 3.7 collective-permute-start
  12.9 1.9 collective-permute-start.1
  15.4 2.7 collective-permute-start.2
  36.4 1.9 copy.754
  38.4 2.2 gather_fusion.18
  45.4 1.9 copy.771
  47.3 2.2 gather_fusion.28
  51.2 1.9 copy.775
  53.8 2.2 gather_fusion.32
  70.5 1.9 copy.742
  72.5 2.3 gather_fusion.4
  77.1 1.9 copy.748
  84.6 2.0 copy.767
  86.6 2.3 gather_fusion.24
  114.9 2.3 gather_fusion.11
  125.3 156.5 %gather_fusion.2 = f32[20480]{0:T(1024)S(1)} fusion(f32[32,2,5,64]{3,2,0,1:T(8,128)S(1)} %broadcast_select_fusion.2, s32[20480]{0:T(1024)S(1)} %reshape.1140), kind=kCustom, calls=%fused_computation.112 | custom fusion | bytes 491520 | tf_op jit(solution)/shard_map/jit(take_along_axis)/gather | solution.py:230
  291.7 2.0 gather_fusion.6
  293.7 1.9 copy.744
  295.7 2.3 gather_fusion.7
  302.5 2.0 gather_fusion.13
  304.5 1.9 copy.750
  306.5 3.0 gather_fusion.14
  347.9 1.6 fusion.164
  349.5 2.2 multiply_reduce_fusion
  354.2 2.3 fusion
  357.3 1.9 collective-permute-start.4
  359.3 5.6 %collective-permute-start.3 = (f32[32,19,512]{2,0,1:T(8,128)S(1)}, f32[32,19,512]{2,0,1:T(8,128)}, u32[]{:S(2)}, u32[]{:S(2)}) collective-permute-start(f32[32,19,512]{2,0,1:T(8,128)S(1)} %bitcast_subtract_fusion), channel_id=1, source_target_pairs={{0,1},{1,2},{2,3},{3,4},{4,5},{5,6},{6,7},{7,8},{8,9},{9,10},{10,1... | collective-permute-start | bytes 3735560 | tf_op jit(solution)/shard_map/ppermute | solution.py:11
  367.7 1.9 copy.843
  369.7 2.3 gather_fusion.74
  373.2 2.9 copy.847
  376.1 2.3 gather_fusion.78
  380.4 1.9 copy.851
  382.4 2.3 gather_fusion.82
  386.6 1.9 copy.855
  388.5 2.3 gather_fusion.86
  394.5 2.9 copy.837
  397.4 3.0 gather_fusion.67
  400.4 1.9 copy.831
  402.4 2.3 gather_fusion.60
  443.1 2.0 gather_fusion.62
  445.0 1.9 copy.833
  447.0 2.3 gather_fusion.63
  453.3 2.0 gather_fusion.69
  455.3 1.9 copy.839
  457.2 3.0 gather_fusion.70
  496.6 2.6 broadcast_select_fusion
  (1027 shorter events, 229.6 us)
Async XLA Ops:
  8.3 11.1 %copy-start.88 = (s32[32,512]{1,0:T(8,128)S(1)}, s32[32,512]{1,0:T(8,128)}, u32[]{:S(2)}) copy-start(s32[32,512]{1,0:T(8,128)} %param.220) | copy-start | bytes 196612
  8.3 23.9 %copy-start.305 = (s32[5]{0:T(128)S(1)}, s32[5]{0:T(128)}, u32[]{:S(2)}) copy-start(s32[5]{0:T(128)} %constant.1183) | copy-start | bytes 64
  8.3 24.5 %copy-start.304 = (s32[64]{0:T(128)S(1)}, s32[64]{0:T(128)}, u32[]{:S(2)}) copy-start(s32[64]{0:T(128)} %constant.1184) | copy-start | bytes 772
  8.3 25.1 %copy-start.175 = (s32[32,6]{0,1:T(8,128)S(1)}, s32[32,6]{0,1:T(8,128)}, u32[]{:S(2)}) copy-start(s32[32,6]{0,1:T(8,128)} %param.218) | copy-start | bytes 2308
  8.3 25.7 %copy-start.297 = (s32[32,2]{0,1:T(2,128)S(1)}, s32[32,2]{0,1:T(2,128)}, u32[]{:S(2)}) copy-start(s32[32,2]{0,1:T(2,128)} %param.219) | copy-start | bytes 772
  8.3 26.3 %copy-start.303 = (s32[5]{0:T(128)S(1)}, s32[5]{0:T(128)}, u32[]{:S(2)}) copy-start(s32[5]{0:T(128)} %constant.1188) | copy-start | bytes 64
  8.3 26.8 %copy-start.292 = (s32[512]{0:T(512)S(1)}, s32[512]{0:T(512)}, u32[]{:S(2)}) copy-start(s32[512]{0:T(512)} %constant.1190) | copy-start | bytes 6148
  8.3 26.8 %copy-start.306 = (s32[5]{0:T(128)S(1)}, s32[5]{0:T(128)}, u32[]{:S(2)}) copy-start(s32[5]{0:T(128)} %constant.1191) | copy-start | bytes 64
  9.2 282.5 %collective-permute-start = (f32[32,19,512]{2,0,1:T(8,128)S(1)}, f32[32,19,512]{2,0,1:T(8,128)}, u32[]{:S(2)}, u32[]{:S(2)}) collective-permute-start(f32[32,19,512]{2,0,1:T(8,128)S(1)} %bitcast_subtract_fusion.1), channel_id=1, source_target_pairs={{0,1},{1,2},{2,3},{3,4},{4,5},{5,6},{6,7},{7,8},{8,9},{9,10},{10,1... | collective-permute-start | bytes 3735560 | tf_op jit(solution)/shard_map/ppermute | solution.py:11
  12.9 289.7 %collective-permute-start.1 = (f32[32,19,512]{2,0,1:T(8,128)S(1)}, f32[32,19,512]{2,0,1:T(8,128)}, u32[]{:S(2)}, u32[]{:S(2)}) collective-permute-start(f32[32,19,512]{2,0,1:T(8,128)S(1)} %bitcast_subtract_fusion.1), channel_id=1, source_target_pairs={{1,0},{2,1},{3,2},{4,3},{5,4},{6,5},{7,6},{8,7},{9,8},{10,9},{11,1... | collective-permute-start | bytes 3735560 | tf_op jit(solution)/shard_map/ppermute | solution.py:11
  15.4 102.5 %collective-permute-start.2 = (f32[2,2,19,64]{3,2,0,1:T(8,128)}, f32[2,2,19,64]{3,2,0,1:T(8,128)}, u32[]{:S(2)}, u32[]{:S(2)}) collective-permute-start(f32[2,2,19,64]{3,2,0,1:T(8,128)} %copy.758), channel_id=1, source_target_pairs={{1,0},{2,1},{3,2},{4,3},{5,4},{6,5},{7,6},{8,7},{9,8},{10,9},{11,1... | collective-permute-start | bytes 58376 | tf_op jit(solution)/shard_map/ppermute | solution.py:11
  34.0 7.5 %copy-start.216 = (pred[32]{0:T(512)(128)(4,1)}, pred[32]{0:T(512)(128)(4,1)S(1)}, u32[]{:S(2)}) copy-start(pred[32]{0:T(512)(128)(4,1)S(1)} %get-tuple-element.190) | copy-start | bytes 100
  34.0 16.4 %copy-start.212 = (pred[32]{0:T(512)(128)(4,1)}, pred[32]{0:T(512)(128)(4,1)S(1)}, u32[]{:S(2)}) copy-start(pred[32]{0:T(512)(128)(4,1)S(1)} %get-tuple-element.186) | copy-start | bytes 100
  56.1 11.1 %copy-start.288 = (s32[512]{0:T(512)S(1)}, s32[512]{0:T(512)}, u32[]{:S(2)}) copy-start(s32[512]{0:T(512)} %constant.1198) | copy-start | bytes 6148
  56.1 11.1 %copy-start.293 = (s32[32]{0:T(128)S(1)}, s32[32]{0:T(128)}, u32[]{:S(2)}) copy-start(s32[32]{0:T(128)} %get-tuple-element.189) | copy-start | bytes 388
  56.1 11.7 %copy-start.286 = (s32[512]{0:T(512)S(1)}, s32[512]{0:T(512)}, u32[]{:S(2)}) copy-start(s32[512]{0:T(512)} %constant.1204) | copy-start | bytes 6148
  56.2 11.7 %copy-start.287 = (s32[512]{0:T(512)S(1)}, s32[512]{0:T(512)}, u32[]{:S(2)}) copy-start(s32[512]{0:T(512)} %constant.1206) | copy-start | bytes 6148
  56.2 12.3 %copy-start.284 = (s32[512]{0:T(512)S(1)}, s32[512]{0:T(512)}, u32[]{:S(2)}) copy-start(s32[512]{0:T(512)} %constant.1208) | copy-start | bytes 6148
  56.2 12.3 %copy-start.285 = (s32[512]{0:T(512)S(1)}, s32[512]{0:T(512)}, u32[]{:S(2)}) copy-start(s32[512]{0:T(512)} %constant.1210) | copy-start | bytes 6148
  56.2 12.9 %copy-start.282 = (s32[512]{0:T(512)S(1)}, s32[512]{0:T(512)}, u32[]{:S(2)}) copy-start(s32[512]{0:T(512)} %constant.1212) | copy-start | bytes 6148
  56.2 12.8 %copy-start.283 = (s32[512]{0:T(512)S(1)}, s32[512]{0:T(512)}, u32[]{:S(2)}) copy-start(s32[512]{0:T(512)} %constant.1214) | copy-start | bytes 6148
  56.2 12.8 %copy-start.280 = (s32[512]{0:T(512)S(1)}, s32[512]{0:T(512)}, u32[]{:S(2)}) copy-start(s32[512]{0:T(512)} %constant.1216) | copy-start | bytes 6148
  56.2 12.8 %copy-start.281 = (s32[512]{0:T(512)S(1)}, s32[512]{0:T(512)}, u32[]{:S(2)}) copy-start(s32[512]{0:T(512)} %constant.1218) | copy-start | bytes 6148
  56.2 12.9 %copy-start.278 = (s32[512]{0:T(512)S(1)}, s32[512]{0:T(512)}, u32[]{:S(2)}) copy-start(s32[512]{0:T(512)} %constant.1220) | copy-start | bytes 6148
  56.3 12.9 %copy-start.279 = (s32[512]{0:T(512)S(1)}, s32[512]{0:T(512)}, u32[]{:S(2)}) copy-start(s32[512]{0:T(512)} %constant.1222) | copy-start | bytes 6148
  56.3 12.9 %copy-start.276 = (s32[512]{0:T(512)S(1)}, s32[512]{0:T(512)}, u32[]{:S(2)}) copy-start(s32[512]{0:T(512)} %constant.1224) | copy-start | bytes 6148
  56.3 12.9 %copy-start.277 = (s32[512]{0:T(512)S(1)}, s32[512]{0:T(512)}, u32[]{:S(2)}) copy-start(s32[512]{0:T(512)} %constant.1226) | copy-start | bytes 6148
  68.4 24.3 %copy-start.142 = (s32[1024]{0:T(1024)}, s32[1024]{0:T(1024)S(1)}, u32[]{:S(2)}) copy-start(s32[1024]{0:T(1024)S(1)} %get-tuple-element.235) | copy-start | bytes 12292
  69.0 25.4 %copy-start.130 = (s32[1024]{0:T(1024)}, s32[1024]{0:T(1024)S(1)}, u32[]{:S(2)}) copy-start(s32[1024]{0:T(1024)S(1)} %get-tuple-element.232) | copy-start | bytes 12292
  69.1 27.2 %copy-start.126 = (s32[1024]{0:T(1024)}, s32[1024]{0:T(1024)S(1)}, u32[]{:S(2)}) copy-start(s32[1024]{0:T(1024)S(1)} %get-tuple-element.231) | copy-start | bytes 12292
  69.1 29.0 %copy-start.122 = (s32[1024]{0:T(1024)}, s32[1024]{0:T(1024)S(1)}, u32[]{:S(2)}) copy-start(s32[1024]{0:T(1024)S(1)} %get-tuple-element.230) | copy-start | bytes 12292
  69.1 30.7 %copy-start.118 = (s32[1024]{0:T(1024)}, s32[1024]{0:T(1024)S(1)}, u32[]{:S(2)}) copy-start(s32[1024]{0:T(1024)S(1)} %get-tuple-element.229) | copy-start | bytes 12292
  69.1 32.5 %copy-start.115 = (s32[1024]{0:T(1024)}, s32[1024]{0:T(1024)S(1)}, u32[]{:S(2)}) copy-start(s32[1024]{0:T(1024)S(1)} %get-tuple-element.228) | copy-start | bytes 12292
  69.2 36.0 %copy-start.152 = (s32[1024]{0:T(1024)}, s32[1024]{0:T(1024)S(1)}, u32[]{:S(2)}) copy-start(s32[1024]{0:T(1024)S(1)} %get-tuple-element.227) | copy-start | bytes 12292
  69.2 37.7 %copy-start.149 = (s32[1024]{0:T(1024)}, s32[1024]{0:T(1024)S(1)}, u32[]{:S(2)}) copy-start(s32[1024]{0:T(1024)S(1)} %get-tuple-element.226) | copy-start | bytes 12292
  69.2 41.2 %copy-start.147 = (s32[1024]{0:T(1024)}, s32[1024]{0:T(1024)S(1)}, u32[]{:S(2)}) copy-start(s32[1024]{0:T(1024)S(1)} %get-tuple-element.225) | copy-start | bytes 12292
  69.2 43.0 %copy-start.144 = (s32[1024]{0:T(1024)}, s32[1024]{0:T(1024)S(1)}, u32[]{:S(2)}) copy-start(s32[1024]{0:T(1024)S(1)} %get-tuple-element.224) | copy-start | bytes 12292
  111.5 7.2 %copy-start.191 = (f32[19,3,1]{0,1,2:T(4,128)S(1)}, f32[19,3,1]{0,1,2:T(4,128)}, u32[]{:S(2)}) copy-start(f32[19,3,1]{0,1,2:T(4,128)} %constant.1279) | copy-start | bytes 688
  111.5 8.2 %copy-start.269 = (f32[19]{0:T(128)S(1)}, f32[19]{0:T(128)}, u32[]{:S(2)}) copy-start(f32[19]{0:T(128)} %constant.176.clone) | copy-start | bytes 232
  114.0 11.1 %copy-start.275 = (pred[32]{0:T(512)(128)(4,1)S(1)}, pred[32]{0:T(512)(128)(4,1)}, u32[]{:S(2)}) copy-start(pred[32]{0:T(512)(128)(4,1)} %get-tuple-element.22) | copy-start | bytes 100
  125.2 156.7 %copy-start.52 = (s32[32,320]{1,0:T(8,128)S(1)}, s32[32,320]{1,0:T(8,128)}, u32[]{:S(2)}) copy-start(s32[32,320]{1,0:T(8,128)} %broadcast_in_dim.1214) | copy-start | bytes 122884
  125.2 156.7 %copy-start.53 = (s32[32,320]{1,0:T(8,128)S(1)}, s32[32,320]{1,0:T(8,128)}, u32[]{:S(2)}) copy-start(s32[32,320]{1,0:T(8,128)} %broadcast_in_dim.1217) | copy-start | bytes 122884
  125.2 157.4 %copy-start.188 = (pred[32]{0:T(512)(128)(4,1)S(1)}, pred[32]{0:T(512)(128)(4,1)}, u32[]{:S(2)}) copy-start(pred[32]{0:T(512)(128)(4,1)} %get-tuple-element.207) | copy-start | bytes 100
  125.2 157.3 %copy-start.214 = (pred[32]{0:T(512)(128)(4,1)S(1)}, pred[32]{0:T(512)(128)(4,1)}, u32[]{:S(2)}) copy-start(pred[32]{0:T(512)(128)(4,1)} %get-tuple-element.188) | copy-start | bytes 100
  125.3 157.6 %copy-start.186 = (s32[1024]{0:T(1024)S(1)}, s32[1024]{0:T(1024)}, u32[]{:S(2)}) copy-start(s32[1024]{0:T(1024)} %get-tuple-element.242) | copy-start | bytes 12292
  357.3 95.9 %collective-permute-start.4 = (f32[32,19,512]{2,0,1:T(8,128)S(1)}, f32[32,19,512]{2,0,1:T(8,128)}, u32[]{:S(2)}, u32[]{:S(2)}) collective-permute-start(f32[32,19,512]{2,0,1:T(8,128)S(1)} %bitcast_subtract_fusion), channel_id=1, source_target_pairs={{1,0},{2,1},{3,2},{4,3},{5,4},{6,5},{7,6},{8,7},{9,8},{10,9},{11,1... | collective-permute-start | bytes 3735560 | tf_op jit(solution)/shard_map/ppermute | solution.py:11
  359.3 83.8 %collective-permute-start.3 = (f32[32,19,512]{2,0,1:T(8,128)S(1)}, f32[32,19,512]{2,0,1:T(8,128)}, u32[]{:S(2)}, u32[]{:S(2)}) collective-permute-start(f32[32,19,512]{2,0,1:T(8,128)S(1)} %bitcast_subtract_fusion), channel_id=1, source_target_pairs={{0,1},{1,2},{2,3},{3,4},{4,5},{5,6},{6,7},{7,8},{8,9},{9,10},{10,1... | collective-permute-start | bytes 3735560 | tf_op jit(solution)/shard_map/ppermute | solution.py:11
  392.3 13.9 %copy-start.8 = (f32[32,512]{1,0:T(8,128)}, f32[32,512]{1,0:T(8,128)S(1)}, u32[]{:S(2)}) copy-start(f32[32,512]{1,0:T(8,128)S(1)} %get-tuple-element.60) | copy-start | bytes 196612
  (264 other events, 1087.8 us)
where the time goes:
time: 508 us; the launch traced here: 500 us
  local copies, waits for them, and re-layouts  389 us (77%)
  other arithmetic  74.5 us (15%)
  starting transfers between devices  15.9 us (3%)
  matrix products  15.3 us (3%)
  between operations  5.19 us (1%)
    gather x3, local copies, waits for them, and re-layouts, spread_quadrant(): jnp.take_along_axis(ghost_view, cell_index, axis=3).reshape(total, 2, 320)  158 us
    gather x120, local copies, waits for them, and re-layouts, stream(): jnp.take(ghost_view[:, face_dir, slot_pos], jnp.asarray(ghost_cell[lattic...  94.5 us
    gather x32, local copies, waits for them, and re-layouts, layer_of(): jnp.take(relaxed, jnp.asarray(crossing_sets[face_dir], dtype=jnp.int32),...  50.4 us
    gather x26, local copies, waits for them, and re-layouts, layer_of(): jnp.take(picked, jnp.asarray(layer_cells[face_dir ^ 1], dtype=jnp.int32),...  40.3 us
    unnamed x16, other arithmetic  18.8 us
    squeeze x16, other arithmetic, stream(): relaxed[:, lattice_dir]  16.8 us
    ppermute x5, starting transfers between devices, shifted(): return lax.ppermute(shard, axis, pairs)  15.9 us
    slice x18, local copies, waits for them, and re-layouts, stream(): usable = jnp.roll(fluid, shift_offsets[lattice_dir], axis=1)  12.2 us
  transfers between devices with their start and end apart: 5, of which 0 were waited for; matrix products, arithmetic and copies ran while one was open for 74% of the time, Pallas kernels for 0%

commit v1 on v0

v1 whole, which is shorter than its diff:
```python
import jax
import jax.numpy as jnp
import numpy as np
from jax import lax
from jax.experimental import pallas as pl
from jax.experimental.pallas import tpu as pltpu
from jax.sharding import PartitionSpec as P

F32, BF16, I32 = jnp.float32, jnp.bfloat16, jnp.int32
LANES = 128
VEL = [
    (0, 0, 0),
    (1, 0, 0), (-1, 0, 0), (0, 1, 0), (0, -1, 0), (0, 0, 1), (0, 0, -1),
    (1, 1, 0), (-1, -1, 0), (1, -1, 0), (-1, 1, 0),
    (1, 0, 1), (-1, 0, -1), (1, 0, -1), (-1, 0, 1),
    (0, 1, 1), (0, -1, -1), (0, 1, -1), (0, -1, 1),
]
Q = len(VEL)
OPP = [VEL.index((-x, -y, -z)) for x, y, z in VEL]
CROSSING = [
    [q for q in range(Q) if VEL[q][d // 2] == (-1 if d % 2 == 0 else 1)] for d in range(6)
]


def rates():
    v = np.array(VEL) * 1.0
    x, y, z = v[:, 0], v[:, 1], v[:, 2]
    s = x * x + y * y + z * z
    rows = [
        np.ones(19), 19 * s - 30, (21 * s * s - 53 * s + 24) / 2,
        x, (5 * s - 9) * x, y, (5 * s - 9) * y, z, (5 * s - 9) * z,
        3 * x * x - s, (3 * s - 5) * (3 * x * x - s),
        y * y - z * z, (3 * s - 5) * (y * y - z * z),
        x * y, y * z, x * z,
        (y * y - z * z) * x, (z * z - x * x) * y, (x * x - y * y) * z,
    ]
    norms = (np.stack(rows) ** 2).sum(1)
    w = 1.0 / 0.6
    relax = np.array([0, 1.19, 1.4, 0, 1.2, 0, 1.2, 0, 1.2, w, 1.4, w, 1.4, w, w, w, 1.98, 1.98, 1.98])
    return [float(c) for c in relax / norms]


def collide(f):
    c = rates()
    s = {q: f[q] + f[q + 1] for q in range(1, 19, 2)}
    d = {q: f[q] - f[q + 1] for q in range(1, 19, 2)}
    a, b, g = s[7] + s[9], s[11] + s[13], s[15] + s[17]
    s1, s2 = s[1] + (s[3] + s[5]), a + b + g
    rho = f[0] + s1 + s2
    ax1, ax2 = d[7] + d[9], d[11] + d[13]
    ay1, ay2 = d[7] - d[9], d[15] + d[17]
    az1, az2 = d[11] - d[13], d[15] - d[17]
    ax, ay, az = ax1 + ax2, ay1 + ay2, az1 + az2
    jx, jy, jz = d[1] + ax, d[3] + ay, d[5] + az
    inv = 1.0 / rho
    ux, uy, uz = jx * inv, jy * inv, jz * inv
    xx, yy, zz = jx * ux, jy * uy, jz * uz
    jj = xx + yy + zz
    r1 = (19 * c[1]) * (s2 - f[0] - jj)
    r2 = c[2] * (9 * f[0] - 7 * s1 - 2 * s2 + 5.5 * jj)
    t1, t2, pe = 2 * s[1] - (s[3] + s[5]), a + b - 2 * g, 3 * xx - jj
    v1, v2, we = s[3] - s[5], a - b, yy - zz
    r9, r10 = c[9] * (t1 + t2 - pe), c[10] * (t2 - 2 * t1 + 0.5 * pe)
    r11, r12 = c[11] * (v1 + v2 - we), c[12] * (v2 - 2 * v1 + 0.5 * we)
    r13 = c[13] * (s[7] - s[9] - jx * uy)
    r14 = c[14] * (s[15] - s[17] - jy * uz)
    r15 = c[15] * (s[11] - s[13] - jx * uz)
    r4 = (c[4] * 5 / 3) * (ax - 2 * d[1])
    r6 = (c[6] * 5 / 3) * (ay - 2 * d[3])
    r8 = (c[8] * 5 / 3) * (az - 2 * d[5])
    r16, r17, r18 = c[16] * (ax1 - ax2), c[17] * (ay2 - ay1), c[18] * (az1 - az2)
    ea, eb = -11 * r1 - 4 * r2, 8 * r1 + r2
    a9, a11 = r9 - 2 * r10, r11 - 2 * r12
    b9, b11 = r9 + r10, r11 + r12
    exy, exz, eyz = eb + b9 + b11, eb + b9 - b11, eb - 2 * b9
    even = {
        1: ea + 2 * a9, 3: ea - a9 + a11, 5: ea - a9 - a11,
        7: exy + r13, 9: exy - r13, 11: exz + r15, 13: exz - r15, 15: eyz + r14, 17: eyz - r14,
    }
    odd = {
        1: -4 * r4, 3: -4 * r6, 5: -4 * r8,
        7: (r4 + r6) + (r16 - r17), 9: (r4 - r6) + (r16 + r17),
        11: (r4 + r8) - (r16 - r18), 13: (r4 - r8) - (r16 + r18),
        15: (r6 + r8) + (r17 - r18), 17: (r6 - r8) + (r17 + r18),
    }
    out = [f[0] + 30 * r1 - 12 * r2]
    for q in range(1, 19, 2):
        out += [f[q] - even[q] - odd[q], f[q + 1] - even[q] + odd[q]]
    return out


def feq(h):
    rho = h[0]
    for q in range(1, Q):
        rho = rho + h[q]
    safe = jnp.where(rho > 0, rho, 1.0)
    u = []
    for axis in range(3):
        m = None
        for q in range(Q):
            if VEL[q][axis]:
                t = h[q] if VEL[q][axis] > 0 else -h[q]
                m = t if m is None else m + t
        u.append(m / safe)
    sq = u[0] * u[0] + u[1] * u[1] + u[2] * u[2]
    out = {}
    for q in CROSSING[2]:
        p = None
        for axis in range(3):
            if VEL[q][axis]:
                t = u[axis] if VEL[q][axis] > 0 else -u[axis]
                p = t if p is None else p + t
        n = sum(abs(e) for e in VEL[q])
        w = 1.0 / 18.0 if n == 1 else 1.0 / 36.0
        out[q] = w * rho * (1.0 + 3.0 * p + 4.5 * p * p - 1.5 * sq)
    return out


def lanes(rows):
    l = lax.broadcasted_iota(I32, (rows, LANES), 1)
    return l >= 64, (l >> 3) & 7, l & 7


def split(x):
    hi = x.astype(BF16)
    lo = (x - hi.astype(F32)).astype(BF16)
    return jnp.concatenate([hi, lo], axis=0)


def dot(a, b):
    return jnp.dot(a, b, preferred_element_type=F32)


def select_rows(row, offset, count):
    r = lax.broadcasted_iota(I32, (count, row.shape[1]), 0)
    hot = jnp.where(r == row - offset, 1.0, 0.0).astype(BF16)
    return jnp.concatenate([hot, hot], axis=1)


def spread_rows(flags):
    n = flags.shape[1]
    eye = lax.broadcasted_iota(I32, (n, n), 0) == lax.broadcasted_iota(I32, (n, n), 1)
    diag = jnp.where(eye, flags.astype(F32), 0.0).astype(BF16)
    return dot(diag, jnp.ones((n, LANES), BF16))


def sources(q, t, tiles, outer, half):
    ex = VEL[q][0]
    if ex == 0:
        return tiles[t]
    n = t - ex
    other = tiles[n] if 0 <= n < len(tiles) else outer
    return jnp.where(half, other, tiles[t]) if ex > 0 else jnp.where(half, tiles[t], other)


def roll(x, by):
    by %= LANES
    return pltpu.roll(x, by, 1) if by else x


def edges(q, t, count, half, j, k):
    ex, ey, ez = VEL[q]
    cx = None
    if ex > 0 and t == 0:
        cx = jnp.logical_not(half)
    if ex < 0 and t == count - 1:
        cx = half
    cy = None if ey == 0 else (j == (0 if ey > 0 else 7))
    cz = None if ez == 0 else (k == (0 if ez > 0 else 7))
    return cx, cy, cz


def face_of(axis, e):
    return 2 * axis + (1 if e > 0 else 0)


def write_bits(bits_ref, solid_ref, absent, tiles):
    rows = solid_ref.shape[0]
    half, j, k = lanes(rows)
    solid = [solid_ref[:, LANES * t : LANES * (t + 1)] for t in range(tiles)]
    for t in range(tiles):
        acc = jnp.where(solid[t] != 0, 1, 0)
        for q in range(1, Q):
            ex, ey, ez = VEL[q]
            v = roll(sources(q, t, solid, solid[t], half), 64 * abs(ex) + 8 * ey + ez)
            crossed = [c for c in zip(edges(q, t, tiles, half, j, k), (ex, ey, ez), range(3)) if c[0] is not None]
            for c, e, axis in crossed:
                v = jnp.where(c, absent[face_of(axis, e)], v)
            for i in range(len(crossed)):
                for m in range(i):
                    v = jnp.where(crossed[i][0] & crossed[m][0], 1, v)
            acc = acc | (jnp.where(v != 0, 1, 0) << q)
        bits_ref[:, LANES * t : LANES * (t + 1)] = acc


def collide_all(src_ref, dst_ref):
    rows, cells = src_ref.shape[1], src_ref.shape[2]
    tiles = cells // LANES

    def step(i, carry):
        r = pl.ds(pl.multiple_of(8 * (i // tiles), 8), 8)
        l = pl.ds(pl.multiple_of(LANES * (i % tiles), LANES), LANES)
        out = collide([src_ref[q, r, l] for q in range(Q)])
        for q in range(Q):
            dst_ref[q, r, l] = out[q]
        return carry

    lax.fori_loop(0, rows // 8 * tiles, step, 0)


def absences(nbr_ref, ifc_ref):
    out = []
    for d in range(6):
        there = nbr_ref[d : d + 1, :] >= 0
        if d == 2:
            there = there | (ifc_ref[0:1, :] >= 0)
        out.append((1.0 - spread_rows(jnp.where(there, 1.0, 0.0))).astype(I32))
    return out


def fine_ghost(out_ref, co_ref, ifc_ref, theta, position):
    count = co_ref.shape[0]
    blocks = ifc_ref.shape[1]
    tiles = out_ref.shape[2] // LANES
    half = lanes(blocks)[0]
    owner = ifc_ref[0:1, :] - (position + 1) * count
    quad = ifc_ref[1:2, :]
    masks = [
        [spread_rows(jnp.where((owner == c) & (quad == w), 1.0, 0.0)) for w in range(4)]
        for c in range(count)
    ]
    vals = []
    for c in range(count):
        h = []
        for q in range(Q):
            h0 = co_ref[c, q, 0:1, :]
            h.append(h0 if theta == 0 else (1.0 - theta) * h0 + theta * co_ref[c, q, 1:2, :])
        e = feq(h)
        row = {q: e[q] + (0.6 / 1.1) * (h[q] - e[q]) for q in CROSSING[2]}
        vals.append({q: jnp.concatenate([row[q], row[q]], axis=1) for q in CROSSING[2]})
    hi, lo = [], []
    for q in CROSSING[2]:
        parts = []
        for pair in (0, 2):
            acc = None
            for c in range(count):
                m = jnp.where(half, masks[c][pair + 1], masks[c][pair])
                v = m * vals[c][q]
                acc = v if acc is None else acc + v
            parts.append(acc)
        x = jnp.concatenate(parts, axis=1)
        h = x.astype(BF16)
        hi.append(h)
        lo.append((x - h.astype(F32)).astype(BF16))
    left = jnp.concatenate(hi + lo, axis=0)
    rows_k = 256
    kk = lax.broadcasted_iota(I32, (rows_k, LANES), 0)
    ll = lax.broadcasted_iota(I32, (rows_k, LANES), 1)
    w, m = kk >> 6, kk & 63
    n = 5 * blocks
    for t in range(tiles):
        i, k = 2 * t + (ll >> 6), ll & 7
        want = 8 * (4 * (w >> 1) + (i >> 1)) + 4 * (w & 1) + (k >> 1)
        e = jnp.where(m == want, 1.0, 0.0).astype(BF16)
        g = dot(left, e)
        g = g[:n] + g[n:]
        for s in range(5):
            out_ref[s, :, LANES * t : LANES * (t + 1)] = g[blocks * s : blocks * (s + 1)]


def send_faces(post_ref, nbr_ref, first, position, sa_ref, sb_ref):
    blocks = post_ref.shape[1]
    last = post_ref.shape[2] - LANES
    half = lanes(blocks)[0]
    even = position % 2 == 0
    packs = []
    for d, lane, by, native in ((0, last, first + blocks, 1), (1, 0, first - blocks, 0)):
        hot = select_rows(nbr_ref[d : d + 1, :], by, blocks)
        got = [dot(hot, split(post_ref[q, :, lane : lane + LANES])) for q in CROSSING[d ^ 1]]
        pack = []
        for s in range(0, 5, 2):
            a = got[s] if native == 0 else roll(got[s], 64)
            if s + 1 < 5:
                b = got[s + 1] if native == 1 else roll(got[s + 1], 64)
                a = jnp.where(half, b, a)
            pack.append(a)
        packs.append(pack)
    for s in range(3):
        sa_ref[s] = jnp.where(even, packs[0][s], packs[1][s])
        sb_ref[s] = jnp.where(even, packs[1][s], packs[0][s])


def received(ra_ref, rb_ref, position):
    even = position % 2 == 0
    half = lanes(ra_ref.shape[1])[0]
    out = {}
    for s in range(3):
        a, b = ra_ref[s], rb_ref[s]
        up, low = jnp.where(even, a, b), jnp.where(even, b, a)
        for i in (2 * s, 2 * s + 1):
            if i < 5:
                out[CROSSING[0][i]] = up if i % 2 == 0 else roll(up, 64)
                out[CROSSING[1][i]] = low if i % 2 == 1 else roll(low, 64)
    return out


def stream(post_ref, dst_ref, init_ref, bits_ref, nbr_ref, fine_ref, remote, first):
    blocks, cells = post_ref.shape[1], post_ref.shape[2]
    tiles = cells // LANES
    half, j, k = lanes(blocks)
    hot = [select_rows(nbr_ref[(d ^ 1) : (d ^ 1) + 1, :], first, blocks) for d in range(6)]
    span = [slice(LANES * t, LANES * (t + 1)) for t in range(tiles)]
    for q in range(Q):
        ex, ey, ez = VEL[q]
        x = [post_ref[q, :, span[t]] for t in range(tiles)]
        if q:
            parts = [split(v) for v in x]
        gx, gy, gz = None, None, None
        if ex:
            t = 0 if ex < 0 else tiles - 1
            gx = dot(hot[face_of(0, ex)], parts[t]) + remote[q]
        if ey:
            gy = [dot(hot[face_of(1, ey)], p) for p in parts]
            if ey < 0:
                s = CROSSING[2].index(q)
                gy = [g + fine_ref[s, :, span[t]] for t, g in enumerate(gy)]
        if ez:
            gz = [dot(hot[face_of(2, ez)], p) for p in parts]
        for t in range(tiles):
            bits = bits_ref[:, span[t]]
            if q == 0:
                out = x[t]
            else:
                out = roll(sources(q, t, x, gx, half), 64 * abs(ex) + 8 * ey + ez)
                _, cy, cz = edges(q, t, tiles, half, j, k)
                if ey:
                    g = roll(sources(q, t, gy, gy[t], half), 64 * abs(ex) - 56 * ey + ez)
                    out = jnp.where(cy, g, out)
                if ez:
                    g = roll(sources(q, t, gz, gz[t], half), 64 * abs(ex) + 8 * ey - 7 * ez)
                    out = jnp.where(cz, g, out)
                out = jnp.where((bits & (1 << q)) != 0, post_ref[OPP[q], :, span[t]], out)
            out = jnp.where((bits & 1) != 0, init_ref[q, :, span[t]], out)
            dst_ref[q, :, span[t]] = out


def first_kernel(pop_ref, nbr_ref, ifc_ref, solid_ref, post_ref, bits_ref, sa_ref, sb_ref):
    position = lax.axis_index("blk")
    first = position * pop_ref.shape[1]
    collide_all(pop_ref, post_ref)
    send_faces(post_ref, nbr_ref, first, position, sa_ref, sb_ref)
    write_bits(bits_ref, solid_ref, absences(nbr_ref, ifc_ref), pop_ref.shape[2] // LANES)


def middle_kernel(post_ref, pop_ref, bits_ref, ra_ref, rb_ref, co_ref, nbr_ref, ifc_ref, out_ref, sa_ref, sb_ref, fine_ref):
    position = lax.axis_index("blk")
    first = position * pop_ref.shape[1]
    fine_ghost(fine_ref, co_ref, ifc_ref, 0.0, position)
    stream(post_ref, out_ref, pop_ref, bits_ref, nbr_ref, fine_ref, received(ra_ref, rb_ref, position), first)
    collide_all(out_ref, out_ref)
    send_faces(out_ref, nbr_ref, first, position, sa_ref, sb_ref)


def last_kernel(post_ref, pop_ref, bits_ref, ra_ref, rb_ref, co_ref, nbr_ref, ifc_ref, out_ref, fine_ref):
    position = lax.axis_index("blk")
    first = position * pop_ref.shape[1]
    fine_ghost(fine_ref, co_ref, ifc_ref, 0.5, position)
    stream(post_ref, out_ref, pop_ref, bits_ref, nbr_ref, fine_ref, received(ra_ref, rb_ref, position), first)


def shifted(x, by):
    n = lax.axis_size("blk")
    return lax.ppermute(x, "blk", [(i, i + by) for i in range(n) if 0 <= i + by < n])


def swapped(x, off):
    n = lax.axis_size("blk")
    low = [(i, i + 1) for i in range(off, n - 1, 2)]
    return lax.ppermute(x, "blk", low + [(b, a) for a, b in low])


def body(populations, coarse_faces, neighbors, interface, solid):
    pop = populations.transpose(1, 0, 2)
    co = coarse_faces.transpose(0, 2, 1, 3)
    nbr, ifc = neighbors.T, interface.T
    blocks = pop.shape[1]
    state = jax.ShapeDtypeStruct(pop.shape, F32)
    faces = jax.ShapeDtypeStruct((3, blocks, LANES), F32)
    fine = pltpu.VMEM((5,) + pop.shape[1:], F32)
    co = shifted(co, -1)
    post, bits, sa, sb = pl.pallas_call(
        first_kernel, out_shape=(state, jax.ShapeDtypeStruct(solid.shape, I32), faces, faces), name="first"
    )(pop, nbr, ifc, solid)
    ra, rb = swapped(sa, 0), swapped(sb, 1)
    post, sa, sb = pl.pallas_call(
        middle_kernel, out_shape=(state, faces, faces), scratch_shapes=[fine], name="middle"
    )(post, pop, bits, ra, rb, co, nbr, ifc)
    ra, rb = swapped(sa, 0), swapped(sb, 1)
    out = pl.pallas_call(last_kernel, out_shape=state, scratch_shapes=[fine], name="last")(
        post, pop, bits, ra, rb, co, nbr, ifc
    )
    return out.transpose(1, 0, 2)


def solution(mesh):
    placed = (P("blk", None, None), P("blk", None, None, None), P("blk", None), P("blk", None), P("blk", None))
    return jax.shard_map(body, mesh=mesh, in_specs=placed, out_specs=P("blk", None, None), check_vma=False)
```

time: 508 us -> 31.2 us (0.06); the launches traced: 500 us -> 30.9 us
  local copies, waits for them, and re-layouts: 389 us -> 1.26 us
  other arithmetic: 74.5 us -> 0 us
  matrix products: 15.3 us -> 0 us
  Pallas kernels: 0 us -> 11.4 us
  waiting for transfers between devices: 0.01 us -> 10.6 us
  starting transfers between devices: 15.9 us -> 7.5 us
  between operations: 5.19 us -> 0.07 us
    gather x205 -> x0, local copies, waits for them, and re-layouts: 358 us -> none  [the longest x3 158 us: spread_quadrant(): jnp.take_along_axis(ghost_view, cell_index, axis=3).reshape(total, 2, 320)]
    slice x72 -> x0, local copies, waits for them, and re-layouts: 20.6 us -> none  [the longest x18 12.2 us: stream(): usable = jnp.roll(fluid, shift_offsets[lattice_dir], axis=1)]
    squeeze x18 -> x0, other arithmetic: 19.8 us -> none  [the longest x16 16.8 us: stream(): relaxed[:, lattice_dir]]
    unnamed x16 -> x0, other arithmetic: 18.8 us -> none
    dot_general x10 -> x0, matrix products: 15.3 us -> none  [the longest x4 5.71 us: equilibrium(): jnp.einsum('qa,mqn->man', velocity_f32, states, precision=lax.Precision.H...]
    gather x23 -> x0, other arithmetic: 13.1 us -> none
    pallas_call x0 -> x3, Pallas kernels: none -> 11.4 us  [the longest x1 4.55 us: body(): pl.pallas_call(middle_kernel, out_shape=(state, faces, faces), scratch_sh...]
    ppermute x5, waiting for transfers between devices: 0.01 us -> 10.6 us  [the longest x4 5.48 us: swapped(): return lax.ppermute(x, 'blk', low + [(b, a) for a, b in low])]
  transfers between devices with their start and end apart: 5 -> 5, of which waited for: 0 -> 2; matrix products, arithmetic and copies ran while one was open for 74% -> 0% of each run, Pallas kernels for 0% -> 0%
where the time goes in v1:
time: 31.2 us; the launch traced here: 30.9 us
  Pallas kernels  11.4 us (37%)
  waiting for transfers between devices  10.6 us (34%)
  starting transfers between devices  7.5 us (24%)
  local copies, waits for them, and re-layouts  1.26 us (4%)
    ppermute x4, starting transfers between devices, swapped(): return lax.ppermute(x, 'blk', low + [(b, a) for a, b in low])  5.58 us
    ppermute x4, waiting for transfers between devices, swapped(): return lax.ppermute(x, 'blk', low + [(b, a) for a, b in low])  5.48 us
    ppermute x1, waiting for transfers between devices, shifted(): lax.ppermute(x, 'blk', [(i, i + by) for i in range(n) if 0 <= i + by < n])  5.17 us
    pallas_call x1, Pallas kernels, body(): pl.pallas_call(middle_kernel, out_shape=(state, faces, faces), scratch_sh...  4.55 us
    pallas_call x1, Pallas kernels, body(): pl.pallas_call(last_kernel, out_shape=state, scratch_shapes=[fine], name=...  3.74 us
    pallas_call x1, Pallas kernels, body(): pl.pallas_call(first_kernel, out_shape=(state, jax.ShapeDtypeStruct(solid...  3.15 us
    ppermute x1, starting transfers between devices, shifted(): lax.ppermute(x, 'blk', [(i, i + by) for i in range(n) if 0 <= i + by < n])  1.92 us
    unnamed x12, local copies, waits for them, and re-layouts  1.26 us
  transfers between devices with their start and end apart: 5, of which 2 were waited for; matrix products, arithmetic and copies ran while one was open for 0% of the time, Pallas kernels for 0%

profile of v1, /device:TPU:23, one launch (start us, length us, event | category | flops | bytes accessed | tf_op | source)
XLA Modules:
  0.0 30.9 jit_solution(14290976097417262446)
XLA Ops:
  0.0 0.0 copy-start.5
  0.0 3.2 %first.1 = (f32[19,32,512]{2,1,0:T(8,128)}, s32[32,512]{1,0:T(8,128)}, f32[3,32,128]{2,1,0:T(8,128)}, f32[3,32,128]{2,1,0:T(8,128)}) custom-call(f32[19,32,512]{2,1,0:T(8,128)} %bitcast.5, s32[6,32]{1,0:T(8,128)} %bitcast.8, s32[2,32]{1,0:T(2,128)} %bitcast.11, s32[32,512]{1,0:T(8,128)} %solid_ref.1), custom_call_target="tpu_custom_call" | custom-call | tf_op jit(solution)/shard_map/first/pallas_call | solution.py:391
  3.2 0.7 %collective-permute-start = (f32[3,32,128]{2,1,0:T(8,128)}, f32[3,32,128]{2,1,0:T(8,128)S(1)}, u32[]{:S(2)}, u32[]{:S(2)}) collective-permute-start(f32[3,32,128]{2,1,0:T(8,128)} %get-tuple-element.14), channel_id=1, source_target_pairs={{0,1},{2,3},{4,5},{6,7},{8,9},{10,11},{12,13},{14,15},{16,17},{18,... | collective-permute-start | bytes 147464 | tf_op jit(solution)/shard_map/ppermute | solution.py:379
  3.8 3.0 %collective-permute-start.1 = (f32[3,32,128]{2,1,0:T(8,128)}, f32[3,32,128]{2,1,0:T(8,128)S(1)}, u32[]{:S(2)}, u32[]{:S(2)}) collective-permute-start(f32[3,32,128]{2,1,0:T(8,128)} %get-tuple-element.15), channel_id=1, source_target_pairs={{1,2},{3,4},{5,6},{7,8},{9,10},{11,12},{13,14},{15,16},{17,18},{19... | collective-permute-start | bytes 147464 | tf_op jit(solution)/shard_map/ppermute | solution.py:379
  6.8 0.0 copy-done.5
  6.8 1.9 %collective-permute-start.2 = (f32[2,19,2,64]{3,2,1,0:T(2,128)S(1)}, f32[2,19,2,64]{3,2,1,0:T(2,128)S(1)}, u32[]{:S(2)}, u32[]{:S(2)}) collective-permute-start(f32[2,19,2,64]{3,2,1,0:T(2,128)S(1)} %bitcast.14), channel_id=1, source_target_pairs={{1,0},{2,1},{3,2},{4,3},{5,4},{6,5},{7,6},{8,7},{9,8},{10,9},{11,1... | collective-permute-start | bytes 58376 | tf_op jit(solution)/shard_map/ppermute | solution.py:373
  8.8 5.2 %collective-permute-done.2.co_ref = f32[2,19,2,64]{3,2,1,0:T(2,128)S(1)} collective-permute-done((f32[2,19,2,64]{3,2,1,0:T(2,128)S(1)}, f32[2,19,2,64]{3,2,1,0:T(2,128)S(1)}, u32[]{:S(2)}, u32[]{:S(2)}) %collective-permute-start.2) | collective-permute-done | bytes 19488 | tf_op jit(solution)/shard_map/ppermute | solution.py:373
  13.9 0.0 copy-start
  13.9 0.0 collective-permute-done.ra_ref
  14.0 0.0 copy-start.3
  14.0 0.0 collective-permute-done.1.rb_ref
  14.0 0.0 copy-start.4
  14.0 0.6 %copy-done = f32[2,19,2,64]{3,2,1,0:T(2,128)} copy-done((f32[2,19,2,64]{3,2,1,0:T(2,128)}, f32[2,19,2,64]{3,2,1,0:T(2,128)S(1)}, u32[]{:S(2)}) %copy-start) | copy-done | bytes 19480
  14.6 0.0 copy-done.3
  14.6 0.0 copy-done.4
  14.6 4.6 %middle.1 = (f32[19,32,512]{2,1,0:T(8,128)}, f32[3,32,128]{2,1,0:T(8,128)}, f32[3,32,128]{2,1,0:T(8,128)}) custom-call(f32[19,32,512]{2,1,0:T(8,128)} %get-tuple-element.12.post_ref, f32[19,32,512]{2,1,0:T(8,128)} %bitcast.6, s32[32,512]{1,0:T(8,128)} %get-tuple-element.13.bits_ref, f32[3,32,128]{2,1,0:T(8,128)} %copy-done.3, f32[3,32,128]{2,1,0:T(8,128)} %copy-done.4, ...), custom_call_target="tpu_custom_call" | custom-call | tf_op jit(solution)/shard_map/middle/pallas_call | solution.py:395
  19.2 0.0 collective-permute-start.3
  19.2 1.9 %collective-permute-start.4 = (f32[3,32,128]{2,1,0:T(8,128)}, f32[3,32,128]{2,1,0:T(8,128)S(1)}, u32[]{:S(2)}, u32[]{:S(2)}) collective-permute-start(f32[3,32,128]{2,1,0:T(8,128)} %get-tuple-element.18), channel_id=1, source_target_pairs={{1,2},{3,4},{5,6},{7,8},{9,10},{11,12},{13,14},{15,16},{17,18},{19... | collective-permute-start | bytes 147464 | tf_op jit(solution)/shard_map/ppermute | solution.py:379
  21.1 0.0 collective-permute-done.3.ra_ref
  21.1 0.0 copy-start.1
  21.1 5.5 %collective-permute-done.4.rb_ref = f32[3,32,128]{2,1,0:T(8,128)S(1)} collective-permute-done((f32[3,32,128]{2,1,0:T(8,128)}, f32[3,32,128]{2,1,0:T(8,128)S(1)}, u32[]{:S(2)}, u32[]{:S(2)}) %collective-permute-start.4) | collective-permute-done | bytes 49184 | tf_op jit(solution)/shard_map/ppermute | solution.py:379
  26.6 0.0 copy-start.2
  26.6 0.0 copy-done.1
  26.6 0.6 %copy-done.2 = f32[3,32,128]{2,1,0:T(8,128)} copy-done((f32[3,32,128]{2,1,0:T(8,128)}, f32[3,32,128]{2,1,0:T(8,128)S(1)}, u32[]{:S(2)}) %copy-start.2) | copy-done | bytes 49176
  27.2 3.7 %last.1 = f32[19,32,512]{2,1,0:T(8,128)} custom-call(f32[19,32,512]{2,1,0:T(8,128)} %get-tuple-element.16.post_ref, f32[19,32,512]{2,1,0:T(8,128)} %bitcast.7, s32[32,512]{1,0:T(8,128)} %get-tuple-element.13.bits_ref, f32[3,32,128]{2,1,0:T(8,128)} %copy-done.1, f32[3,32,128]{2,1,0:T(8,128)} %copy-done.2, f32[2,19,2,64]{3,2,1,0:T(2,128)} %copy-done, ...), custom_call_target="tpu_custom_call" | custom-call | tf_op jit(solution)/shard_map/last/pallas_call | solution.py:399
Async XLA Ops:
  0.0 6.8 %copy-start.5 = (f32[2,2,19,64]{3,1,2,0:T(2,128)S(1)}, f32[2,2,19,64]{3,1,2,0:T(2,128)}, u32[]{:S(2)}) copy-start(f32[2,2,19,64]{3,1,2,0:T(2,128)} %param.6) | copy-start | bytes 58372
  3.2 10.8 %collective-permute-start = (f32[3,32,128]{2,1,0:T(8,128)}, f32[3,32,128]{2,1,0:T(8,128)S(1)}, u32[]{:S(2)}, u32[]{:S(2)}) collective-permute-start(f32[3,32,128]{2,1,0:T(8,128)} %get-tuple-element.14), channel_id=1, source_target_pairs={{0,1},{2,3},{4,5},{6,7},{8,9},{10,11},{12,13},{14,15},{16,17},{18,... | collective-permute-start | bytes 147464 | tf_op jit(solution)/shard_map/ppermute | solution.py:379
  3.8 10.1 %collective-permute-start.1 = (f32[3,32,128]{2,1,0:T(8,128)}, f32[3,32,128]{2,1,0:T(8,128)S(1)}, u32[]{:S(2)}, u32[]{:S(2)}) collective-permute-start(f32[3,32,128]{2,1,0:T(8,128)} %get-tuple-element.15), channel_id=1, source_target_pairs={{1,2},{3,4},{5,6},{7,8},{9,10},{11,12},{13,14},{15,16},{17,18},{19... | collective-permute-start | bytes 147464 | tf_op jit(solution)/shard_map/ppermute | solution.py:379
  6.8 7.1 %collective-permute-start.2 = (f32[2,19,2,64]{3,2,1,0:T(2,128)S(1)}, f32[2,19,2,64]{3,2,1,0:T(2,128)S(1)}, u32[]{:S(2)}, u32[]{:S(2)}) collective-permute-start(f32[2,19,2,64]{3,2,1,0:T(2,128)S(1)} %bitcast.14), channel_id=1, source_target_pairs={{1,0},{2,1},{3,2},{4,3},{5,4},{6,5},{7,6},{8,7},{9,8},{10,9},{11,1... | collective-permute-start | bytes 58376 | tf_op jit(solution)/shard_map/ppermute | solution.py:373
  13.9 0.6 %copy-start = (f32[2,19,2,64]{3,2,1,0:T(2,128)}, f32[2,19,2,64]{3,2,1,0:T(2,128)S(1)}, u32[]{:S(2)}) copy-start(f32[2,19,2,64]{3,2,1,0:T(2,128)S(1)} %collective-permute-done.2.co_ref) | copy-start | bytes 58372
  14.0 0.6 %copy-start.3 = (f32[3,32,128]{2,1,0:T(8,128)}, f32[3,32,128]{2,1,0:T(8,128)S(1)}, u32[]{:S(2)}) copy-start(f32[3,32,128]{2,1,0:T(8,128)S(1)} %collective-permute-done.ra_ref) | copy-start | bytes 147460
  14.0 0.6 %copy-start.4 = (f32[3,32,128]{2,1,0:T(8,128)}, f32[3,32,128]{2,1,0:T(8,128)S(1)}, u32[]{:S(2)}) copy-start(f32[3,32,128]{2,1,0:T(8,128)S(1)} %collective-permute-done.1.rb_ref) | copy-start | bytes 147460
  19.2 1.9 %collective-permute-start.3 = (f32[3,32,128]{2,1,0:T(8,128)}, f32[3,32,128]{2,1,0:T(8,128)S(1)}, u32[]{:S(2)}, u32[]{:S(2)}) collective-permute-start(f32[3,32,128]{2,1,0:T(8,128)} %get-tuple-element.17), channel_id=1, source_target_pairs={{0,1},{2,3},{4,5},{6,7},{8,9},{10,11},{12,13},{14,15},{16,17},{18,... | collective-permute-start | bytes 147464 | tf_op jit(solution)/shard_map/ppermute | solution.py:379
  19.2 7.4 %collective-permute-start.4 = (f32[3,32,128]{2,1,0:T(8,128)}, f32[3,32,128]{2,1,0:T(8,128)S(1)}, u32[]{:S(2)}, u32[]{:S(2)}) collective-permute-start(f32[3,32,128]{2,1,0:T(8,128)} %get-tuple-element.18), channel_id=1, source_target_pairs={{1,2},{3,4},{5,6},{7,8},{9,10},{11,12},{13,14},{15,16},{17,18},{19... | collective-permute-start | bytes 147464 | tf_op jit(solution)/shard_map/ppermute | solution.py:379
  21.1 5.5 %copy-start.1 = (f32[3,32,128]{2,1,0:T(8,128)}, f32[3,32,128]{2,1,0:T(8,128)S(1)}, u32[]{:S(2)}) copy-start(f32[3,32,128]{2,1,0:T(8,128)S(1)} %collective-permute-done.3.ra_ref) | copy-start | bytes 147460
  26.6 0.6 %copy-start.2 = (f32[3,32,128]{2,1,0:T(8,128)}, f32[3,32,128]{2,1,0:T(8,128)S(1)}, u32[]{:S(2)}) copy-start(f32[3,32,128]{2,1,0:T(8,128)S(1)} %collective-permute-done.4.rb_ref) | copy-start | bytes 147460

commit v2 on v1

v2 whole, which is shorter than its diff:
```python
import functools

import jax
import jax.numpy as jnp
import numpy as np
from jax import lax
from jax.experimental import pallas as pl
from jax.experimental.pallas import tpu as pltpu
from jax.sharding import PartitionSpec as P

F32, BF16, I32 = jnp.float32, jnp.bfloat16, jnp.int32
LANES = 128
VEL = [
    (0, 0, 0),
    (1, 0, 0), (-1, 0, 0), (0, 1, 0), (0, -1, 0), (0, 0, 1), (0, 0, -1),
    (1, 1, 0), (-1, -1, 0), (1, -1, 0), (-1, 1, 0),
    (1, 0, 1), (-1, 0, -1), (1, 0, -1), (-1, 0, 1),
    (0, 1, 1), (0, -1, -1), (0, 1, -1), (0, -1, 1),
]
Q = len(VEL)
OPP = [VEL.index((-x, -y, -z)) for x, y, z in VEL]
CROSSING = [
    [q for q in range(Q) if VEL[q][d // 2] == (-1 if d % 2 == 0 else 1)] for d in range(6)
]


def rates():
    v = np.array(VEL) * 1.0
    x, y, z = v[:, 0], v[:, 1], v[:, 2]
    s = x * x + y * y + z * z
    rows = [
        np.ones(19), 19 * s - 30, (21 * s * s - 53 * s + 24) / 2,
        x, (5 * s - 9) * x, y, (5 * s - 9) * y, z, (5 * s - 9) * z,
        3 * x * x - s, (3 * s - 5) * (3 * x * x - s),
        y * y - z * z, (3 * s - 5) * (y * y - z * z),
        x * y, y * z, x * z,
        (y * y - z * z) * x, (z * z - x * x) * y, (x * x - y * y) * z,
    ]
    norms = (np.stack(rows) ** 2).sum(1)
    w = 1.0 / 0.6
    relax = np.array([0, 1.19, 1.4, 0, 1.2, 0, 1.2, 0, 1.2, w, 1.4, w, 1.4, w, w, w, 1.98, 1.98, 1.98])
    return [float(c) for c in relax / norms]


def collide(f):
    c = rates()
    s = {q: f[q] + f[q + 1] for q in range(1, 19, 2)}
    d = {q: f[q] - f[q + 1] for q in range(1, 19, 2)}
    a, b, g = s[7] + s[9], s[11] + s[13], s[15] + s[17]
    s1, s2 = s[1] + (s[3] + s[5]), a + b + g
    rho = f[0] + s1 + s2
    ax1, ax2 = d[7] + d[9], d[11] + d[13]
    ay1, ay2 = d[7] - d[9], d[15] + d[17]
    az1, az2 = d[11] - d[13], d[15] - d[17]
    ax, ay, az = ax1 + ax2, ay1 + ay2, az1 + az2
    jx, jy, jz = d[1] + ax, d[3] + ay, d[5] + az
    inv = 1.0 / rho
    ux, uy, uz = jx * inv, jy * inv, jz * inv
    xx, yy, zz = jx * ux, jy * uy, jz * uz
    jj = xx + yy + zz
    r1 = (19 * c[1]) * (s2 - f[0] - jj)
    r2 = c[2] * (9 * f[0] - 7 * s1 - 2 * s2 + 5.5 * jj)
    t1, t2, pe = 2 * s[1] - (s[3] + s[5]), a + b - 2 * g, 3 * xx - jj
    v1, v2, we = s[3] - s[5], a - b, yy - zz
    r9, r10 = c[9] * (t1 + t2 - pe), c[10] * (t2 - 2 * t1 + 0.5 * pe)
    r11, r12 = c[11] * (v1 + v2 - we), c[12] * (v2 - 2 * v1 + 0.5 * we)
    r13 = c[13] * (s[7] - s[9] - jx * uy)
    r14 = c[14] * (s[15] - s[17] - jy * uz)
    r15 = c[15] * (s[11] - s[13] - jx * uz)
    r4 = (c[4] * 5 / 3) * (ax - 2 * d[1])
    r6 = (c[6] * 5 / 3) * (ay - 2 * d[3])
    r8 = (c[8] * 5 / 3) * (az - 2 * d[5])
    r16, r17, r18 = c[16] * (ax1 - ax2), c[17] * (ay2 - ay1), c[18] * (az1 - az2)
    ea, eb = -11 * r1 - 4 * r2, 8 * r1 + r2
    a9, a11 = r9 - 2 * r10, r11 - 2 * r12
    b9, b11 = r9 + r10, r11 + r12
    exy, exz, eyz = eb + b9 + b11, eb + b9 - b11, eb - 2 * b9
    even = {
        1: ea + 2 * a9, 3: ea - a9 + a11, 5: ea - a9 - a11,
        7: exy + r13, 9: exy - r13, 11: exz + r15, 13: exz - r15, 15: eyz + r14, 17: eyz - r14,
    }
    odd = {
        1: -4 * r4, 3: -4 * r6, 5: -4 * r8,
        7: (r4 + r6) + (r16 - r17), 9: (r4 - r6) + (r16 + r17),
        11: (r4 + r8) - (r16 - r18), 13: (r4 - r8) - (r16 + r18),
        15: (r6 + r8) + (r17 - r18), 17: (r6 - r8) + (r17 + r18),
    }
    out = [f[0] + 30 * r1 - 12 * r2]
    for q in range(1, 19, 2):
        out += [f[q] - even[q] - odd[q], f[q + 1] - even[q] + odd[q]]
    return out


def feq(h):
    rho = h[0]
    for q in range(1, Q):
        rho = rho + h[q]
    safe = jnp.where(rho > 0, rho, 1.0)
    u = []
    for axis in range(3):
        m = None
        for q in range(Q):
            if VEL[q][axis]:
                t = h[q] if VEL[q][axis] > 0 else -h[q]
                m = t if m is None else m + t
        u.append(m / safe)
    sq = u[0] * u[0] + u[1] * u[1] + u[2] * u[2]
    out = {}
    for q in CROSSING[2]:
        p = None
        for axis in range(3):
            if VEL[q][axis]:
                t = u[axis] if VEL[q][axis] > 0 else -u[axis]
                p = t if p is None else p + t
        n = sum(abs(e) for e in VEL[q])
        w = 1.0 / 18.0 if n == 1 else 1.0 / 36.0
        out[q] = w * rho * (1.0 + 3.0 * p + 4.5 * p * p - 1.5 * sq)
    return out


def lanes(rows):
    l = lax.broadcasted_iota(I32, (rows, LANES), 1)
    return l >= 64, (l >> 3) & 7, l & 7


def split(x):
    hi = x.astype(BF16)
    lo = (x - hi.astype(F32)).astype(BF16)
    return jnp.concatenate([hi, lo], axis=0)


def dot(a, b):
    return jnp.dot(a, b, preferred_element_type=F32)


def select_rows(row, offset, count):
    r = lax.broadcasted_iota(I32, (count, row.shape[1]), 0)
    hot = jnp.where(r == row - offset, 1.0, 0.0).astype(BF16)
    return jnp.concatenate([hot, hot], axis=1)


def spread_rows(flags):
    n = flags.shape[1]
    eye = lax.broadcasted_iota(I32, (n, n), 0) == lax.broadcasted_iota(I32, (n, n), 1)
    diag = jnp.where(eye, flags.astype(F32), 0.0).astype(BF16)
    return dot(diag, jnp.ones((n, LANES), BF16))


def sources(q, t, tiles, outer, half):
    ex = VEL[q][0]
    if ex == 0:
        return tiles[t]
    n = t - ex
    other = tiles[n] if 0 <= n < len(tiles) else outer
    return jnp.where(half, other, tiles[t]) if ex > 0 else jnp.where(half, tiles[t], other)


def roll(x, by):
    by %= LANES
    return pltpu.roll(x, by, 1) if by else x


def edges(q, t, count, half, j, k):
    ex, ey, ez = VEL[q]
    cx = None
    if ex > 0 and t == 0:
        cx = jnp.logical_not(half)
    if ex < 0 and t == count - 1:
        cx = half
    cy = None if ey == 0 else (j == (0 if ey > 0 else 7))
    cz = None if ez == 0 else (k == (0 if ez > 0 else 7))
    return cx, cy, cz


def face_of(axis, e):
    return 2 * axis + (1 if e > 0 else 0)


def bounce_bits(t, solid, absent):
    half, j, k = lanes(solid[0].shape[0])
    acc = jnp.where(solid[t] != 0, 1, 0)
    for q in range(1, Q):
        ex, ey, ez = VEL[q]
        v = roll(sources(q, t, solid, solid[t], half), 64 * abs(ex) + 8 * ey + ez)
        sides = zip(edges(q, t, len(solid), half, j, k), (ex, ey, ez), range(3))
        crossed = [c for c in sides if c[0] is not None]
        for c, e, axis in crossed:
            v = jnp.where(c, absent[face_of(axis, e)], v)
        for i in range(len(crossed)):
            for m in range(i):
                v = jnp.where(crossed[i][0] & crossed[m][0], 1, v)
        acc = acc | (jnp.where(v != 0, 1, 0) << q)
    return acc


def absences(nbr_ref, ifc_ref):
    out = []
    for d in range(6):
        there = nbr_ref[d : d + 1, :] >= 0
        if d == 2:
            there = there | (ifc_ref[0:1, :] >= 0)
        out.append((1.0 - spread_rows(jnp.where(there, 1.0, 0.0))).astype(I32))
    return out


def local_hots(nbr_ref, first):
    n = nbr_ref.shape[1]
    return [select_rows(nbr_ref[(d ^ 1) : (d ^ 1) + 1, :], first, n) for d in range(6)]


def send_rows(row, first, count, cap):
    rel = row - first
    gone = (rel >= 0) & (rel < count)
    rel = jnp.where(gone, rel, 255)
    ahead = spread_rows(rel)[:, :count] < rel.astype(F32)
    rank = jnp.sum(jnp.where(ahead, 1.0, 0.0), axis=0, keepdims=True)
    r = lax.broadcasted_iota(I32, (cap, count), 0).astype(F32)
    hot = jnp.where((r == rank) & gone, 1.0, 0.0).astype(BF16)
    return jnp.concatenate([hot, hot], axis=1)


def take_rows(row, first, count, cap):
    rel = row - first
    gone = jnp.where((rel >= 0) & (rel < count), 1.0, 0.0)
    b = lax.broadcasted_iota(I32, (count, count), 0)
    a = lax.broadcasted_iota(I32, (count, count), 1)
    rank = dot(jnp.where(a < b, gone, 0.0).astype(BF16), jnp.ones((count, LANES), BF16))[:, :cap]
    there = spread_rows(gone)[:, :cap] > 0.5
    r = lax.broadcasted_iota(I32, (count, cap), 1).astype(F32)
    hot = jnp.where((r == rank) & there, 1.0, 0.0).astype(BF16)
    return jnp.concatenate([hot, hot], axis=1)


def coarse_code(ifc_ref, position, count):
    c = ifc_ref[0:1, :]
    code = jnp.where(c >= 0, 2 + 4 * (c - (position + 1) * count) + ifc_ref[1:2, :], 1)
    return spread_rows(code)


def coarse_values(co_ref, cg_ref):
    count = co_ref.shape[0]
    h = []
    for q in range(Q):
        h0 = co_ref[:, q, 0, :]
        h1 = (1.0 - 0.5) * h0 + 0.5 * co_ref[:, q, 1, :]
        h.append(jnp.concatenate([h0, h1], axis=1))
    e = feq(h)
    cg_ref[...] = jnp.zeros_like(cg_ref)
    for s, q in enumerate(CROSSING[2]):
        v = e[q] + (0.6 / 1.1) * (h[q] - e[q])
        for c in range(count):
            cg_ref[5 * c + s : 5 * c + s + 1, :] = v[c : c + 1]


def both_halves(x, upper):
    half = lanes(x.shape[0])[0]
    return jnp.where(half, x, roll(x, 64)) if upper else jnp.where(half, roll(x, 64), x)


def spread_matrix(tiles):
    kk = lax.broadcasted_iota(I32, (256, LANES), 0)
    ll = lax.broadcasted_iota(I32, (256, LANES), 1)
    w, m, k = kk >> 6, kk & 63, ll & 7
    out = []
    for t in range(tiles + 1):
        i = (ll >> 6) * 7 if t == tiles else 2 * t + (ll >> 6)
        want = 8 * (4 * (w >> 1) + (i >> 1)) + 4 * (w & 1) + (k >> 1)
        out.append(jnp.where(m == want, 1.0, 0.0).astype(BF16))
    return out


def coarse_rows(code, cg, count):
    half = lanes(code.shape[0])[0]
    hi, lo = [], []
    for s in range(5):
        parts = []
        for pair in (0, 2):
            acc = jnp.zeros_like(code)
            for c in range(count):
                want = jnp.where(half, 3.0 + 4 * c + pair, 2.0 + 4 * c + pair)
                acc = jnp.where(code == want, cg[5 * c + s : 5 * c + s + 1, :], acc)
            parts.append(acc)
        x = jnp.concatenate(parts, axis=1)
        h = x.astype(BF16)
        hi.append(h)
        lo.append((x - h.astype(F32)).astype(BF16))
    return jnp.concatenate(hi + lo, axis=0)


def coarse_tile(rows, matrix):
    g = dot(rows, matrix)
    n = g.shape[0] // 2
    g = g[:n] + g[n:]
    b = n // 5
    return [g[b * s : b * (s + 1)] for s in range(5)]


def pull(q, t, x, parts, gx, hot, fine, bits, bounced, init):
    if q == 0:
        return jnp.where((bits & 1) != 0, init, x[t])
    half, j, k = lanes(bits.shape[0])
    ex, ey, ez = VEL[q]
    turn = 64 * abs(ex)
    out = roll(sources(q, t, x, gx, half), turn + 8 * ey + ez)
    _, cy, cz = edges(q, t, len(x), half, j, k)
    if ey:
        g = parts[1]
        out = jnp.where(cy, roll(sources(q, t, g, g[t], half), turn - 56 * ey + ez), out)
    if ez:
        g = parts[2]
        out = jnp.where(cz, roll(sources(q, t, g, g[t], half), turn + 8 * ey - 7 * ez), out)
    out = jnp.where((bits & (1 << q)) != 0, bounced, out)
    return jnp.where((bits & 1) != 0, init, out)


def gathers(q, x, hot, fine, remote):
    ex, ey, ez = VEL[q]
    gx, gy, gz = None, None, None
    if q:
        parts = [split(v) for v in x]
    if ex:
        gx = dot(hot[face_of(0, ex)], parts[0 if ex < 0 else len(x) - 1])
        if remote is not None:
            gx = gx + remote[q]
    if ey:
        gy = [dot(hot[face_of(1, ey)], p) for p in parts]
        if ey < 0 and fine is not None:
            s = CROSSING[2].index(q)
            gy = [g + fine(s, t) for t, g in enumerate(gy)]
    if ez:
        gz = [dot(hot[face_of(2, ez)], p) for p in parts]
    return gx, gy, gz


def side_slots(d):
    e = 1 if d == 0 else -1
    return [q for q in range(Q) if VEL[q][0] == e], [q for q in range(Q) if VEL[q][0] != -e]


def outer_kernel(pop_ref, nbr_ref, ifc_ref, solid_ref, co_ref, post_ref, bits_ref, cg_ref, sa_ref, sb_ref, buf_ref, pack_ref, sem):
    position = lax.axis_index("blk")
    blocks = solid_ref.shape[0]
    tiles = solid_ref.shape[1] // LANES
    first = position * blocks
    even = position % 2 == 0
    count = co_ref.shape[0]
    copies = []
    for side, t in ((0, tiles - 1), (1, 0)):
        copy = pltpu.make_async_copy(
            pop_ref.at[:, :, pl.ds(LANES * t, LANES)], buf_ref.at[side], sem.at[side]
        )
        copy.start()
        copies.append(copy)
    half, j, k = lanes(blocks)
    coarse_values(co_ref, cg_ref)
    code = coarse_code(ifc_ref, position, count)
    absent = absences(nbr_ref, ifc_ref)
    hot = local_hots(nbr_ref, first)
    solid = [solid_ref[:, LANES * t : LANES * (t + 1)] for t in range(tiles)]
    bits_ref[0] = bounce_bits(tiles - 1, solid, absent)
    bits_ref[1] = bounce_bits(0, solid, absent)
    for side, t in ((0, tiles - 1), (1, 0)):
        copies[side].wait()

        def step(g, carry, side=side):
            r = pl.ds(pl.multiple_of(8 * g, 8), 8)
            out = collide([buf_ref[side, q, r, :] for q in range(Q)])
            for q in range(Q):
                post_ref[side, q, r, :] = out[q]
            return carry

        lax.fori_loop(0, blocks // 8, step, 0)
        bits = bits_ref[side]
        to = send_rows(nbr_ref[side : side + 1, :], first + (blocks if side == 0 else -blocks), blocks, pack_ref.shape[2])
        face, layer = side_slots(side)
        slots = [post_ref[side, q] for q in face]
        for q in layer:
            ex, ey, ez = VEL[q]
            x = post_ref[side, q]
            turn = 64 * abs(ex)
            out = roll(x, turn + 8 * ey + ez)
            _, cy, cz = edges(q, t, tiles, half, j, k)
            if ey or ez:
                parts = split(x)
            if ey:
                out = jnp.where(cy, roll(dot(hot[face_of(1, ey)], parts), turn - 56 * ey + ez), out)
            if ez:
                out = jnp.where(cz, roll(dot(hot[face_of(2, ez)], parts), turn + 8 * ey - 7 * ez), out)
            if q:
                out = jnp.where((bits & (1 << q)) != 0, post_ref[side, OPP[q]], out)
            slots.append(out)
        slots.append(code)
        for s in range(0, len(slots), 2):
            a, b = slots[s], slots[s + 1]
            packed = jnp.where(half, b, roll(a, 64)) if side == 0 else jnp.where(half, roll(b, 64), a)
            pack_ref[side, s // 2] = dot(to, split(packed))
    n = pack_ref.shape[1]
    for s in range(n):
        sa_ref[s] = jnp.where(even, pack_ref[0, s], pack_ref[1, s])
        sb_ref[s] = jnp.where(even, pack_ref[1, s], pack_ref[0, s])
    sa_ref[n] = cg_ref[...]
    sb_ref[n] = cg_ref[...]


def inner_kernel(pop_ref, nbr_ref, ifc_ref, solid_ref, outer_ref, obits_ref, cur_ref, bits_ref, code_ref, spread_ref, take_ref, mid_ref, *, count):
    position = lax.axis_index("blk")
    blocks = solid_ref.shape[0]
    tiles = solid_ref.shape[1] // LANES
    first = position * blocks
    groups = blocks // 8

    def step(i, carry):
        n, g = i // groups, i % groups
        r = pl.ds(pl.multiple_of(8 * g, 8), 8)
        l = pl.ds(pl.multiple_of(LANES * (n + 1), LANES), LANES)
        out = collide([pop_ref[q, r, l] for q in range(Q)])
        for q in range(Q):
            mid_ref[n, q, r, :] = out[q]
        return carry

    lax.fori_loop(0, groups * (tiles - 2), step, 0)
    code_ref[...] = coarse_code(ifc_ref, position, count)
    for t, m in enumerate(spread_matrix(tiles)):
        spread_ref[t] = m
    cap = take_ref.shape[2] // 2
    take_ref[0] = take_rows(nbr_ref[0:1, :], first + blocks, blocks, cap)
    take_ref[1] = take_rows(nbr_ref[1:2, :], first - blocks, blocks, cap)
    absent = absences(nbr_ref, ifc_ref)
    hot = local_hots(nbr_ref, first)
    span = [slice(LANES * t, LANES * (t + 1)) for t in range(tiles)]
    solid = [solid_ref[:, span[t]] for t in range(tiles)]
    bits_ref[:, span[0]] = obits_ref[1]
    bits_ref[:, span[-1]] = obits_ref[0]
    for t in range(1, tiles - 1):
        bits_ref[:, span[t]] = bounce_bits(t, solid, absent)

    def post(q, t):
        if t == 0:
            return outer_ref[1, q]
        return outer_ref[0, q] if t == tiles - 1 else mid_ref[t - 1, q]

    for q in range(Q):
        x = [post(q, t) for t in range(tiles)]
        ghosts = gathers(q, x, hot, None, None)
        for t in range(tiles):
            cur_ref[q, :, span[t]] = pull(
                q, t, x, ghosts, ghosts[0], hot, None, bits_ref[:, span[t]], post(OPP[q], t), pop_ref[q, :, span[t]]
            )


def final_kernel(cur_ref, outer_ref, bits_ref, code_ref, spread_ref, take_ref, cg_ref, far_ref, ra_ref, rb_ref, nbr_ref, out_ref, now_ref, post_ref, fine_ref, buf_ref, ghost_ref, got_ref, sem, *, count):
    position = lax.axis_index("blk")
    blocks, cells = bits_ref.shape
    tiles = cells // LANES
    first = position * blocks
    even = position % 2 == 0
    half, j, k = lanes(blocks)
    span = [slice(LANES * t, LANES * (t + 1)) for t in range(tiles)]
    n = ra_ref.shape[0] - 1

    for s in range(n):
        got_ref[0, s] = dot(take_ref[0], split(jnp.where(even, ra_ref[s], rb_ref[s])))
        got_ref[1, s] = dot(take_ref[1], split(jnp.where(even, rb_ref[s], ra_ref[s])))

    def from_next(s):
        return got_ref[0, s // 2] if s % 2 == 0 else roll(got_ref[0, s // 2], 64)

    def from_prev(s):
        return got_ref[1, s // 2] if s % 2 == 1 else roll(got_ref[1, s // 2], 64)

    up_face, up_layer = side_slots(1)
    low_face, low_layer = side_slots(0)
    up = {q: from_next(s) for s, q in enumerate(up_face)}
    low = {q: from_prev(s) for s, q in enumerate(low_face)}
    code = code_ref[...]
    up_code = both_halves(from_next(2 * n - 1), False)
    low_code = both_halves(from_prev(2 * n - 1), True)
    near = jnp.where(even, ra_ref[n], rb_ref[n])

    rows = coarse_rows(code, both_halves(near, False), count)
    for t in range(tiles):
        for s, v in enumerate(coarse_tile(rows, spread_ref[t])):
            fine_ref[s, :, span[t]] = v
    patched = [q for q in range(Q) if VEL[q][0] or VEL[q][1] < 0]
    for q in patched:
        ex, ey, ez = VEL[q]
        for t in range(tiles):
            v = cur_ref[q, :, span[t]]
            cx, cy, cz = edges(q, t, tiles, half, j, k)
            if ey < 0:
                f = [fine_ref[CROSSING[2].index(q), :, span[m]] for m in range(tiles)]
                g = roll(sources(q, t, f, f[t], half), 64 * abs(ex) - 56 * ey + ez)
                ok = cy
                if cx is not None:
                    ok = ok & jnp.logical_not(cx)
                if cz is not None:
                    ok = ok & jnp.logical_not(cz)
                v = v + jnp.where(ok, g, 0.0)
            if cx is not None:
                ok = cx
                for c in (cy, cz):
                    if c is not None:
                        ok = ok & jnp.logical_not(c)
                v = v + jnp.where(ok, roll(up[q] if ex < 0 else low[q], 64 + 8 * ey + ez), 0.0)
            now_ref[q, :, span[t]] = v

    up_rows = coarse_rows(up_code, both_halves(far_ref[...], False), count)
    low_rows = coarse_rows(low_code, both_halves(cg_ref[...], False), count)
    up_fine = coarse_tile(up_rows, spread_ref[tiles])
    low_fine = coarse_tile(low_rows, spread_ref[tiles])
    for q in range(Q):
        ex, ey, ez = VEL[q]
        _, cy, cz = edges(q, 0, tiles, half, j, k)
        corner = cy if cz is None else (cz if cy is None else cy | cz)
        sides = []
        for e, layer, face, take, mine in (
            (-1, up_layer, up, from_next, outer_ref.at[0]),
            (1, low_layer, low, from_prev, outer_ref.at[1]),
        ):
            if ex == -e:
                v = roll(mine[q], 64 + 8 * ey + ez)
                if corner is not None:
                    v = jnp.where(corner, face[OPP[q]], v)
            else:
                v = take(5 + layer.index(q))
                if ey < 0:
                    f = (up_fine if e < 0 else low_fine)[CROSSING[2].index(q)]
                    ok = cy if cz is None else cy & jnp.logical_not(cz)
                    v = v + jnp.where(ok, roll(f, ez), 0.0)
            sides.append(v)
        ghost_ref[q] = jnp.where(half, sides[1], sides[0])

    def layer_step(g, carry):
        r = pl.ds(pl.multiple_of(8 * g, 8), 8)
        out = collide([ghost_ref[q, r, :] for q in range(Q)])
        for q in range(Q):
            if VEL[q][0]:
                ghost_ref[q, r, :] = out[q]
        return carry

    lax.fori_loop(0, blocks // 8, layer_step, 0)

    def now(q):
        return now_ref if q in patched else cur_ref

    def step(i, carry):
        r = pl.ds(pl.multiple_of(8 * (i // tiles), 8), 8)
        l = pl.ds(pl.multiple_of(LANES * (i % tiles), LANES), LANES)
        out = collide([now(q)[q, r, l] for q in range(Q)])
        for q in range(Q):
            post_ref[q, r, l] = out[q]
        return carry

    lax.fori_loop(0, blocks // 8 * tiles, step, 0)

    rows = coarse_rows(code, both_halves(near, True), count)
    for t in range(tiles):
        for s, v in enumerate(coarse_tile(rows, spread_ref[t])):
            fine_ref[s, :, span[t]] = v
    hot = local_hots(nbr_ref, first)
    remote = {}
    for q in range(Q):
        if VEL[q][0]:
            there = (up_code if VEL[q][0] < 0 else low_code) > 0.5
            remote[q] = jnp.where(there, ghost_ref[q], 0.0)
    copies = []
    for q in range(Q):
        x = [post_ref[q, :, span[t]] for t in range(tiles)]
        ghosts = gathers(q, x, hot, lambda s, t: fine_ref[s, :, span[t]], remote)
        for t in range(tiles):
            buf_ref[q, :, span[t]] = pull(
                q, t, x, ghosts, ghosts[0], hot, None, bits_ref[:, span[t]], post_ref[OPP[q], :, span[t]], now(q)[q, :, span[t]]
            )
        copy = pltpu.make_async_copy(buf_ref.at[q], out_ref.at[q], sem.at[q])
        copy.start()
        copies.append(copy)
    for copy in copies:
        copy.wait()


def shifted(x, by):
    n = lax.axis_size("blk")
    return lax.ppermute(x, "blk", [(i, i + by) for i in range(n) if 0 <= i + by < n])


def swapped(x, off):
    n = lax.axis_size("blk")
    low = [(i, i + 1) for i in range(off, n - 1, 2)]
    return lax.ppermute(x, "blk", low + [(b, a) for a, b in low])


def held(x):
    return pltpu.with_memory_space_constraint(x, pltpu.VMEM)


def body(populations, coarse_faces, neighbors, interface, solid):
    pop = populations.transpose(1, 0, 2)
    co = coarse_faces.transpose(0, 2, 1, 3)
    nbr, ifc = neighbors.T, interface.T
    blocks, cells = pop.shape[1:]
    count = co.shape[0]
    tiles = cells // LANES
    dense = pl.BlockSpec(memory_space=pltpu.VMEM)
    away = pl.BlockSpec(memory_space=pl.ANY)
    cap = blocks // 2
    payload = pltpu.VMEM((11, cap, LANES), F32)
    room = pltpu.CompilerParams(vmem_limit_bytes=20 << 20)
    outer, obits, cg, sa, sb = pl.pallas_call(
        outer_kernel,
        in_specs=[away] + [dense] * 4,
        out_shape=(
            pltpu.VMEM((2, Q, blocks, LANES), F32),
            pltpu.VMEM((2, blocks, LANES), I32),
            pltpu.VMEM((cap, LANES), F32),
            payload,
            payload,
        ),
        scratch_shapes=[
            pltpu.VMEM((2, Q, blocks, LANES), F32),
            pltpu.VMEM((2, 10, cap, LANES), F32),
            pltpu.SemaphoreType.DMA((2,)),
        ],
        name="outer",
    )(pop, nbr, ifc, solid, co)
    ra, rb, far = swapped(sa, 0), swapped(sb, 1), shifted(cg, -2)
    outer, obits = held(outer), held(obits)
    cur, bits, code, spread, take = pl.pallas_call(
        functools.partial(inner_kernel, count=count),
        in_specs=[dense] * 6,
        out_shape=(
            pltpu.VMEM((Q, blocks, cells), F32),
            pltpu.VMEM((blocks, cells), I32),
            pltpu.VMEM((blocks, LANES), F32),
            pltpu.VMEM((tiles + 1, 256, LANES), BF16),
            pltpu.VMEM((2, blocks, 2 * cap), BF16),
        ),
        compiler_params=room,
        scratch_shapes=[pltpu.VMEM((tiles - 2, Q, blocks, LANES), F32)],
        cost_estimate=pl.CostEstimate(flops=100_000_000, bytes_accessed=4_000_000, transcendentals=0),
        name="inner",
    )(pop, nbr, ifc, solid, outer, obits)
    out = pl.pallas_call(
        functools.partial(final_kernel, count=count),
        in_specs=[dense] * 11,
        out_specs=away,
        out_shape=jax.ShapeDtypeStruct(pop.shape, F32),
        scratch_shapes=[
            pltpu.VMEM((Q, blocks, cells), F32),
            pltpu.VMEM((Q, blocks, cells), F32),
            pltpu.VMEM((5, blocks, cells), F32),
            pltpu.VMEM((Q, blocks, cells), F32),
            pltpu.VMEM((Q, blocks, LANES), F32),
            pltpu.VMEM((2, 10, blocks, LANES), F32),
            pltpu.SemaphoreType.DMA((Q,)),
        ],
        compiler_params=room,
        name="final",
    )(*(held(x) for x in (cur, outer, bits, code, spread, take, cg, far, ra, rb)), nbr)
    return out.transpose(1, 0, 2)


def solution(mesh):
    placed = (P("blk", None, None), P("blk", None, None, None), P("blk", None), P("blk", None), P("blk", None))
    return jax.shard_map(body, mesh=mesh, in_specs=placed, out_specs=P("blk", None, None), check_vma=False)
```

time: 31.2 us -> 17 us (0.54)
  waiting for transfers between devices: 10.6 us -> 2.77 us
  Pallas kernels: 11.4 us -> 8.06 us
  starting transfers between devices: 7.5 us -> 5.92 us
  local copies, waits for them, and re-layouts: 1.26 us -> 0.02 us
    ppermute x4 -> x2, waiting for transfers between devices: 5.48 us -> 0.01 us  [swapped(): return lax.ppermute(x, 'blk', low + [(b, a) for a, b in low])]
    pallas_call x3, Pallas kernels: 11.4 us -> 8.06 us  [the longest x1 3.25 us: body(): pl.pallas_call(outer_kernel, in_specs=[away] + [dense] * 4, out_shape=(pl...]
    ppermute x1, waiting for transfers between devices: 5.17 us -> 2.76 us  [shifted(): lax.ppermute(x, 'blk', [(i, i + by) for i in range(n) if 0 <= i + by < n])]
    ppermute x4 -> x2, starting transfers between devices: 5.58 us -> 3.76 us  [swapped(): return lax.ppermute(x, 'blk', low + [(b, a) for a, b in low])]
    unnamed x12 -> x8, local copies, waits for them, and re-layouts: 1.26 us -> 0.02 us
  transfers between devices with their start and end apart: 5 -> 3, of which waited for: 2 -> 1; matrix products, arithmetic and copies ran while one was open for 0% -> 0% of each run, Pallas kernels for 0% -> 9%
where the time goes in v2:
time: 17 us; the launch traced here: 16.8 us
  Pallas kernels  8.06 us (47%)
  starting transfers between devices  5.92 us (35%)
  waiting for transfers between devices  2.77 us (16%)
    ppermute x2, starting transfers between devices, swapped(): return lax.ppermute(x, 'blk', low + [(b, a) for a, b in low])  3.76 us
    pallas_call x1, Pallas kernels, body(): pl.pallas_call(outer_kernel, in_specs=[away] + [dense] * 4, out_shape=(pl...  3.25 us
    pallas_call x1, Pallas kernels, body(): pl.pallas_call(functools.partial(final_kernel, count=count), in_specs=[de...  3.24 us
    ppermute x1, waiting for transfers between devices, shifted(): lax.ppermute(x, 'blk', [(i, i + by) for i in range(n) if 0 <= i + by < n])  2.76 us
    ppermute x1, starting transfers between devices, shifted(): lax.ppermute(x, 'blk', [(i, i + by) for i in range(n) if 0 <= i + by < n])  2.16 us
    pallas_call x1, Pallas kernels, body(): pl.pallas_call(functools.partial(inner_kernel, count=count), in_specs=[de...  1.56 us
  transfers between devices with their start and end apart: 3, of which 1 were waited for; matrix products, arithmetic and copies ran while one was open for 0% of the time, Pallas kernels for 9%

profile of v2, /device:TPU:23, one launch (start us, length us, event | category | flops | bytes accessed | tf_op | source)
XLA Modules:
  0.0 16.8 jit_solution(14974681424883336341)
XLA Ops:
  0.0 0.0 copy-start.1
  0.0 0.0 copy-start.3
  0.0 0.0 copy-start.2
  0.0 0.0 copy-start
  0.0 3.3 %outer.1 = (f32[2,19,32,128]{3,2,1,0:T(8,128)S(1)}, s32[2,32,128]{2,1,0:T(8,128)S(1)}, f32[16,128]{1,0:T(8,128)S(1)}, f32[11,16,128]{2,1,0:T(8,128)S(1)}, f32[11,16,128]{2,1,0:T(8,128)S(1)}) custom-call(f32[19,32,512]{2,1,0:T(8,128)} %bitcast.5, s32[6,32]{1,0:T(8,128)} %bitcast.7, s32[2,32]{1,0:T(2,128)} %bitcast.10, s32[32,512]{1,0:T(8,128)} %solid_ref.3, ...), custom_call_target="tpu_custom_call" | custom-call | tf_op jit(solution)/shard_map/outer/pallas_call | solution.py:608
  3.3 0.7 %collective-permute-start.1 = (f32[11,16,128]{2,1,0:T(8,128)S(1)}, f32[11,16,128]{2,1,0:T(8,128)S(1)}, u32[]{:S(2)}, u32[]{:S(2)}) collective-permute-start(f32[11,16,128]{2,1,0:T(8,128)S(1)} %get-tuple-element.23), channel_id=1, source_target_pairs={{0,1},{2,3},{4,5},{6,7},{8,9},{10,11},{12,13},{14,15},{16,17},{18,... | collective-permute-start | bytes 270344 | tf_op jit(solution)/shard_map/ppermute | solution.py:589
  4.0 3.0 %collective-permute-start.2 = (f32[11,16,128]{2,1,0:T(8,128)S(1)}, f32[11,16,128]{2,1,0:T(8,128)S(1)}, u32[]{:S(2)}, u32[]{:S(2)}) collective-permute-start(f32[11,16,128]{2,1,0:T(8,128)S(1)} %get-tuple-element.24), channel_id=1, source_target_pairs={{1,2},{3,4},{5,6},{7,8},{9,10},{11,12},{13,14},{15,16},{17,18},{19... | collective-permute-start | bytes 270344 | tf_op jit(solution)/shard_map/ppermute | solution.py:589
  7.0 2.2 %collective-permute-start = (f32[16,128]{1,0:T(8,128)S(1)}, f32[16,128]{1,0:T(8,128)S(1)}, u32[]{:S(2)}, u32[]{:S(2)}) collective-permute-start(f32[16,128]{1,0:T(8,128)S(1)} %get-tuple-element.22.cg_ref), channel_id=1, source_target_pairs={{2,0},{3,1},{4,2},{5,3},{6,4},{7,5},{8,6},{9,7},{10,8},{11,9},{12,... | collective-permute-start | bytes 24584 | tf_op jit(solution)/shard_map/ppermute | solution.py:583
  9.2 0.0 copy-done.1
  9.2 0.0 copy-done.3
  9.2 0.0 copy-done.2
  9.2 0.0 copy-done
  9.3 1.6 %inner.1 = (f32[19,32,512]{2,1,0:T(8,128)S(1)}, s32[32,512]{1,0:T(8,128)S(1)}, f32[32,128]{1,0:T(8,128)S(1)}, bf16[5,256,128]{2,1,0:T(8,128)(2,1)S(1)}, bf16[2,32,32]{2,1,0:T(8,128)(2,1)S(1)}) custom-call(f32[19,32,512]{2,1,0:T(8,128)S(1)} %bitcast.6, s32[6,32]{1,0:T(8,128)S(1)} %bitcast.8, s32[2,32]{1,0:T(2,128)S(1)} %bitcast.11, s32[32,512]{1,0:T(8,128)S(1)} %copy-done.1, ...), custom_call_target="tpu_custom_call" | custom-call | flops 100000000 | bytes 4000000 | tf_op jit(solution)/shard_map/inner/pallas_call | solution.py:627
  10.8 2.8 %collective-permute-done.far_ref = f32[16,128]{1,0:T(8,128)S(1)} collective-permute-done((f32[16,128]{1,0:T(8,128)S(1)}, f32[16,128]{1,0:T(8,128)S(1)}, u32[]{:S(2)}, u32[]{:S(2)}) %collective-permute-start) | collective-permute-done | bytes 8224 | tf_op jit(solution)/shard_map/ppermute | solution.py:583
  13.6 0.0 collective-permute-done.1.ra_ref
  13.6 0.0 collective-permute-done.2.rb_ref
  13.6 3.2 %final.1 = f32[19,32,512]{2,1,0:T(8,128)} custom-call(f32[19,32,512]{2,1,0:T(8,128)S(1)} %get-tuple-element.17.cur_ref, f32[2,19,32,128]{3,2,1,0:T(8,128)S(1)} %get-tuple-element.15.outer_ref, s32[32,512]{1,0:T(8,128)S(1)} %get-tuple-element.18.bits_ref, f32[32,128]{1,0:T(8,128)S(1)} %get-tuple-element.19.code_ref, ...), custom_call_target="tpu_custom_call" | custom-call | tf_op jit(solution)/shard_map/final/pallas_call | solution.py:642
Async XLA Ops:
  0.0 9.2 %copy-start.1 = (s32[32,512]{1,0:T(8,128)S(1)}, s32[32,512]{1,0:T(8,128)}, u32[]{:S(2)}) copy-start(s32[32,512]{1,0:T(8,128)} %solid_ref.3) | copy-start | bytes 196612
  0.0 9.2 %copy-start.3 = (s32[32,2]{0,1:T(2,128)S(1)}, s32[32,2]{0,1:T(2,128)}, u32[]{:S(2)}) copy-start(s32[32,2]{0,1:T(2,128)} %param.8) | copy-start | bytes 772
  0.0 9.2 %copy-start.2 = (s32[32,6]{0,1:T(8,128)S(1)}, s32[32,6]{0,1:T(8,128)}, u32[]{:S(2)}) copy-start(s32[32,6]{0,1:T(8,128)} %param.7) | copy-start | bytes 2308
  0.0 9.2 %copy-start = (f32[32,19,512]{2,0,1:T(8,128)S(1)}, f32[32,19,512]{2,0,1:T(8,128)}, u32[]{:S(2)}) copy-start(f32[32,19,512]{2,0,1:T(8,128)} %param.5) | copy-start | bytes 3735556
  3.3 10.3 %collective-permute-start.1 = (f32[11,16,128]{2,1,0:T(8,128)S(1)}, f32[11,16,128]{2,1,0:T(8,128)S(1)}, u32[]{:S(2)}, u32[]{:S(2)}) collective-permute-start(f32[11,16,128]{2,1,0:T(8,128)S(1)} %get-tuple-element.23), channel_id=1, source_target_pairs={{0,1},{2,3},{4,5},{6,7},{8,9},{10,11},{12,13},{14,15},{16,17},{18,... | collective-permute-start | bytes 270344 | tf_op jit(solution)/shard_map/ppermute | solution.py:589
  4.0 9.6 %collective-permute-start.2 = (f32[11,16,128]{2,1,0:T(8,128)S(1)}, f32[11,16,128]{2,1,0:T(8,128)S(1)}, u32[]{:S(2)}, u32[]{:S(2)}) collective-permute-start(f32[11,16,128]{2,1,0:T(8,128)S(1)} %get-tuple-element.24), channel_id=1, source_target_pairs={{1,2},{3,4},{5,6},{7,8},{9,10},{11,12},{13,14},{15,16},{17,18},{19... | collective-permute-start | bytes 270344 | tf_op jit(solution)/shard_map/ppermute | solution.py:589
  7.0 6.5 %collective-permute-start = (f32[16,128]{1,0:T(8,128)S(1)}, f32[16,128]{1,0:T(8,128)S(1)}, u32[]{:S(2)}, u32[]{:S(2)}) collective-permute-start(f32[16,128]{1,0:T(8,128)S(1)} %get-tuple-element.22.cg_ref), channel_id=1, source_target_pairs={{2,0},{3,1},{4,2},{5,3},{6,4},{7,5},{8,6},{9,7},{10,8},{11,9},{12,... | collective-permute-start | bytes 24584 | tf_op jit(solution)/shard_map/ppermute | solution.py:583

commit v3 on v2

--- a/solution.py
+++ b/solution.py
@@ -337,7 +337,12 @@
     return [q for q in range(Q) if VEL[q][0] == e], [q for q in range(Q) if VEL[q][0] != -e]
 
 
-def outer_kernel(pop_ref, nbr_ref, ifc_ref, solid_ref, co_ref, post_ref, bits_ref, cg_ref, sa_ref, sb_ref, buf_ref, pack_ref, sem):
+def outer_kernel(pop_ref, *refs):
+    given, (post_ref, bits_ref, cg_ref, sa_ref, sb_ref), (buf_ref, pack_ref, *held_refs, sem) = refs[:4], refs[4:9], refs[9:]
+    small = [pltpu.make_async_copy(a, b, sem.at[2 + i]) for i, (a, b) in enumerate(zip(given, held_refs))]
+    for copy in small:
+        copy.start()
+    nbr_ref, ifc_ref, solid_ref, co_ref = held_refs
     position = lax.axis_index("blk")
     blocks = solid_ref.shape[0]
     tiles = solid_ref.shape[1] // LANES
@@ -352,6 +357,8 @@
         copy.start()
         copies.append(copy)
     half, j, k = lanes(blocks)
+    for copy in small:
+        copy.wait()
     coarse_values(co_ref, cg_ref)
     code = coarse_code(ifc_ref, position, count)
     absent = absences(nbr_ref, ifc_ref)
@@ -448,11 +455,14 @@
             )
 
 
-def final_kernel(cur_ref, outer_ref, bits_ref, code_ref, spread_ref, take_ref, cg_ref, far_ref, ra_ref, rb_ref, nbr_ref, out_ref, now_ref, post_ref, fine_ref, buf_ref, ghost_ref, got_ref, sem, *, count):
+def patched(q):
+    return VEL[q][0] != 0 or VEL[q][1] < 0
+
+
+def current_kernel(cur_ref, outer_ref, code_ref, spread_ref, take_ref, cg_ref, ra_ref, rb_ref, now_ref, post_ref, fine_ref, ghost_ref, codes_ref, got_ref, *, count):
     position = lax.axis_index("blk")
-    blocks, cells = bits_ref.shape
+    blocks, cells = cur_ref.shape[1:]
     tiles = cells // LANES
-    first = position * blocks
     even = position % 2 == 0
     half, j, k = lanes(blocks)
     span = [slice(LANES * t, LANES * (t + 1)) for t in range(tiles)]
@@ -475,14 +485,15 @@
     code = code_ref[...]
     up_code = both_halves(from_next(2 * n - 1), False)
     low_code = both_halves(from_prev(2 * n - 1), True)
+    codes_ref[0] = up_code
+    codes_ref[1] = low_code
     near = jnp.where(even, ra_ref[n], rb_ref[n])
 
     rows = coarse_rows(code, both_halves(near, False), count)
     for t in range(tiles):
         for s, v in enumerate(coarse_tile(rows, spread_ref[t])):
             fine_ref[s, :, span[t]] = v
-    patched = [q for q in range(Q) if VEL[q][0] or VEL[q][1] < 0]
-    for q in patched:
+    for q in range(Q):
         ex, ey, ez = VEL[q]
         for t in range(tiles):
             v = cur_ref[q, :, span[t]]
@@ -504,9 +515,7 @@
                 v = v + jnp.where(ok, roll(up[q] if ex < 0 else low[q], 64 + 8 * ey + ez), 0.0)
             now_ref[q, :, span[t]] = v
 
-    up_rows = coarse_rows(up_code, both_halves(far_ref[...], False), count)
     low_rows = coarse_rows(low_code, both_halves(cg_ref[...], False), count)
-    up_fine = coarse_tile(up_rows, spread_ref[tiles])
     low_fine = coarse_tile(low_rows, spread_ref[tiles])
     for q in range(Q):
         ex, ey, ez = VEL[q]
@@ -523,12 +532,46 @@
                     v = jnp.where(corner, face[OPP[q]], v)
             else:
                 v = take(5 + layer.index(q))
-                if ey < 0:
-                    f = (up_fine if e < 0 else low_fine)[CROSSING[2].index(q)]
+                if ey < 0 and e > 0:
                     ok = cy if cz is None else cy & jnp.logical_not(cz)
-                    v = v + jnp.where(ok, roll(f, ez), 0.0)
+                    v = v + jnp.where(ok, roll(low_fine[CROSSING[2].index(q)], ez), 0.0)
             sides.append(v)
         ghost_ref[q] = jnp.where(half, sides[1], sides[0])
+
+    def step(i, carry):
+        r = pl.ds(pl.multiple_of(8 * (i // tiles), 8), 8)
+        l = pl.ds(pl.multiple_of(LANES * (i % tiles), LANES), LANES)
+        out = collide([now_ref[q, r, l] for q in range(Q)])
+        for q in range(Q):
+            post_ref[q, r, l] = out[q]
+        return carry
+
+    lax.fori_loop(0, blocks // 8 * tiles, step, 0)
+
+    rows = coarse_rows(code, both_halves(near, True), count)
+    for t in range(tiles):
+        for s, v in enumerate(coarse_tile(rows, spread_ref[t])):
+            fine_ref[s, :, span[t]] = v
+
+
+def final_kernel(now_ref, post_ref, fine_ref, half_ref, codes_ref, bits_ref, spread_ref, far_ref, nbr_ref, out_ref, buf_ref, ghost_ref, sem, *, count):
+    position = lax.axis_index("blk")
+    blocks, cells = bits_ref.shape
+    tiles = cells // LANES
+    first = position * blocks
+    half, j, k = lanes(blocks)
+    span = [slice(LANES * t, LANES * (t + 1)) for t in range(tiles)]
+    up_rows = coarse_rows(codes_ref[0], both_halves(far_ref[...], False), count)
+    up_fine = coarse_tile(up_rows, spread_ref[tiles])
+    for q in range(Q):
+        v = half_ref[q]
+        if VEL[q][1] < 0 and VEL[q][0] <= 0:
+            _, cy, cz = edges(q, 0, tiles, half, j, k)
+            ok = cy & jnp.logical_not(half)
+            if cz is not None:
+                ok = ok & jnp.logical_not(cz)
+            v = v + jnp.where(ok, roll(up_fine[CROSSING[2].index(q)], VEL[q][2]), 0.0)
+        ghost_ref[q] = v
 
     def layer_step(g, carry):
         r = pl.ds(pl.multiple_of(8 * g, 8), 8)
@@ -539,29 +582,11 @@
         return carry
 
     lax.fori_loop(0, blocks // 8, layer_step, 0)
-
-    def now(q):
-        return now_ref if q in patched else cur_ref
-
-    def step(i, carry):
-        r = pl.ds(pl.multiple_of(8 * (i // tiles), 8), 8)
-        l = pl.ds(pl.multiple_of(LANES * (i % tiles), LANES), LANES)
-        out = collide([now(q)[q, r, l] for q in range(Q)])
-        for q in range(Q):
-            post_ref[q, r, l] = out[q]
-        return carry
-
-    lax.fori_loop(0, blocks // 8 * tiles, step, 0)
-
-    rows = coarse_rows(code, both_halves(near, True), count)
-    for t in range(tiles):
-        for s, v in enumerate(coarse_tile(rows, spread_ref[t])):
-            fine_ref[s, :, span[t]] = v
     hot = local_hots(nbr_ref, first)
     remote = {}
     for q in range(Q):
         if VEL[q][0]:
-            there = (up_code if VEL[q][0] < 0 else low_code) > 0.5
+            there = codes_ref[0 if VEL[q][0] < 0 else 1] > 0.5
             remote[q] = jnp.where(there, ghost_ref[q], 0.0)
     copies = []
     for q in range(Q):
@@ -569,7 +594,7 @@
         ghosts = gathers(q, x, hot, lambda s, t: fine_ref[s, :, span[t]], remote)
         for t in range(tiles):
             buf_ref[q, :, span[t]] = pull(
-                q, t, x, ghosts, ghosts[0], hot, None, bits_ref[:, span[t]], post_ref[OPP[q], :, span[t]], now(q)[q, :, span[t]]
+                q, t, x, ghosts, ghosts[0], hot, None, bits_ref[:, span[t]], post_ref[OPP[q], :, span[t]], now_ref[q, :, span[t]]
             )
         copy = pltpu.make_async_copy(buf_ref.at[q], out_ref.at[q], sem.at[q])
         copy.start()
@@ -607,7 +632,7 @@
     room = pltpu.CompilerParams(vmem_limit_bytes=20 << 20)
     outer, obits, cg, sa, sb = pl.pallas_call(
         outer_kernel,
-        in_specs=[away] + [dense] * 4,
+        in_specs=[away] * 5,
         out_shape=(
             pltpu.VMEM((2, Q, blocks, LANES), F32),
             pltpu.VMEM((2, blocks, LANES), I32),
@@ -618,11 +643,14 @@
         scratch_shapes=[
             pltpu.VMEM((2, Q, blocks, LANES), F32),
             pltpu.VMEM((2, 10, cap, LANES), F32),
-            pltpu.SemaphoreType.DMA((2,)),
+            *(pltpu.VMEM(a.shape, a.dtype) for a in (nbr, ifc, solid, co)),
+            pltpu.SemaphoreType.DMA((6,)),
         ],
         name="outer",
     )(pop, nbr, ifc, solid, co)
-    ra, rb, far = swapped(sa, 0), swapped(sb, 1), shifted(cg, -2)
+    rb = swapped(sb, 1)
+    far = shifted(cg, -2)
+    ra = swapped(sa, 0)
     outer, obits = held(outer), held(obits)
     cur, bits, code, spread, take = pl.pallas_call(
         functools.partial(inner_kernel, count=count),
@@ -639,23 +667,26 @@
         cost_estimate=pl.CostEstimate(flops=100_000_000, bytes_accessed=4_000_000, transcendentals=0),
         name="inner",
     )(pop, nbr, ifc, solid, outer, obits)
+    state = pltpu.VMEM((Q, blocks, cells), F32)
+    layer = pltpu.VMEM((Q, blocks, LANES), F32)
+    now, post, fine, ghost, codes = pl.pallas_call(
+        functools.partial(current_kernel, count=count),
+        in_specs=[dense] * 8,
+        out_shape=(state, state, pltpu.VMEM((5, blocks, cells), F32), layer, pltpu.VMEM((2, blocks, LANES), F32)),
+        scratch_shapes=[pltpu.VMEM((2, 10, blocks, LANES), F32)],
+        compiler_params=room,
+        cost_estimate=pl.CostEstimate(flops=100_000_000, bytes_accessed=4_000_000, transcendentals=0),
+        name="current",
+    )(*(held(x) for x in (cur, outer, code, spread, take, cg, ra, rb)))
     out = pl.pallas_call(
         functools.partial(final_kernel, count=count),
-        in_specs=[dense] * 11,
+        in_specs=[dense] * 9,
         out_specs=away,
         out_shape=jax.ShapeDtypeStruct(pop.shape, F32),
-        scratch_shapes=[
-            pltpu.VMEM((Q, blocks, cells), F32),
-            pltpu.VMEM((Q, blocks, cells), F32),
-            pltpu.VMEM((5, blocks, cells), F32),
-            pltpu.VMEM((Q, blocks, cells), F32),
-            pltpu.VMEM((Q, blocks, LANES), F32),
-            pltpu.VMEM((2, 10, blocks, LANES), F32),
-            pltpu.SemaphoreType.DMA((Q,)),
-        ],
+        scratch_shapes=[state, layer, pltpu.SemaphoreType.DMA((Q,))],
         compiler_params=room,
         name="final",
-    )(*(held(x) for x in (cur, outer, bits, code, spread, take, cg, far, ra, rb)), nbr)
+    )(*(held(x) for x in (now, post, fine, ghost, codes, bits, spread, far)), nbr)
     return out.transpose(1, 0, 2)
 
 

time: 17 us -> 16 us (0.941)
  the two profiles are of different devices: /device:TPU:23 before, /device:TPU:25 now
where the time goes in v3:
time: 16 us; the launch traced here: 15.9 us
  Pallas kernels  8.01 us (50%)
  starting transfers between devices  7.72 us (48%)
    ppermute x1, starting transfers between devices, shifted(): lax.ppermute(x, 'blk', [(i, i + by) for i in range(n) if 0 <= i + by < n])  3.96 us
    ppermute x2, starting transfers between devices, swapped(): return lax.ppermute(x, 'blk', low + [(b, a) for a, b in low])  3.76 us
    pallas_call x1, Pallas kernels, body(): pl.pallas_call(outer_kernel, in_specs=[away] * 5, out_shape=(pltpu.VMEM((...  2.57 us
    pallas_call x1, Pallas kernels, body(): pl.pallas_call(functools.partial(final_kernel, count=count), in_specs=[de...  2.18 us
    pallas_call x1, Pallas kernels, body(): pl.pallas_call(functools.partial(current_kernel, count=count), in_specs=[...  1.69 us
    pallas_call x1, Pallas kernels, body(): pl.pallas_call(functools.partial(inner_kernel, count=count), in_specs=[de...  1.57 us
  transfers between devices with their start and end apart: 3, of which 0 were waited for; matrix products, arithmetic and copies ran while one was open for 0% of the time, Pallas kernels for 20%

profile of v3, /device:TPU:25, one launch (start us, length us, event | category | flops | bytes accessed | tf_op | source)
XLA Modules:
  0.0 15.9 jit_solution(1682700672689823387)
XLA Ops:
  0.0 0.0 copy-start.2
  0.0 0.0 copy-start
  0.0 0.0 copy-start.3
  0.0 0.0 copy-start.1
  0.0 2.6 %outer.1 = (f32[2,19,32,128]{3,2,1,0:T(8,128)S(1)}, s32[2,32,128]{2,1,0:T(8,128)S(1)}, f32[16,128]{1,0:T(8,128)S(1)}, f32[11,16,128]{2,1,0:T(8,128)S(1)}, f32[11,16,128]{2,1,0:T(8,128)S(1)}) custom-call(f32[19,32,512]{2,1,0:T(8,128)} %bitcast.5, s32[6,32]{1,0:T(8,128)} %bitcast.7, s32[2,32]{1,0:T(2,128)} %bitcast.10, s32[32,512]{1,0:T(8,128)} %solid_ref.1, ...), custom_call_target="tpu_custom_call" | custom-call | tf_op jit(solution)/shard_map/outer/pallas_call | solution.py:633
  2.6 0.7 %collective-permute-start = (f32[11,16,128]{2,1,0:T(8,128)S(1)}, f32[11,16,128]{2,1,0:T(8,128)S(1)}, u32[]{:S(2)}, u32[]{:S(2)}) collective-permute-start(f32[11,16,128]{2,1,0:T(8,128)S(1)} %get-tuple-element.27), channel_id=1, source_target_pairs={{0,1},{2,3},{4,5},{6,7},{8,9},{10,11},{12,13},{14,15},{16,17},{18,... | collective-permute-start | bytes 270344 | tf_op jit(solution)/shard_map/ppermute | solution.py:614
  3.3 3.0 %collective-permute-start.1 = (f32[11,16,128]{2,1,0:T(8,128)S(1)}, f32[11,16,128]{2,1,0:T(8,128)S(1)}, u32[]{:S(2)}, u32[]{:S(2)}) collective-permute-start(f32[11,16,128]{2,1,0:T(8,128)S(1)} %get-tuple-element.28), channel_id=1, source_target_pairs={{1,2},{3,4},{5,6},{7,8},{9,10},{11,12},{13,14},{15,16},{17,18},{19... | collective-permute-start | bytes 270344 | tf_op jit(solution)/shard_map/ppermute | solution.py:614
  6.4 4.0 %collective-permute-start.2 = (f32[16,128]{1,0:T(8,128)S(1)}, f32[16,128]{1,0:T(8,128)S(1)}, u32[]{:S(2)}, u32[]{:S(2)}) collective-permute-start(f32[16,128]{1,0:T(8,128)S(1)} %get-tuple-element.26.cg_ref), channel_id=1, source_target_pairs={{2,0},{3,1},{4,2},{5,3},{6,4},{7,5},{8,6},{9,7},{10,8},{11,9},{12,... | collective-permute-start | bytes 24584 | tf_op jit(solution)/shard_map/ppermute | solution.py:608
  10.3 0.0 copy-done.2
  10.3 0.0 copy-done
  10.3 0.0 copy-done.3
  10.4 0.0 copy-done.1
  10.4 1.6 %inner.1 = (f32[19,32,512]{2,1,0:T(8,128)S(1)}, s32[32,512]{1,0:T(8,128)S(1)}, f32[32,128]{1,0:T(8,128)S(1)}, bf16[5,256,128]{2,1,0:T(8,128)(2,1)S(1)}, bf16[2,32,32]{2,1,0:T(8,128)(2,1)S(1)}) custom-call(f32[19,32,512]{2,1,0:T(8,128)S(1)} %bitcast.6, s32[6,32]{1,0:T(8,128)S(1)} %bitcast.8, s32[2,32]{1,0:T(2,128)S(1)} %bitcast.11, s32[32,512]{1,0:T(8,128)S(1)} %copy-done.1, ...), custom_call_target="tpu_custom_call" | custom-call | flops 100000000 | bytes 4000000 | tf_op jit(solution)/shard_map/inner/pallas_call | solution.py:655
  11.9 0.0 collective-permute-done.ra_ref
  12.0 0.0 collective-permute-done.1.rb_ref
  12.0 1.7 %current.1 = (f32[19,32,512]{2,1,0:T(8,128)S(1)}, f32[19,32,512]{2,1,0:T(8,128)S(1)}, f32[5,32,512]{2,1,0:T(8,128)S(1)}, f32[19,32,128]{2,1,0:T(8,128)S(1)}, f32[2,32,128]{2,1,0:T(8,128)S(1)}) custom-call(f32[19,32,512]{2,1,0:T(8,128)S(1)} %get-tuple-element.22.cur_ref, f32[2,19,32,128]{3,2,1,0:T(8,128)S(1)} %get-tuple-element.20.outer_ref, ...), custom_call_target="tpu_custom_call" | custom-call | flops 100000000 | bytes 4000000 | tf_op jit(solution)/shard_map/current/pallas_call | solution.py:672
  13.7 0.0 collective-permute-done.2.far_ref
  13.7 2.2 %final.1 = f32[19,32,512]{2,1,0:T(8,128)} custom-call(f32[19,32,512]{2,1,0:T(8,128)S(1)} %get-tuple-element.29.now_ref, f32[19,32,512]{2,1,0:T(8,128)S(1)} %get-tuple-element.30.post_ref, f32[5,32,512]{2,1,0:T(8,128)S(1)} %get-tuple-element.31.fine_ref, f32[19,32,128]{2,1,0:T(8,128)S(1)} %get-tuple-element.32.half_ref, ...), custom_call_target="tpu_custom_call" | custom-call | tf_op jit(solution)/shard_map/final/pallas_call | solution.py:681
Async XLA Ops:
  0.0 10.3 %copy-start.2 = (s32[32,6]{0,1:T(8,128)S(1)}, s32[32,6]{0,1:T(8,128)}, u32[]{:S(2)}) copy-start(s32[32,6]{0,1:T(8,128)} %param.7) | copy-start | bytes 2308
  0.0 10.3 %copy-start = (f32[32,19,512]{2,0,1:T(8,128)S(1)}, f32[32,19,512]{2,0,1:T(8,128)}, u32[]{:S(2)}) copy-start(f32[32,19,512]{2,0,1:T(8,128)} %param.5) | copy-start | bytes 3735556
  0.0 10.3 %copy-start.3 = (s32[32,2]{0,1:T(2,128)S(1)}, s32[32,2]{0,1:T(2,128)}, u32[]{:S(2)}) copy-start(s32[32,2]{0,1:T(2,128)} %param.8) | copy-start | bytes 772
  0.0 10.4 %copy-start.1 = (s32[32,512]{1,0:T(8,128)S(1)}, s32[32,512]{1,0:T(8,128)}, u32[]{:S(2)}) copy-start(s32[32,512]{1,0:T(8,128)} %solid_ref.1) | copy-start | bytes 196612
  2.6 9.4 %collective-permute-start = (f32[11,16,128]{2,1,0:T(8,128)S(1)}, f32[11,16,128]{2,1,0:T(8,128)S(1)}, u32[]{:S(2)}, u32[]{:S(2)}) collective-permute-start(f32[11,16,128]{2,1,0:T(8,128)S(1)} %get-tuple-element.27), channel_id=1, source_target_pairs={{0,1},{2,3},{4,5},{6,7},{8,9},{10,11},{12,13},{14,15},{16,17},{18,... | collective-permute-start | bytes 270344 | tf_op jit(solution)/shard_map/ppermute | solution.py:614
  3.3 8.6 %collective-permute-start.1 = (f32[11,16,128]{2,1,0:T(8,128)S(1)}, f32[11,16,128]{2,1,0:T(8,128)S(1)}, u32[]{:S(2)}, u32[]{:S(2)}) collective-permute-start(f32[11,16,128]{2,1,0:T(8,128)S(1)} %get-tuple-element.28), channel_id=1, source_target_pairs={{1,2},{3,4},{5,6},{7,8},{9,10},{11,12},{13,14},{15,16},{17,18},{19... | collective-permute-start | bytes 270344 | tf_op jit(solution)/shard_map/ppermute | solution.py:614
  6.4 7.3 %collective-permute-start.2 = (f32[16,128]{1,0:T(8,128)S(1)}, f32[16,128]{1,0:T(8,128)S(1)}, u32[]{:S(2)}, u32[]{:S(2)}) collective-permute-start(f32[16,128]{1,0:T(8,128)S(1)} %get-tuple-element.26.cg_ref), channel_id=1, source_target_pairs={{2,0},{3,1},{4,2},{5,3},{6,4},{7,5},{8,6},{9,7},{10,8},{11,9},{12,... | collective-permute-start | bytes 24584 | tf_op jit(solution)/shard_map/ppermute | solution.py:608

commit v4 on v3

--- a/solution.py
+++ b/solution.py
@@ -7,6 +7,7 @@
 from jax.experimental import pallas as pl
 from jax.experimental.pallas import tpu as pltpu
 from jax.sharding import PartitionSpec as P
+
 
 F32, BF16, I32 = jnp.float32, jnp.bfloat16, jnp.int32
 LANES = 128
@@ -237,19 +238,23 @@
     return spread_rows(code)
 
 
-def coarse_values(co_ref, cg_ref):
+def pack_kernel(part_ref, co_ref, far_co_ref, send_ref):
+    refs = (co_ref, far_co_ref)
     count = co_ref.shape[0]
+    n = part_ref.shape[0]
+    send_ref[:n] = part_ref[...]
     h = []
     for q in range(Q):
-        h0 = co_ref[:, q, 0, :]
-        h1 = (1.0 - 0.5) * h0 + 0.5 * co_ref[:, q, 1, :]
+        h0 = jnp.concatenate([r[:, q, 0, :] for r in refs], axis=0)
+        h1 = (1.0 - 0.5) * h0 + 0.5 * jnp.concatenate([r[:, q, 1, :] for r in refs], axis=0)
         h.append(jnp.concatenate([h0, h1], axis=1))
     e = feq(h)
-    cg_ref[...] = jnp.zeros_like(cg_ref)
+    send_ref[n:] = jnp.zeros_like(send_ref[n:])
     for s, q in enumerate(CROSSING[2]):
         v = e[q] + (0.6 / 1.1) * (h[q] - e[q])
-        for c in range(count):
-            cg_ref[5 * c + s : 5 * c + s + 1, :] = v[c : c + 1]
+        for o in range(2):
+            for c in range(count):
+                send_ref[n + o, 5 * c + s : 5 * c + s + 1, :] = v[count * o + c : count * o + c + 1]
 
 
 def both_halves(x, upper):
@@ -295,7 +300,7 @@
     return [g[b * s : b * (s + 1)] for s in range(5)]
 
 
-def pull(q, t, x, parts, gx, hot, fine, bits, bounced, init):
+def pull(q, t, x, parts, gx, bits, bounced, init):
     if q == 0:
         return jnp.where((bits & 1) != 0, init, x[t])
     half, j, k = lanes(bits.shape[0])
@@ -337,84 +342,108 @@
     return [q for q in range(Q) if VEL[q][0] == e], [q for q in range(Q) if VEL[q][0] != -e]
 
 
-def outer_kernel(pop_ref, *refs):
-    given, (post_ref, bits_ref, cg_ref, sa_ref, sb_ref), (buf_ref, pack_ref, *held_refs, sem) = refs[:4], refs[4:9], refs[9:]
-    small = [pltpu.make_async_copy(a, b, sem.at[2 + i]) for i, (a, b) in enumerate(zip(given, held_refs))]
-    for copy in small:
-        copy.start()
-    nbr_ref, ifc_ref, solid_ref, co_ref = held_refs
+def prepare_side(side, load, nbr_ref, solid, bits_put, post_ref, send_ref, hot, absent, code, first, ready=None):
+    tiles = len(solid)
+    blocks = solid[0].shape[0]
+    t = tiles - 1 if side == 0 else 0
+    half, j, k = lanes(blocks)
+    bits = bounce_bits(t, solid, absent)
+    bits_put(t, bits)
+    if ready is not None:
+        ready()
+
+    def step(g, carry):
+        r = pl.ds(pl.multiple_of(8 * g, 8), 8)
+        out = collide([load(q, r, t) for q in range(Q)])
+        for q in range(Q):
+            post_ref[side, q, r, :] = out[q]
+        return carry
+
+    lax.fori_loop(0, blocks // 8, step, 0)
+    to = send_rows(nbr_ref[side : side + 1, :], first + (blocks if side == 0 else -blocks), blocks, send_ref.shape[1])
+    face, layer = side_slots(side)
+    slots = [post_ref[side, q] for q in face]
+    for q in layer:
+        ex, ey, ez = VEL[q]
+        x = post_ref[side, q]
+        turn = 64 * abs(ex)
+        out = roll(x, turn + 8 * ey + ez)
+        _, cy, cz = edges(q, t, tiles, half, j, k)
+        if ey or ez:
+            parts = split(x)
+        if ey:
+            out = jnp.where(cy, roll(dot(hot[face_of(1, ey)], parts), turn - 56 * ey + ez), out)
+        if ez:
+            out = jnp.where(cz, roll(dot(hot[face_of(2, ez)], parts), turn + 8 * ey - 7 * ez), out)
+        if q:
+            out = jnp.where((bits & (1 << q)) != 0, post_ref[side, OPP[q]], out)
+        slots.append(out)
+    slots.append(code)
+    for s in range(0, len(slots), 2):
+        a, b = slots[s], slots[s + 1]
+        packed = jnp.where(half, b, roll(a, 64)) if side == 0 else jnp.where(half, roll(b, 64), a)
+        send_ref[s // 2] = dot(to, split(packed))
+
+
+def outer_kernel(pop_hbm, *refs):
+    given, (post_ref, bits_ref, co_ref, send_ref), (tile_ref, *small_refs, sem) = refs[:4], refs[4:8], refs[8:]
+    nbr_ref, ifc_ref, solid_ref = small_refs
     position = lax.axis_index("blk")
     blocks = solid_ref.shape[0]
     tiles = solid_ref.shape[1] // LANES
+    even = position % 2 == 0
+    mine = pl.ds(pl.multiple_of(jnp.where(even, 0, LANES * (tiles - 1)), LANES), LANES)
+    pairs = [(pop_hbm.at[:, :, mine], tile_ref), *zip(given, (*small_refs, co_ref))]
+    copies = [pltpu.make_async_copy(a, b, sem.at[i]) for i, (a, b) in enumerate(pairs)]
+    for copy in copies[1:] + copies[:1]:
+        copy.start()
+    for copy in copies[1:]:
+        copy.wait()
     first = position * blocks
-    even = position % 2 == 0
-    count = co_ref.shape[0]
-    copies = []
-    for side, t in ((0, tiles - 1), (1, 0)):
-        copy = pltpu.make_async_copy(
-            pop_ref.at[:, :, pl.ds(LANES * t, LANES)], buf_ref.at[side], sem.at[side]
-        )
-        copy.start()
-        copies.append(copy)
-    half, j, k = lanes(blocks)
-    for copy in small:
-        copy.wait()
-    coarse_values(co_ref, cg_ref)
-    code = coarse_code(ifc_ref, position, count)
+    code = coarse_code(ifc_ref, position, co_ref.shape[0])
     absent = absences(nbr_ref, ifc_ref)
     hot = local_hots(nbr_ref, first)
     solid = [solid_ref[:, LANES * t : LANES * (t + 1)] for t in range(tiles)]
-    bits_ref[0] = bounce_bits(tiles - 1, solid, absent)
-    bits_ref[1] = bounce_bits(0, solid, absent)
-    for side, t in ((0, tiles - 1), (1, 0)):
-        copies[side].wait()
-
-        def step(g, carry, side=side):
-            r = pl.ds(pl.multiple_of(8 * g, 8), 8)
-            out = collide([buf_ref[side, q, r, :] for q in range(Q)])
-            for q in range(Q):
-                post_ref[side, q, r, :] = out[q]
-            return carry
-
-        lax.fori_loop(0, blocks // 8, step, 0)
-        bits = bits_ref[side]
-        to = send_rows(nbr_ref[side : side + 1, :], first + (blocks if side == 0 else -blocks), blocks, pack_ref.shape[2])
-        face, layer = side_slots(side)
-        slots = [post_ref[side, q] for q in face]
-        for q in layer:
-            ex, ey, ez = VEL[q]
-            x = post_ref[side, q]
-            turn = 64 * abs(ex)
-            out = roll(x, turn + 8 * ey + ez)
-            _, cy, cz = edges(q, t, tiles, half, j, k)
-            if ey or ez:
-                parts = split(x)
-            if ey:
-                out = jnp.where(cy, roll(dot(hot[face_of(1, ey)], parts), turn - 56 * ey + ez), out)
-            if ez:
-                out = jnp.where(cz, roll(dot(hot[face_of(2, ez)], parts), turn + 8 * ey - 7 * ez), out)
-            if q:
-                out = jnp.where((bits & (1 << q)) != 0, post_ref[side, OPP[q]], out)
-            slots.append(out)
-        slots.append(code)
-        for s in range(0, len(slots), 2):
-            a, b = slots[s], slots[s + 1]
-            packed = jnp.where(half, b, roll(a, 64)) if side == 0 else jnp.where(half, roll(b, 64), a)
-            pack_ref[side, s // 2] = dot(to, split(packed))
-    n = pack_ref.shape[1]
-    for s in range(n):
-        sa_ref[s] = jnp.where(even, pack_ref[0, s], pack_ref[1, s])
-        sb_ref[s] = jnp.where(even, pack_ref[1, s], pack_ref[0, s])
-    sa_ref[n] = cg_ref[...]
-    sb_ref[n] = cg_ref[...]
-
-
-def inner_kernel(pop_ref, nbr_ref, ifc_ref, solid_ref, outer_ref, obits_ref, cur_ref, bits_ref, code_ref, spread_ref, take_ref, mid_ref, *, count):
+
+    def load(q, r, t):
+        return tile_ref[q, r, :]
+
+    def put(t, bits):
+        bits_ref[...] = bits
+
+    for side in (0, 1):
+
+        @pl.when(position % 2 == 1 - side)
+        def _(side=side):
+            prepare_side(side, load, nbr_ref, solid, put, post_ref, send_ref, hot, absent, code, first, copies[0].wait)
+
+
+def inner_kernel(pop_ref, nbr_ref, ifc_ref, solid_ref, ahead_ref, abits_ref, cur_ref, outer_ref, bits_ref, code_ref, spread_ref, take_ref, send_ref, mid_ref, *, count):
     position = lax.axis_index("blk")
     blocks = solid_ref.shape[0]
     tiles = solid_ref.shape[1] // LANES
     first = position * blocks
     groups = blocks // 8
+    span = [slice(LANES * t, LANES * (t + 1)) for t in range(tiles)]
+    code = coarse_code(ifc_ref, position, count)
+    code_ref[...] = code
+    absent = absences(nbr_ref, ifc_ref)
+    hot = local_hots(nbr_ref, first)
+    solid = [solid_ref[:, span[t]] for t in range(tiles)]
+
+    def load(q, r, t):
+        return pop_ref[q, r, span[t]]
+
+    def put(t, bits):
+        bits_ref[:, span[t]] = bits
+
+    for side in (0, 1):
+
+        @pl.when(position % 2 == side)
+        def _(side=side):
+            prepare_side(side, load, nbr_ref, solid, put, outer_ref, send_ref, hot, absent, code, first)
+            outer_ref[1 - side] = ahead_ref[1 - side]
+            put(0 if side == 0 else tiles - 1, abits_ref[...])
 
     def step(i, carry):
         n, g = i // groups, i % groups
@@ -426,20 +455,13 @@
         return carry
 
     lax.fori_loop(0, groups * (tiles - 2), step, 0)
-    code_ref[...] = coarse_code(ifc_ref, position, count)
     for t, m in enumerate(spread_matrix(tiles)):
         spread_ref[t] = m
     cap = take_ref.shape[2] // 2
     take_ref[0] = take_rows(nbr_ref[0:1, :], first + blocks, blocks, cap)
     take_ref[1] = take_rows(nbr_ref[1:2, :], first - blocks, blocks, cap)
-    absent = absences(nbr_ref, ifc_ref)
-    hot = local_hots(nbr_ref, first)
-    span = [slice(LANES * t, LANES * (t + 1)) for t in range(tiles)]
-    solid = [solid_ref[:, span[t]] for t in range(tiles)]
-    bits_ref[:, span[0]] = obits_ref[1]
-    bits_ref[:, span[-1]] = obits_ref[0]
     for t in range(1, tiles - 1):
-        bits_ref[:, span[t]] = bounce_bits(t, solid, absent)
+        put(t, bounce_bits(t, solid, absent))
 
     def post(q, t):
         if t == 0:
@@ -451,22 +473,18 @@
         ghosts = gathers(q, x, hot, None, None)
         for t in range(tiles):
             cur_ref[q, :, span[t]] = pull(
-                q, t, x, ghosts, ghosts[0], hot, None, bits_ref[:, span[t]], post(OPP[q], t), pop_ref[q, :, span[t]]
+                q, t, x, ghosts, ghosts[0], bits_ref[:, span[t]], post(OPP[q], t), pop_ref[q, :, span[t]]
             )
 
 
-def patched(q):
-    return VEL[q][0] != 0 or VEL[q][1] < 0
-
-
-def current_kernel(cur_ref, outer_ref, code_ref, spread_ref, take_ref, cg_ref, ra_ref, rb_ref, now_ref, post_ref, fine_ref, ghost_ref, codes_ref, got_ref, *, count):
+def current_kernel(cur_ref, outer_ref, code_ref, spread_ref, take_ref, sb_ref, ra_ref, rb_ref, now_ref, post_ref, fine_ref, ghost_ref, codes_ref, got_ref, *, count):
     position = lax.axis_index("blk")
     blocks, cells = cur_ref.shape[1:]
     tiles = cells // LANES
     even = position % 2 == 0
     half, j, k = lanes(blocks)
     span = [slice(LANES * t, LANES * (t + 1)) for t in range(tiles)]
-    n = ra_ref.shape[0] - 1
+    n = ra_ref.shape[0]
 
     for s in range(n):
         got_ref[0, s] = dot(take_ref[0], split(jnp.where(even, ra_ref[s], rb_ref[s])))
@@ -487,7 +505,7 @@
     low_code = both_halves(from_prev(2 * n - 1), True)
     codes_ref[0] = up_code
     codes_ref[1] = low_code
-    near = jnp.where(even, ra_ref[n], rb_ref[n])
+    near = jnp.where(even, sb_ref[n + 1], rb_ref[n])
 
     rows = coarse_rows(code, both_halves(near, False), count)
     for t in range(tiles):
@@ -515,7 +533,7 @@
                 v = v + jnp.where(ok, roll(up[q] if ex < 0 else low[q], 64 + 8 * ey + ez), 0.0)
             now_ref[q, :, span[t]] = v
 
-    low_rows = coarse_rows(low_code, both_halves(cg_ref[...], False), count)
+    low_rows = coarse_rows(low_code, both_halves(sb_ref[n], False), count)
     low_fine = coarse_tile(low_rows, spread_ref[tiles])
     for q in range(Q):
         ex, ey, ez = VEL[q]
@@ -554,14 +572,33 @@
             fine_ref[s, :, span[t]] = v
 
 
-def final_kernel(now_ref, post_ref, fine_ref, half_ref, codes_ref, bits_ref, spread_ref, far_ref, nbr_ref, out_ref, buf_ref, ghost_ref, sem, *, count):
+def final_kernel(now_ref, post_ref, fine_ref, half_ref, codes_ref, bits_ref, spread_ref, rb_ref, relay_ref, nbr_ref, out_ref, buf_ref, ghost_ref, sem, *, count):
     position = lax.axis_index("blk")
     blocks, cells = bits_ref.shape
     tiles = cells // LANES
     first = position * blocks
     half, j, k = lanes(blocks)
     span = [slice(LANES * t, LANES * (t + 1)) for t in range(tiles)]
-    up_rows = coarse_rows(codes_ref[0], both_halves(far_ref[...], False), count)
+    hot = local_hots(nbr_ref, first)
+    copies = []
+
+    def emit(q, remote):
+        x = [post_ref[q, :, span[t]] for t in range(tiles)]
+        ghosts = gathers(q, x, hot, lambda s, t: fine_ref[s, :, span[t]], remote)
+        for t in range(tiles):
+            buf_ref[q, :, span[t]] = pull(
+                q, t, x, ghosts, ghosts[0], bits_ref[:, span[t]], post_ref[OPP[q], :, span[t]], now_ref[q, :, span[t]]
+            )
+        copy = pltpu.make_async_copy(buf_ref.at[q], out_ref.at[q], sem.at[q])
+        copy.start()
+        copies.append(copy)
+
+    for q in range(Q):
+        if VEL[q][0] == 0:
+            emit(q, None)
+    n = rb_ref.shape[0] - 2
+    far = jnp.where(position % 2 == 0, relay_ref[n], rb_ref[n + 1])
+    up_rows = coarse_rows(codes_ref[0], both_halves(far, False), count)
     up_fine = coarse_tile(up_rows, spread_ref[tiles])
     for q in range(Q):
         v = half_ref[q]
@@ -582,30 +619,16 @@
         return carry
 
     lax.fori_loop(0, blocks // 8, layer_step, 0)
-    hot = local_hots(nbr_ref, first)
     remote = {}
     for q in range(Q):
         if VEL[q][0]:
             there = codes_ref[0 if VEL[q][0] < 0 else 1] > 0.5
             remote[q] = jnp.where(there, ghost_ref[q], 0.0)
-    copies = []
     for q in range(Q):
-        x = [post_ref[q, :, span[t]] for t in range(tiles)]
-        ghosts = gathers(q, x, hot, lambda s, t: fine_ref[s, :, span[t]], remote)
-        for t in range(tiles):
-            buf_ref[q, :, span[t]] = pull(
-                q, t, x, ghosts, ghosts[0], hot, None, bits_ref[:, span[t]], post_ref[OPP[q], :, span[t]], now_ref[q, :, span[t]]
-            )
-        copy = pltpu.make_async_copy(buf_ref.at[q], out_ref.at[q], sem.at[q])
-        copy.start()
-        copies.append(copy)
+        if VEL[q][0]:
+            emit(q, remote)
     for copy in copies:
         copy.wait()
-
-
-def shifted(x, by):
-    n = lax.axis_size("blk")
-    return lax.ppermute(x, "blk", [(i, i + by) for i in range(n) if 0 <= i + by < n])
 
 
 def swapped(x, off):
@@ -628,48 +651,58 @@
     dense = pl.BlockSpec(memory_space=pltpu.VMEM)
     away = pl.BlockSpec(memory_space=pl.ANY)
     cap = blocks // 2
-    payload = pltpu.VMEM((11, cap, LANES), F32)
     room = pltpu.CompilerParams(vmem_limit_bytes=20 << 20)
-    outer, obits, cg, sa, sb = pl.pallas_call(
+    sides = pltpu.VMEM((2, Q, blocks, LANES), F32)
+    payload = pltpu.VMEM((10, cap, LANES), F32)
+    small = (nbr, ifc, solid)
+    far_co = swapped(co, 0)
+    outer = pl.pallas_call(
         outer_kernel,
         in_specs=[away] * 5,
-        out_shape=(
-            pltpu.VMEM((2, Q, blocks, LANES), F32),
-            pltpu.VMEM((2, blocks, LANES), I32),
-            pltpu.VMEM((cap, LANES), F32),
-            payload,
-            payload,
-        ),
+        out_shape=(sides, pltpu.VMEM((blocks, LANES), I32), pltpu.VMEM(co.shape, F32), payload),
         scratch_shapes=[
-            pltpu.VMEM((2, Q, blocks, LANES), F32),
-            pltpu.VMEM((2, 10, cap, LANES), F32),
-            *(pltpu.VMEM(a.shape, a.dtype) for a in (nbr, ifc, solid, co)),
-            pltpu.SemaphoreType.DMA((6,)),
+            pltpu.VMEM((Q, blocks, LANES), F32),
+            *(pltpu.VMEM(a.shape, a.dtype) for a in small),
+            pltpu.SemaphoreType.DMA((5,)),
         ],
+        compiler_params=pltpu.CompilerParams(vmem_limit_bytes=56 << 20),
+        cost_estimate=pl.CostEstimate(flops=20_000_000, bytes_accessed=1_000_000, transcendentals=0),
         name="outer",
-    )(pop, nbr, ifc, solid, co)
+    )
+    ahead, abits, co, part = outer(pop, *small, co)
+    sb = pl.pallas_call(
+        pack_kernel,
+        in_specs=[dense] * 3,
+        out_shape=pltpu.VMEM((12, cap, LANES), F32),
+        compiler_params=room,
+        name="pack",
+    )(held(part), held(co), held(far_co))
     rb = swapped(sb, 1)
-    far = shifted(cg, -2)
-    ra = swapped(sa, 0)
-    outer, obits = held(outer), held(obits)
-    cur, bits, code, spread, take = pl.pallas_call(
+    pop, nbr, ifc, solid, ahead = lax.optimization_barrier((pop, nbr, ifc, solid, ahead))
+    ahead, abits = held(ahead), held(abits)
+    inner = pl.pallas_call(
         functools.partial(inner_kernel, count=count),
         in_specs=[dense] * 6,
         out_shape=(
             pltpu.VMEM((Q, blocks, cells), F32),
+            sides,
             pltpu.VMEM((blocks, cells), I32),
             pltpu.VMEM((blocks, LANES), F32),
             pltpu.VMEM((tiles + 1, 256, LANES), BF16),
             pltpu.VMEM((2, blocks, 2 * cap), BF16),
+            payload,
         ),
+        scratch_shapes=[pltpu.VMEM((tiles - 2, Q, blocks, LANES), F32)],
         compiler_params=room,
-        scratch_shapes=[pltpu.VMEM((tiles - 2, Q, blocks, LANES), F32)],
         cost_estimate=pl.CostEstimate(flops=100_000_000, bytes_accessed=4_000_000, transcendentals=0),
         name="inner",
-    )(pop, nbr, ifc, solid, outer, obits)
+    )
+    cur, outer, bits, code, spread, take, sa = inner(pop, nbr, ifc, solid, ahead, abits)
+    ra = swapped(sa, 0)
+    relay = swapped(rb, 0)
     state = pltpu.VMEM((Q, blocks, cells), F32)
     layer = pltpu.VMEM((Q, blocks, LANES), F32)
-    now, post, fine, ghost, codes = pl.pallas_call(
+    current = pl.pallas_call(
         functools.partial(current_kernel, count=count),
         in_specs=[dense] * 8,
         out_shape=(state, state, pltpu.VMEM((5, blocks, cells), F32), layer, pltpu.VMEM((2, blocks, LANES), F32)),
@@ -677,16 +710,18 @@
         compiler_params=room,
         cost_estimate=pl.CostEstimate(flops=100_000_000, bytes_accessed=4_000_000, transcendentals=0),
         name="current",
-    )(*(held(x) for x in (cur, outer, code, spread, take, cg, ra, rb)))
+    )
+    given = [held(x) for x in (cur, outer, code, spread, take, sb, ra, rb)]
+    now, post, fine, ghost, codes = current(*given)
     out = pl.pallas_call(
         functools.partial(final_kernel, count=count),
-        in_specs=[dense] * 9,
+        in_specs=[dense] * 10,
         out_specs=away,
         out_shape=jax.ShapeDtypeStruct(pop.shape, F32),
         scratch_shapes=[state, layer, pltpu.SemaphoreType.DMA((Q,))],
         compiler_params=room,
         name="final",
-    )(*(held(x) for x in (now, post, fine, ghost, codes, bits, spread, far)), nbr)
+    )(*(held(x) for x in (now, post, fine, ghost, codes, bits, spread, rb, relay)), nbr)
     return out.transpose(1, 0, 2)
 
 

time: 16 us -> 18.3 us (1.14)
  the two profiles are of different devices: /device:TPU:25 before, /device:TPU:23 now
where the time goes in v4:
time: 18.3 us; the launch traced here: 18.1 us
  Pallas kernels  8.05 us (44%)
  waiting for transfers between devices  5.56 us (30%)
  starting transfers between devices  4.41 us (24%)
    ppermute x4, waiting for transfers between devices, swapped(): return lax.ppermute(x, 'blk', low + [(b, a) for a, b in low])  5.56 us
    ppermute x4, starting transfers between devices, swapped(): return lax.ppermute(x, 'blk', low + [(b, a) for a, b in low])  4.41 us
    pallas_call x1, Pallas kernels, body(): inner(pop, nbr, ifc, solid, ahead, abits)  2.4 us
    pallas_call x1, Pallas kernels, body(): pl.pallas_call(functools.partial(final_kernel, count=count), in_specs=[de...  1.99 us
    pallas_call x1, Pallas kernels, body(): ahead, abits, co, part = outer(pop, *small, co)  1.85 us
    pallas_call x1, Pallas kernels, body(): now, post, fine, ghost, codes = current(*given)  1.68 us
  transfers between devices with their start and end apart: 4, of which 2 were waited for; matrix products, arithmetic and copies ran while one was open for 0% of the time, Pallas kernels for 33%

profile of v4, /device:TPU:23, one launch (start us, length us, event | category | flops | bytes accessed | tf_op | source)
XLA Modules:
  0.0 18.1 jit_solution(12816522978028959046)
XLA Ops:
  0.0 0.0 copy-start
  0.0 0.0 copy-start.2
  0.0 0.0 copy-start.3
  0.0 0.0 copy-start.1
  0.0 0.7 %collective-permute-start = (f32[2,19,2,64]{3,2,1,0:T(2,128)}, f32[2,19,2,64]{3,2,1,0:T(2,128)S(1)}, u32[]{:S(2)}, u32[]{:S(2)}) collective-permute-start(f32[2,19,2,64]{3,2,1,0:T(2,128)} %bitcast.12), channel_id=1, source_target_pairs={{0,1},{2,3},{4,5},{6,7},{8,9},{10,11},{12,13},{14,15},{16,17},{18,... | collective-permute-start | bytes 58376 | tf_op jit(solution)/shard_map/ppermute | solution.py:637
  0.8 1.8 %outer.1 = (f32[2,19,32,128]{3,2,1,0:T(8,128)S(1)}, s32[32,128]{1,0:T(8,128)S(1)}, f32[2,19,2,64]{3,2,1,0:T(2,128)S(1)}, f32[10,16,128]{2,1,0:T(8,128)S(1)}) custom-call(f32[19,32,512]{2,1,0:T(8,128)} %bitcast.5, s32[6,32]{1,0:T(8,128)} %bitcast.7, s32[2,32]{1,0:T(2,128)} %bitcast.10, s32[32,512]{1,0:T(8,128)} %solid_ref, f32[2,19,2,64]{3,2,1,0:T(2,128)} %bitcast.13), custom_call_target="tpu_custom_call" | custom-call | flops 20000000 | bytes 1000000 | tf_op jit(solution)/shard_map/outer/pallas_call | solution.py:672
  2.6 0.0 collective-permute-done.far_co_ref
  2.6 0.1 pack.1.sb_ref
  2.8 3.1 %collective-permute-start.2 = (f32[12,16,128]{2,1,0:T(8,128)S(1)}, f32[12,16,128]{2,1,0:T(8,128)S(1)}, u32[]{:S(2)}, u32[]{:S(2)}) collective-permute-start(f32[12,16,128]{2,1,0:T(8,128)S(1)} %pack.1.sb_ref), channel_id=1, source_target_pairs={{1,2},{3,4},{5,6},{7,8},{9,10},{11,12},{13,14},{15,16},{17,18},{19... | collective-permute-start | bytes 294920 | tf_op jit(solution)/shard_map/ppermute | solution.py:637
  5.9 4.6 %collective-permute-done.2.rb_ref = f32[12,16,128]{2,1,0:T(8,128)S(1)} collective-permute-done((f32[12,16,128]{2,1,0:T(8,128)S(1)}, f32[12,16,128]{2,1,0:T(8,128)S(1)}, u32[]{:S(2)}, u32[]{:S(2)}) %collective-permute-start.2) | collective-permute-done | bytes 98336 | tf_op jit(solution)/shard_map/ppermute | solution.py:637
  10.5 0.0 collective-permute-start.3
  10.5 0.0 copy-done
  10.5 0.0 copy-done.2
  10.5 0.0 copy-done.3
  10.5 0.0 copy-done.1
  10.5 2.4 %inner.1 = (f32[19,32,512]{2,1,0:T(8,128)S(1)}, f32[2,19,32,128]{3,2,1,0:T(8,128)S(1)}, s32[32,512]{1,0:T(8,128)S(1)}, f32[32,128]{1,0:T(8,128)S(1)}, bf16[5,256...) custom-call(f32[19,32,512]{2,1,0:T(8,128)S(1)} %bitcast.6, ...), custom_call_target="tpu_custom_call" | custom-call | flops 100000000 | bytes 4000000 | tf_op jit(solution)/shard_map/inner/pallas_call | solution.py:700
  12.9 0.6 %collective-permute-start.1 = (f32[10,16,128]{2,1,0:T(8,128)S(1)}, f32[10,16,128]{2,1,0:T(8,128)S(1)}, u32[]{:S(2)}, u32[]{:S(2)}) collective-permute-start(f32[10,16,128]{2,1,0:T(8,128)S(1)} %get-tuple-element.40), channel_id=1, source_target_pairs={{0,1},{2,3},{4,5},{6,7},{8,9},{10,11},{12,13},{14,15},{16,17},{18,... | collective-permute-start | bytes 245768 | tf_op jit(solution)/shard_map/ppermute | solution.py:637
  13.5 0.9 %collective-permute-done.1.ra_ref = f32[10,16,128]{2,1,0:T(8,128)S(1)} collective-permute-done((f32[10,16,128]{2,1,0:T(8,128)S(1)}, f32[10,16,128]{2,1,0:T(8,128)S(1)}, u32[]{:S(2)}, u32[]{:S(2)}) %collective-permute-start.1) | collective-permute-done | bytes 81952 | tf_op jit(solution)/shard_map/ppermute | solution.py:637
  14.4 1.7 %current.1 = (f32[19,32,512]{2,1,0:T(8,128)S(1)}, f32[19,32,512]{2,1,0:T(8,128)S(1)}, f32[5,32,512]{2,1,0:T(8,128)S(1)}, f32[19,32,128]{2,1,0:T(8,128)S(1)}, f32[2,32,128]{2,1,0:T(8,128)S(1)}) custom-call(f32[19,32,512]{2,1,0:T(8,128)S(1)} %get-tuple-element.33.cur_ref, f32[2,19,32,128]{3,2,1,0:T(8,128)S(1)} %get-tuple-element.34.outer_ref, ...), custom_call_target="tpu_custom_call" | custom-call | flops 100000000 | bytes 4000000 | tf_op jit(solution)/shard_map/current/pallas_call | solution.py:715
  16.1 0.0 collective-permute-done.3.relay_ref
  16.1 2.0 %final.1 = f32[19,32,512]{2,1,0:T(8,128)} custom-call(f32[19,32,512]{2,1,0:T(8,128)S(1)} %get-tuple-element.41.now_ref, f32[19,32,512]{2,1,0:T(8,128)S(1)} %get-tuple-element.42.post_ref, f32[5,32,512]{2,1,0:T(8,128)S(1)} %get-tuple-element.43.fine_ref, f32[19,32,128]{2,1,0:T(8,128)S(1)} %get-tuple-element.44.half_ref, ...), custom_call_target="tpu_custom_call" | custom-call | tf_op jit(solution)/shard_map/final/pallas_call | solution.py:716
Async XLA Ops:
  0.0 10.5 %copy-start = (f32[32,19,512]{2,0,1:T(8,128)S(1)}, f32[32,19,512]{2,0,1:T(8,128)}, u32[]{:S(2)}) copy-start(f32[32,19,512]{2,0,1:T(8,128)} %param.5) | copy-start | bytes 3735556
  0.0 10.5 %copy-start.2 = (s32[32,6]{0,1:T(8,128)S(1)}, s32[32,6]{0,1:T(8,128)}, u32[]{:S(2)}) copy-start(s32[32,6]{0,1:T(8,128)} %param.7) | copy-start | bytes 2308
  0.0 10.5 %copy-start.3 = (s32[32,2]{0,1:T(2,128)S(1)}, s32[32,2]{0,1:T(2,128)}, u32[]{:S(2)}) copy-start(s32[32,2]{0,1:T(2,128)} %param.8) | copy-start | bytes 772
  0.0 10.5 %copy-start.1 = (s32[32,512]{1,0:T(8,128)S(1)}, s32[32,512]{1,0:T(8,128)}, u32[]{:S(2)}) copy-start(s32[32,512]{1,0:T(8,128)} %solid_ref) | copy-start | bytes 196612
  0.0 2.6 %collective-permute-start = (f32[2,19,2,64]{3,2,1,0:T(2,128)}, f32[2,19,2,64]{3,2,1,0:T(2,128)S(1)}, u32[]{:S(2)}, u32[]{:S(2)}) collective-permute-start(f32[2,19,2,64]{3,2,1,0:T(2,128)} %bitcast.12), channel_id=1, source_target_pairs={{0,1},{2,3},{4,5},{6,7},{8,9},{10,11},{12,13},{14,15},{16,17},{18,... | collective-permute-start | bytes 58376 | tf_op jit(solution)/shard_map/ppermute | solution.py:637
  2.8 7.7 %collective-permute-start.2 = (f32[12,16,128]{2,1,0:T(8,128)S(1)}, f32[12,16,128]{2,1,0:T(8,128)S(1)}, u32[]{:S(2)}, u32[]{:S(2)}) collective-permute-start(f32[12,16,128]{2,1,0:T(8,128)S(1)} %pack.1.sb_ref), channel_id=1, source_target_pairs={{1,2},{3,4},{5,6},{7,8},{9,10},{11,12},{13,14},{15,16},{17,18},{19... | collective-permute-start | bytes 294920 | tf_op jit(solution)/shard_map/ppermute | solution.py:637
  10.5 5.6 %collective-permute-start.3 = (f32[12,16,128]{2,1,0:T(8,128)S(1)}, f32[12,16,128]{2,1,0:T(8,128)S(1)}, u32[]{:S(2)}, u32[]{:S(2)}) collective-permute-start(f32[12,16,128]{2,1,0:T(8,128)S(1)} %collective-permute-done.2.rb_ref), channel_id=1, source_target_pairs={{0,1},{2,3},{4,5},{6,7},{8,9},{10,11},{12,13},{14,15},{16,17},{18,... | collective-permute-start | bytes 294920 | tf_op jit(solution)/shard_map/ppermute | solution.py:637
  12.9 1.5 %collective-permute-start.1 = (f32[10,16,128]{2,1,0:T(8,128)S(1)}, f32[10,16,128]{2,1,0:T(8,128)S(1)}, u32[]{:S(2)}, u32[]{:S(2)}) collective-permute-start(f32[10,16,128]{2,1,0:T(8,128)S(1)} %get-tuple-element.40), channel_id=1, source_target_pairs={{0,1},{2,3},{4,5},{6,7},{8,9},{10,11},{12,13},{14,15},{16,17},{18,... | collective-permute-start | bytes 245768 | tf_op jit(solution)/shard_map/ppermute | solution.py:637

commit v5 on v4

--- a/solution.py
+++ b/solution.py
@@ -238,7 +238,11 @@
     return spread_rows(code)
 
 
-def pack_kernel(part_ref, co_ref, far_co_ref, send_ref):
+def far_row(c, s, count):
+    return 5 * count + 5 * (c // 2) + s
+
+
+def pack_kernel(part_ref, co_ref, far_co_ref, send_ref, near_ref):
     refs = (co_ref, far_co_ref)
     count = co_ref.shape[0]
     n = part_ref.shape[0]
@@ -249,12 +253,19 @@
         h1 = (1.0 - 0.5) * h0 + 0.5 * jnp.concatenate([r[:, q, 1, :] for r in refs], axis=0)
         h.append(jnp.concatenate([h0, h1], axis=1))
     e = feq(h)
-    send_ref[n:] = jnp.zeros_like(send_ref[n:])
+    send_ref[n] = jnp.zeros_like(send_ref[n])
+    near_ref[...] = jnp.zeros_like(near_ref)
+    upper = lanes(1)[0]
     for s, q in enumerate(CROSSING[2]):
         v = e[q] + (0.6 / 1.1) * (h[q] - e[q])
-        for o in range(2):
-            for c in range(count):
-                send_ref[n + o, 5 * c + s : 5 * c + s + 1, :] = v[count * o + c : count * o + c + 1]
+        for c in range(count):
+            send_ref[n, 5 * c + s : 5 * c + s + 1, :] = v[c : c + 1]
+            near_ref[5 * c + s : 5 * c + s + 1, :] = v[count + c : count + c + 1]
+        turned = roll(v, 64)
+        for c in range(0, count, 2):
+            other = min(c + 1, count - 1)
+            to = far_row(c, s, count)
+            send_ref[n, to : to + 1, :] = jnp.where(upper, turned[count + other : count + other + 1], v[count + c : count + c + 1])
 
 
 def both_halves(x, upper):
@@ -274,6 +285,10 @@
     return out
 
 
+def rows_of(cg):
+    return lambda c, s: cg[5 * c + s : 5 * c + s + 1, :]
+
+
 def coarse_rows(code, cg, count):
     half = lanes(code.shape[0])[0]
     hi, lo = [], []
@@ -283,7 +298,7 @@
             acc = jnp.zeros_like(code)
             for c in range(count):
                 want = jnp.where(half, 3.0 + 4 * c + pair, 2.0 + 4 * c + pair)
-                acc = jnp.where(code == want, cg[5 * c + s : 5 * c + s + 1, :], acc)
+                acc = jnp.where(code == want, cg(c, s), acc)
             parts.append(acc)
         x = jnp.concatenate(parts, axis=1)
         h = x.astype(BF16)
@@ -342,6 +357,10 @@
     return [q for q in range(Q) if VEL[q][0] == e], [q for q in range(Q) if VEL[q][0] != -e]
 
 
+def groups(blocks):
+    return [slice(g, g + 8) for g in range(0, blocks, 8)]
+
+
 def prepare_side(side, load, nbr_ref, solid, bits_put, post_ref, send_ref, hot, absent, code, first, ready=None):
     tiles = len(solid)
     blocks = solid[0].shape[0]
@@ -352,14 +371,10 @@
     if ready is not None:
         ready()
 
-    def step(g, carry):
-        r = pl.ds(pl.multiple_of(8 * g, 8), 8)
+    for r in groups(blocks):
         out = collide([load(q, r, t) for q in range(Q)])
         for q in range(Q):
             post_ref[side, q, r, :] = out[q]
-        return carry
-
-    lax.fori_loop(0, blocks // 8, step, 0)
     to = send_rows(nbr_ref[side : side + 1, :], first + (blocks if side == 0 else -blocks), blocks, send_ref.shape[1])
     face, layer = side_slots(side)
     slots = [post_ref[side, q] for q in face]
@@ -423,7 +438,6 @@
     blocks = solid_ref.shape[0]
     tiles = solid_ref.shape[1] // LANES
     first = position * blocks
-    groups = blocks // 8
     span = [slice(LANES * t, LANES * (t + 1)) for t in range(tiles)]
     code = coarse_code(ifc_ref, position, count)
     code_ref[...] = code
@@ -437,24 +451,6 @@
     def put(t, bits):
         bits_ref[:, span[t]] = bits
 
-    for side in (0, 1):
-
-        @pl.when(position % 2 == side)
-        def _(side=side):
-            prepare_side(side, load, nbr_ref, solid, put, outer_ref, send_ref, hot, absent, code, first)
-            outer_ref[1 - side] = ahead_ref[1 - side]
-            put(0 if side == 0 else tiles - 1, abits_ref[...])
-
-    def step(i, carry):
-        n, g = i // groups, i % groups
-        r = pl.ds(pl.multiple_of(8 * g, 8), 8)
-        l = pl.ds(pl.multiple_of(LANES * (n + 1), LANES), LANES)
-        out = collide([pop_ref[q, r, l] for q in range(Q)])
-        for q in range(Q):
-            mid_ref[n, q, r, :] = out[q]
-        return carry
-
-    lax.fori_loop(0, groups * (tiles - 2), step, 0)
     for t, m in enumerate(spread_matrix(tiles)):
         spread_ref[t] = m
     cap = take_ref.shape[2] // 2
@@ -462,6 +458,19 @@
     take_ref[1] = take_rows(nbr_ref[1:2, :], first - blocks, blocks, cap)
     for t in range(1, tiles - 1):
         put(t, bounce_bits(t, solid, absent))
+    for side in (0, 1):
+
+        @pl.when(position % 2 == side)
+        def _(side=side):
+            prepare_side(side, load, nbr_ref, solid, put, outer_ref, send_ref, hot, absent, code, first)
+            outer_ref[1 - side] = ahead_ref[1 - side]
+            put(0 if side == 0 else tiles - 1, abits_ref[...])
+
+    for t in range(1, tiles - 1):
+        for r in groups(blocks):
+            out = collide([pop_ref[q, r, span[t]] for q in range(Q)])
+            for q in range(Q):
+                mid_ref[t - 1, q, r, :] = out[q]
 
     def post(q, t):
         if t == 0:
@@ -477,7 +486,7 @@
             )
 
 
-def current_kernel(cur_ref, outer_ref, code_ref, spread_ref, take_ref, sb_ref, ra_ref, rb_ref, now_ref, post_ref, fine_ref, ghost_ref, codes_ref, got_ref, *, count):
+def current_kernel(cur_ref, outer_ref, code_ref, spread_ref, take_ref, sb_ref, near_ref, ra_ref, rb_ref, now_ref, post_ref, fine_ref, ghost_ref, codes_ref, got_ref, *, count):
     position = lax.axis_index("blk")
     blocks, cells = cur_ref.shape[1:]
     tiles = cells // LANES
@@ -505,9 +514,9 @@
     low_code = both_halves(from_prev(2 * n - 1), True)
     codes_ref[0] = up_code
     codes_ref[1] = low_code
-    near = jnp.where(even, sb_ref[n + 1], rb_ref[n])
-
-    rows = coarse_rows(code, both_halves(near, False), count)
+    near = jnp.where(even, near_ref[...], rb_ref[n])
+
+    rows = coarse_rows(code, rows_of(both_halves(near, False)), count)
     for t in range(tiles):
         for s, v in enumerate(coarse_tile(rows, spread_ref[t])):
             fine_ref[s, :, span[t]] = v
@@ -533,7 +542,7 @@
                 v = v + jnp.where(ok, roll(up[q] if ex < 0 else low[q], 64 + 8 * ey + ez), 0.0)
             now_ref[q, :, span[t]] = v
 
-    low_rows = coarse_rows(low_code, both_halves(sb_ref[n], False), count)
+    low_rows = coarse_rows(low_code, rows_of(both_halves(sb_ref[n], False)), count)
     low_fine = coarse_tile(low_rows, spread_ref[tiles])
     for q in range(Q):
         ex, ey, ez = VEL[q]
@@ -556,17 +565,13 @@
             sides.append(v)
         ghost_ref[q] = jnp.where(half, sides[1], sides[0])
 
-    def step(i, carry):
-        r = pl.ds(pl.multiple_of(8 * (i // tiles), 8), 8)
-        l = pl.ds(pl.multiple_of(LANES * (i % tiles), LANES), LANES)
-        out = collide([now_ref[q, r, l] for q in range(Q)])
-        for q in range(Q):
-            post_ref[q, r, l] = out[q]
-        return carry
-
-    lax.fori_loop(0, blocks // 8 * tiles, step, 0)
-
-    rows = coarse_rows(code, both_halves(near, True), count)
+    for t in range(tiles):
+        for r in groups(blocks):
+            out = collide([now_ref[q, r, span[t]] for q in range(Q)])
+            for q in range(Q):
+                post_ref[q, r, span[t]] = out[q]
+
+    rows = coarse_rows(code, rows_of(both_halves(near, True)), count)
     for t in range(tiles):
         for s, v in enumerate(coarse_tile(rows, spread_ref[t])):
             fine_ref[s, :, span[t]] = v
@@ -596,9 +601,15 @@
     for q in range(Q):
         if VEL[q][0] == 0:
             emit(q, None)
-    n = rb_ref.shape[0] - 2
-    far = jnp.where(position % 2 == 0, relay_ref[n], rb_ref[n + 1])
-    up_rows = coarse_rows(codes_ref[0], both_halves(far, False), count)
+    n = rb_ref.shape[0] - 1
+    handed = rows_of(both_halves(relay_ref[n], False))
+    direct = [both_halves(rb_ref[n], u) for u in (False, True)]
+
+    def far(c, s):
+        row = far_row(c, s, count)
+        return jnp.where(position % 2 == 0, handed(c, s), direct[c % 2][row : row + 1])
+
+    up_rows = coarse_rows(codes_ref[0], far, count)
     up_fine = coarse_tile(up_rows, spread_ref[tiles])
     for q in range(Q):
         v = half_ref[q]
@@ -610,15 +621,11 @@
             v = v + jnp.where(ok, roll(up_fine[CROSSING[2].index(q)], VEL[q][2]), 0.0)
         ghost_ref[q] = v
 
-    def layer_step(g, carry):
-        r = pl.ds(pl.multiple_of(8 * g, 8), 8)
+    for r in groups(blocks):
         out = collide([ghost_ref[q, r, :] for q in range(Q)])
         for q in range(Q):
             if VEL[q][0]:
                 ghost_ref[q, r, :] = out[q]
-        return carry
-
-    lax.fori_loop(0, blocks // 8, layer_step, 0)
     remote = {}
     for q in range(Q):
         if VEL[q][0]:
@@ -670,15 +677,14 @@
         name="outer",
     )
     ahead, abits, co, part = outer(pop, *small, co)
-    sb = pl.pallas_call(
+    sb, near = pl.pallas_call(
         pack_kernel,
         in_specs=[dense] * 3,
-        out_shape=pltpu.VMEM((12, cap, LANES), F32),
+        out_shape=(pltpu.VMEM((11, cap, LANES), F32), pltpu.VMEM((cap, LANES), F32)),
         compiler_params=room,
         name="pack",
     )(held(part), held(co), held(far_co))
     rb = swapped(sb, 1)
-    pop, nbr, ifc, solid, ahead = lax.optimization_barrier((pop, nbr, ifc, solid, ahead))
     ahead, abits = held(ahead), held(abits)
     inner = pl.pallas_call(
         functools.partial(inner_kernel, count=count),
@@ -704,14 +710,14 @@
     layer = pltpu.VMEM((Q, blocks, LANES), F32)
     current = pl.pallas_call(
         functools.partial(current_kernel, count=count),
-        in_specs=[dense] * 8,
+        in_specs=[dense] * 9,
         out_shape=(state, state, pltpu.VMEM((5, blocks, cells), F32), layer, pltpu.VMEM((2, blocks, LANES), F32)),
         scratch_shapes=[pltpu.VMEM((2, 10, blocks, LANES), F32)],
         compiler_params=room,
         cost_estimate=pl.CostEstimate(flops=100_000_000, bytes_accessed=4_000_000, transcendentals=0),
         name="current",
     )
-    given = [held(x) for x in (cur, outer, code, spread, take, sb, ra, rb)]
+    given = [held(x) for x in (cur, outer, code, spread, take, sb, near, ra, rb)]
     now, post, fine, ghost, codes = current(*given)
     out = pl.pallas_call(
         functools.partial(final_kernel, count=count),

time: 18.3 us -> 13.8 us (0.75)
  waiting for transfers between devices: 5.56 us -> 2.61 us
  Pallas kernels: 8.05 us -> 6.99 us
  starting transfers between devices: 4.41 us -> 3.91 us
    ppermute x4, waiting for transfers between devices: 5.56 us -> 2.61 us  [swapped(): return lax.ppermute(x, 'blk', low + [(b, a) for a, b in low])]
    pallas_call x1, Pallas kernels: 1.68 us -> 1.05 us  [body(): now, post, fine, ghost, codes = current(*given)]
    ppermute x4, starting transfers between devices: 4.41 us -> 3.91 us  [swapped(): return lax.ppermute(x, 'blk', low + [(b, a) for a, b in low])]
    pallas_call x1, Pallas kernels: 2.4 us -> 2.03 us  [body(): inner(pop, nbr, ifc, solid, ahead, abits)]
  transfers between devices with their start and end apart: 4 -> 4, of which waited for: 2 -> 2; matrix products, arithmetic and copies ran while one was open for 0% -> 0% of each run, Pallas kernels for 33% -> 36%
where the time goes in v5:
time: 13.8 us; the launch traced here: 13.6 us
  Pallas kernels  6.99 us (51%)
  starting transfers between devices  3.91 us (28%)
  waiting for transfers between devices  2.61 us (19%)
    ppermute x4, starting transfers between devices, swapped(): return lax.ppermute(x, 'blk', low + [(b, a) for a, b in low])  3.91 us
    ppermute x4, waiting for transfers between devices, swapped(): return lax.ppermute(x, 'blk', low + [(b, a) for a, b in low])  2.61 us
    pallas_call x1, Pallas kernels, body(): inner(pop, nbr, ifc, solid, ahead, abits)  2.03 us
    pallas_call x1, Pallas kernels, body(): pl.pallas_call(functools.partial(final_kernel, count=count), in_specs=[de...  1.94 us
    pallas_call x1, Pallas kernels, body(): ahead, abits, co, part = outer(pop, *small, co)  1.76 us
    pallas_call x1, Pallas kernels, body(): now, post, fine, ghost, codes = current(*given)  1.05 us
  transfers between devices with their start and end apart: 4, of which 2 were waited for; matrix products, arithmetic and copies ran while one was open for 0% of the time, Pallas kernels for 36%

profile of v5, /device:TPU:23, one launch (start us, length us, event | category | flops | bytes accessed | tf_op | source)
XLA Modules:
  0.0 13.6 jit_solution(5940959420209706825)
XLA Ops:
  0.0 0.0 copy-start.2
  0.0 0.0 copy-start
  0.0 0.0 copy-start.3
  0.0 0.0 copy-start.1
  0.0 0.7 %collective-permute-start = (f32[2,19,2,64]{3,2,1,0:T(2,128)}, f32[2,19,2,64]{3,2,1,0:T(2,128)S(1)}, u32[]{:S(2)}, u32[]{:S(2)}) collective-permute-start(f32[2,19,2,64]{3,2,1,0:T(2,128)} %bitcast.12), channel_id=1, source_target_pairs={{0,1},{2,3},{4,5},{6,7},{8,9},{10,11},{12,13},{14,15},{16,17},{18,... | collective-permute-start | bytes 58376 | tf_op jit(solution)/shard_map/ppermute | solution.py:644
  0.8 1.8 %outer.1 = (f32[2,19,32,128]{3,2,1,0:T(8,128)S(1)}, s32[32,128]{1,0:T(8,128)S(1)}, f32[2,19,2,64]{3,2,1,0:T(2,128)S(1)}, f32[10,16,128]{2,1,0:T(8,128)S(1)}) custom-call(f32[19,32,512]{2,1,0:T(8,128)} %bitcast.5, s32[6,32]{1,0:T(8,128)} %bitcast.7, s32[2,32]{1,0:T(2,128)} %bitcast.10, s32[32,512]{1,0:T(8,128)} %solid_ref.1, f32[2,19,2,64]{3,2,1,0:T(2,128)} %bitcast.13), custom_call_target="tpu_custom_call" | custom-call | flops 20000000 | bytes 1000000 | tf_op jit(solution)/shard_map/outer/pallas_call | solution.py:679
  2.5 0.0 collective-permute-done.far_co_ref
  2.5 0.2 %pack.1 = (f32[11,16,128]{2,1,0:T(8,128)S(1)}, f32[16,128]{1,0:T(8,128)S(1)}) custom-call(f32[10,16,128]{2,1,0:T(8,128)S(1)} %get-tuple-element.30.part_ref, f32[2,19,2,64]{3,2,1,0:T(2,128)S(1)} %get-tuple-element.31.co_ref, f32[2,19,2,64]{3,2,1,0:T(2,128)S(1)} %collective-permute-done.far_co_ref), custom_call_target="tpu_custom_call" | custom-call | tf_op jit(solution)/shard_map/pack/pallas_call | solution.py:680
  2.7 3.1 %collective-permute-start.2 = (f32[11,16,128]{2,1,0:T(8,128)S(1)}, f32[11,16,128]{2,1,0:T(8,128)S(1)}, u32[]{:S(2)}, u32[]{:S(2)}) collective-permute-start(f32[11,16,128]{2,1,0:T(8,128)S(1)} %get-tuple-element.32.sb_ref), channel_id=1, source_target_pairs={{1,2},{3,4},{5,6},{7,8},{9,10},{11,12},{13,14},{15,16},{17,18},{19... | collective-permute-start | bytes 270344 | tf_op jit(solution)/shard_map/ppermute | solution.py:644
  5.8 0.0 copy-done.2
  5.9 0.0 copy-done
  5.9 0.0 copy-done.3
  5.9 0.0 copy-done.1
  5.9 2.0 %inner.1 = (f32[19,32,512]{2,1,0:T(8,128)S(1)}, f32[2,19,32,128]{3,2,1,0:T(8,128)S(1)}, s32[32,512]{1,0:T(8,128)S(1)}, f32[32,128]{1,0:T(8,128)S(1)}, bf16[5,256...) custom-call(f32[19,32,512]{2,1,0:T(8,128)S(1)} %bitcast.6, ...), custom_call_target="tpu_custom_call" | custom-call | flops 100000000 | bytes 4000000 | tf_op jit(solution)/shard_map/inner/pallas_call | solution.py:706
  7.9 0.1 collective-permute-start.1
  8.0 2.4 %collective-permute-done.2.rb_ref = f32[11,16,128]{2,1,0:T(8,128)S(1)} collective-permute-done((f32[11,16,128]{2,1,0:T(8,128)S(1)}, f32[11,16,128]{2,1,0:T(8,128)S(1)}, u32[]{:S(2)}, u32[]{:S(2)}) %collective-permute-start.2) | collective-permute-done | bytes 90144 | tf_op jit(solution)/shard_map/ppermute | solution.py:644
  10.4 0.0 collective-permute-start.3
  10.4 0.0 collective-permute-done.1.ra_ref
  10.4 1.1 %current.1 = (f32[19,32,512]{2,1,0:T(8,128)S(1)}, f32[19,32,512]{2,1,0:T(8,128)S(1)}, f32[5,32,512]{2,1,0:T(8,128)S(1)}, f32[19,32,128]{2,1,0:T(8,128)S(1)}, f32[2,32,128]{2,1,0:T(8,128)S(1)}) custom-call(f32[19,32,512]{2,1,0:T(8,128)S(1)} %get-tuple-element.25.cur_ref, f32[2,19,32,128]{3,2,1,0:T(8,128)S(1)} %get-tuple-element.26.outer_ref, ...), custom_call_target="tpu_custom_call" | custom-call | flops 100000000 | bytes 4000000 | tf_op jit(solution)/shard_map/current/pallas_call | solution.py:721
  11.4 0.2 %collective-permute-done.3.relay_ref = f32[11,16,128]{2,1,0:T(8,128)S(1)} collective-permute-done((f32[11,16,128]{2,1,0:T(8,128)S(1)}, f32[11,16,128]{2,1,0:T(8,128)S(1)}, u32[]{:S(2)}, u32[]{:S(2)}) %collective-permute-start.3) | collective-permute-done | bytes 90144 | tf_op jit(solution)/shard_map/ppermute | solution.py:644
  11.7 1.9 %final.1 = f32[19,32,512]{2,1,0:T(8,128)} custom-call(f32[19,32,512]{2,1,0:T(8,128)S(1)} %get-tuple-element.35.now_ref, f32[19,32,512]{2,1,0:T(8,128)S(1)} %get-tuple-element.36.post_ref, f32[5,32,512]{2,1,0:T(8,128)S(1)} %get-tuple-element.37.fine_ref, f32[19,32,128]{2,1,0:T(8,128)S(1)} %get-tuple-element.38.half_ref, ...), custom_call_target="tpu_custom_call" | custom-call | tf_op jit(solution)/shard_map/final/pallas_call | solution.py:722
Async XLA Ops:
  0.0 5.8 %copy-start.2 = (s32[32,6]{0,1:T(8,128)S(1)}, s32[32,6]{0,1:T(8,128)}, u32[]{:S(2)}) copy-start(s32[32,6]{0,1:T(8,128)} %param.7) | copy-start | bytes 2308
  0.0 5.9 %copy-start = (f32[32,19,512]{2,0,1:T(8,128)S(1)}, f32[32,19,512]{2,0,1:T(8,128)}, u32[]{:S(2)}) copy-start(f32[32,19,512]{2,0,1:T(8,128)} %param.5) | copy-start | bytes 3735556
  0.0 5.9 %copy-start.3 = (s32[32,2]{0,1:T(2,128)S(1)}, s32[32,2]{0,1:T(2,128)}, u32[]{:S(2)}) copy-start(s32[32,2]{0,1:T(2,128)} %param.8) | copy-start | bytes 772
  0.0 5.9 %copy-start.1 = (s32[32,512]{1,0:T(8,128)S(1)}, s32[32,512]{1,0:T(8,128)}, u32[]{:S(2)}) copy-start(s32[32,512]{1,0:T(8,128)} %solid_ref.1) | copy-start | bytes 196612
  0.0 2.5 %collective-permute-start = (f32[2,19,2,64]{3,2,1,0:T(2,128)}, f32[2,19,2,64]{3,2,1,0:T(2,128)S(1)}, u32[]{:S(2)}, u32[]{:S(2)}) collective-permute-start(f32[2,19,2,64]{3,2,1,0:T(2,128)} %bitcast.12), channel_id=1, source_target_pairs={{0,1},{2,3},{4,5},{6,7},{8,9},{10,11},{12,13},{14,15},{16,17},{18,... | collective-permute-start | bytes 58376 | tf_op jit(solution)/shard_map/ppermute | solution.py:644
  2.7 7.6 %collective-permute-start.2 = (f32[11,16,128]{2,1,0:T(8,128)S(1)}, f32[11,16,128]{2,1,0:T(8,128)S(1)}, u32[]{:S(2)}, u32[]{:S(2)}) collective-permute-start(f32[11,16,128]{2,1,0:T(8,128)S(1)} %get-tuple-element.32.sb_ref), channel_id=1, source_target_pairs={{1,2},{3,4},{5,6},{7,8},{9,10},{11,12},{13,14},{15,16},{17,18},{19... | collective-permute-start | bytes 270344 | tf_op jit(solution)/shard_map/ppermute | solution.py:644
  7.9 2.5 %collective-permute-start.1 = (f32[10,16,128]{2,1,0:T(8,128)S(1)}, f32[10,16,128]{2,1,0:T(8,128)S(1)}, u32[]{:S(2)}, u32[]{:S(2)}) collective-permute-start(f32[10,16,128]{2,1,0:T(8,128)S(1)} %get-tuple-element.34), channel_id=1, source_target_pairs={{0,1},{2,3},{4,5},{6,7},{8,9},{10,11},{12,13},{14,15},{16,17},{18,... | collective-permute-start | bytes 245768 | tf_op jit(solution)/shard_map/ppermute | solution.py:644
  10.4 1.3 %collective-permute-start.3 = (f32[11,16,128]{2,1,0:T(8,128)S(1)}, f32[11,16,128]{2,1,0:T(8,128)S(1)}, u32[]{:S(2)}, u32[]{:S(2)}) collective-permute-start(f32[11,16,128]{2,1,0:T(8,128)S(1)} %collective-permute-done.2.rb_ref), channel_id=1, source_target_pairs={{0,1},{2,3},{4,5},{6,7},{8,9},{10,11},{12,13},{14,15},{16,17},{18,... | collective-permute-start | bytes 270344 | tf_op jit(solution)/shard_map/ppermute | solution.py:644

commit v6 on v5

--- a/solution.py
+++ b/solution.py
@@ -25,7 +25,13 @@
 ]
 
 
-def rates():
+MIRROR = [VEL.index((-x, y, z)) for x, y, z in VEL]
+FACE = CROSSING[0]
+LAYER = [q for q in range(Q) if VEL[q][0] <= 0]
+MIXED = [q for q in LAYER if VEL[q][1] < 0]
+
+
+def moments():
     v = np.array(VEL) * 1.0
     x, y, z = v[:, 0], v[:, 1], v[:, 2]
     s = x * x + y * y + z * z
@@ -37,10 +43,72 @@
         x * y, y * z, x * z,
         (y * y - z * z) * x, (z * z - x * x) * y, (x * x - y * y) * z,
     ]
-    norms = (np.stack(rows) ** 2).sum(1)
+    return np.stack(rows)
+
+
+def rates():
+    norms = (moments() ** 2).sum(1)
     w = 1.0 / 0.6
     relax = np.array([0, 1.19, 1.4, 0, 1.2, 0, 1.2, 0, 1.2, w, 1.4, w, 1.4, w, w, w, 1.98, 1.98, 1.98])
     return [float(c) for c in relax / norms]
+
+
+def linear(p, items):
+    m = moments()
+    row = np.eye(Q)[p] - (m.T @ (np.array(rates())[:, None] * m))[p]
+    same = {}
+    for q, v in items:
+        if abs(row[q]) > 1e-12:
+            same.setdefault(round(abs(float(row[q])), 10), []).append((row[q] > 0, abs(float(row[q])), v))
+    total = None
+    for terms in same.values():
+        part = None
+        for plus, _, v in terms:
+            if part is None:
+                part = v if plus else -v
+            else:
+                part = part + v if plus else part - v
+        part = terms[0][1] * part
+        total = part if total is None else total + part
+    return total
+
+
+def shares(items):
+    out = [linear(p, items) for p in FACE]
+    total = None
+    for _, v in items:
+        total = v if total is None else total + v
+    out.append(total)
+    for axis in range(3):
+        total = None
+        for q, v in items:
+            if VEL[q][axis]:
+                v = v if VEL[q][axis] > 0 else -v
+                total = v if total is None else total + v
+        out.append(total)
+    return out
+
+
+def finish(parts):
+    c = rates()
+    rho, jx, jy, jz = parts[5:]
+    inv = 1.0 / rho
+    ux, uy, uz = jx * inv, jy * inv, jz * inv
+    xx, yy, zz = jx * ux, jy * uy, jz * uz
+    jj = xx + yy + zz
+    pe, we = 3 * xx - jj, yy - zz
+    r1, r2 = c[1] * (19 * jj - 11 * rho), c[2] * (3 * rho - 5.5 * jj)
+    r4, r6, r8 = (c[4] * -2 / 3) * jx, (c[6] * -2 / 3) * jy, (c[8] * -2 / 3) * jz
+    r13, r15 = c[13] * (jx * uy), c[15] * (jx * uz)
+    ea, eb = -11 * r1 - 4 * r2, 8 * r1 + r2
+    b9, b11 = (c[9] - 0.5 * c[10]) * pe, (c[11] - 0.5 * c[12]) * we
+    exy, exz = eb + b9 + b11, eb + b9 - b11
+    own = {
+        (-1, 0, 0): ea + (2 * (c[9] + c[10])) * pe + 4 * r4,
+        (-1, -1, 0): exy + r13 - (r4 + r6), (-1, 1, 0): exy - r13 - (r4 - r6),
+        (-1, 0, -1): exz + r15 - (r4 + r8), (-1, 0, 1): exz - r15 - (r4 - r8),
+    }
+    return {p: parts[i] + own[VEL[p]] for i, p in enumerate(FACE)}
 
 
 def collide(f):
@@ -352,9 +420,9 @@
     return gx, gy, gz
 
 
-def side_slots(d):
-    e = 1 if d == 0 else -1
-    return [q for q in range(Q) if VEL[q][0] == e], [q for q in range(Q) if VEL[q][0] != -e]
+def corners(q, half, j, k):
+    _, cy, cz = edges(q, 0, 0, half, j, k)
+    return cy if cz is None else (cz if cy is None else cy | cz)
 
 
 def groups(blocks):
@@ -376,9 +444,10 @@
         for q in range(Q):
             post_ref[side, q, r, :] = out[q]
     to = send_rows(nbr_ref[side : side + 1, :], first + (blocks if side == 0 else -blocks), blocks, send_ref.shape[1])
-    face, layer = side_slots(side)
-    slots = [post_ref[side, q] for q in face]
-    for q in layer:
+    actual = list(range(Q)) if side == 1 else MIRROR
+    streamed = []
+    for c in LAYER:
+        q = actual[c]
         ex, ey, ez = VEL[q]
         x = post_ref[side, q]
         turn = 64 * abs(ex)
@@ -392,10 +461,14 @@
             out = jnp.where(cz, roll(dot(hot[face_of(2, ez)], parts), turn + 8 * ey - 7 * ez), out)
         if q:
             out = jnp.where((bits & (1 << q)) != 0, post_ref[side, OPP[q]], out)
-        slots.append(out)
-    slots.append(code)
+        streamed.append((c, out))
+    for c in range(Q):
+        corner = corners(c, half, j, k)
+        if VEL[c][0] > 0 and corner is not None:
+            streamed.append((c, jnp.where(corner, post_ref[side, OPP[actual[c]]], 0.0)))
+    slots = [post_ref[side, actual[c]] for c in FACE] + shares(streamed) + [code]
     for s in range(0, len(slots), 2):
-        a, b = slots[s], slots[s + 1]
+        a, b = slots[s], slots[min(s + 1, len(slots) - 1)]
         packed = jnp.where(half, b, roll(a, 64)) if side == 0 else jnp.where(half, roll(b, 64), a)
         send_ref[s // 2] = dot(to, split(packed))
 
@@ -433,7 +506,7 @@
             prepare_side(side, load, nbr_ref, solid, put, post_ref, send_ref, hot, absent, code, first, copies[0].wait)
 
 
-def inner_kernel(pop_ref, nbr_ref, ifc_ref, solid_ref, ahead_ref, abits_ref, cur_ref, outer_ref, bits_ref, code_ref, spread_ref, take_ref, send_ref, mid_ref, *, count):
+def inner_kernel(pop_ref, nbr_ref, ifc_ref, solid_ref, ahead_ref, abits_ref, cur_ref, bits_ref, code_ref, spread_ref, take_ref, send_ref, own_ref, mid_ref, outer_ref, *, count):
     position = lax.axis_index("blk")
     blocks = solid_ref.shape[0]
     tiles = solid_ref.shape[1] // LANES
@@ -472,6 +545,17 @@
             for q in range(Q):
                 mid_ref[t - 1, q, r, :] = out[q]
 
+    half, j, k = lanes(blocks)
+    items = []
+    for q in range(Q):
+        if VEL[q][0] > 0:
+            turn = 64 + 8 * VEL[q][1] + VEL[q][2]
+            v = jnp.where(half, roll(outer_ref[1, MIRROR[q]], turn), roll(outer_ref[0, q], turn))
+            corner = corners(q, half, j, k)
+            items.append((q, v if corner is None else jnp.where(corner, 0.0, v)))
+    for i, v in enumerate(shares(items)):
+        own_ref[i] = v
+
     def post(q, t):
         if t == 0:
             return outer_ref[1, q]
@@ -486,7 +570,7 @@
             )
 
 
-def current_kernel(cur_ref, outer_ref, code_ref, spread_ref, take_ref, sb_ref, near_ref, ra_ref, rb_ref, now_ref, post_ref, fine_ref, ghost_ref, codes_ref, got_ref, *, count):
+def current_kernel(cur_ref, own_ref, code_ref, spread_ref, take_ref, near_ref, ra_ref, rb_ref, now_ref, post_ref, fine_ref, ghost_ref, codes_ref, got_ref, *, count):
     position = lax.axis_index("blk")
     blocks, cells = cur_ref.shape[1:]
     tiles = cells // LANES
@@ -505,13 +589,11 @@
     def from_prev(s):
         return got_ref[1, s // 2] if s % 2 == 1 else roll(got_ref[1, s // 2], 64)
 
-    up_face, up_layer = side_slots(1)
-    low_face, low_layer = side_slots(0)
-    up = {q: from_next(s) for s, q in enumerate(up_face)}
-    low = {q: from_prev(s) for s, q in enumerate(low_face)}
+    up = {q: from_next(s) for s, q in enumerate(FACE)}
+    low = {MIRROR[q]: from_prev(s) for s, q in enumerate(FACE)}
     code = code_ref[...]
-    up_code = both_halves(from_next(2 * n - 1), False)
-    low_code = both_halves(from_prev(2 * n - 1), True)
+    up_code = both_halves(from_next(14), False)
+    low_code = both_halves(from_prev(14), True)
     codes_ref[0] = up_code
     codes_ref[1] = low_code
     near = jnp.where(even, near_ref[...], rb_ref[n])
@@ -542,28 +624,8 @@
                 v = v + jnp.where(ok, roll(up[q] if ex < 0 else low[q], 64 + 8 * ey + ez), 0.0)
             now_ref[q, :, span[t]] = v
 
-    low_rows = coarse_rows(low_code, rows_of(both_halves(sb_ref[n], False)), count)
-    low_fine = coarse_tile(low_rows, spread_ref[tiles])
-    for q in range(Q):
-        ex, ey, ez = VEL[q]
-        _, cy, cz = edges(q, 0, tiles, half, j, k)
-        corner = cy if cz is None else (cz if cy is None else cy | cz)
-        sides = []
-        for e, layer, face, take, mine in (
-            (-1, up_layer, up, from_next, outer_ref.at[0]),
-            (1, low_layer, low, from_prev, outer_ref.at[1]),
-        ):
-            if ex == -e:
-                v = roll(mine[q], 64 + 8 * ey + ez)
-                if corner is not None:
-                    v = jnp.where(corner, face[OPP[q]], v)
-            else:
-                v = take(5 + layer.index(q))
-                if ey < 0 and e > 0:
-                    ok = cy if cz is None else cy & jnp.logical_not(cz)
-                    v = v + jnp.where(ok, roll(low_fine[CROSSING[2].index(q)], ez), 0.0)
-            sides.append(v)
-        ghost_ref[q] = jnp.where(half, sides[1], sides[0])
+    for i in range(9):
+        ghost_ref[i] = own_ref[i] + jnp.where(half, from_prev(5 + i), from_next(5 + i))
 
     for t in range(tiles):
         for r in groups(blocks):
@@ -577,7 +639,7 @@
             fine_ref[s, :, span[t]] = v
 
 
-def final_kernel(now_ref, post_ref, fine_ref, half_ref, codes_ref, bits_ref, spread_ref, rb_ref, relay_ref, nbr_ref, out_ref, buf_ref, ghost_ref, sem, *, count):
+def final_kernel(now_ref, post_ref, fine_ref, half_ref, codes_ref, bits_ref, spread_ref, sb_ref, rb_ref, relay_ref, nbr_ref, out_ref, buf_ref, sem, *, count):
     position = lax.axis_index("blk")
     blocks, cells = bits_ref.shape
     tiles = cells // LANES
@@ -611,26 +673,19 @@
 
     up_rows = coarse_rows(codes_ref[0], far, count)
     up_fine = coarse_tile(up_rows, spread_ref[tiles])
-    for q in range(Q):
-        v = half_ref[q]
-        if VEL[q][1] < 0 and VEL[q][0] <= 0:
-            _, cy, cz = edges(q, 0, tiles, half, j, k)
-            ok = cy & jnp.logical_not(half)
-            if cz is not None:
-                ok = ok & jnp.logical_not(cz)
-            v = v + jnp.where(ok, roll(up_fine[CROSSING[2].index(q)], VEL[q][2]), 0.0)
-        ghost_ref[q] = v
-
-    for r in groups(blocks):
-        out = collide([ghost_ref[q, r, :] for q in range(Q)])
-        for q in range(Q):
-            if VEL[q][0]:
-                ghost_ref[q, r, :] = out[q]
+    low_rows = coarse_rows(codes_ref[1], rows_of(both_halves(sb_ref[n], False)), count)
+    low_fine = coarse_tile(low_rows, spread_ref[tiles])
+    items = []
+    for q in MIXED:
+        _, cy, cz = edges(q, 0, tiles, half, j, k)
+        ok = cy if cz is None else cy & jnp.logical_not(cz)
+        v = jnp.where(half, low_fine[CROSSING[2].index(MIRROR[q])], up_fine[CROSSING[2].index(q)])
+        items.append((q, jnp.where(ok, roll(v, VEL[q][2]), 0.0)))
+    parts = [half_ref[i] + v for i, v in enumerate(shares(items))]
     remote = {}
-    for q in range(Q):
-        if VEL[q][0]:
-            there = codes_ref[0 if VEL[q][0] < 0 else 1] > 0.5
-            remote[q] = jnp.where(there, ghost_ref[q], 0.0)
+    for q, v in finish(parts).items():
+        remote[q] = jnp.where(codes_ref[0] > 0.5, v, 0.0)
+        remote[MIRROR[q]] = jnp.where(codes_ref[1] > 0.5, v, 0.0)
     for q in range(Q):
         if VEL[q][0]:
             emit(q, remote)
@@ -660,7 +715,7 @@
     cap = blocks // 2
     room = pltpu.CompilerParams(vmem_limit_bytes=20 << 20)
     sides = pltpu.VMEM((2, Q, blocks, LANES), F32)
-    payload = pltpu.VMEM((10, cap, LANES), F32)
+    payload = pltpu.VMEM((8, cap, LANES), F32)
     small = (nbr, ifc, solid)
     far_co = swapped(co, 0)
     outer = pl.pallas_call(
@@ -680,7 +735,7 @@
     sb, near = pl.pallas_call(
         pack_kernel,
         in_specs=[dense] * 3,
-        out_shape=(pltpu.VMEM((11, cap, LANES), F32), pltpu.VMEM((cap, LANES), F32)),
+        out_shape=(pltpu.VMEM((9, cap, LANES), F32), pltpu.VMEM((cap, LANES), F32)),
         compiler_params=room,
         name="pack",
     )(held(part), held(co), held(far_co))
@@ -691,43 +746,43 @@
         in_specs=[dense] * 6,
         out_shape=(
             pltpu.VMEM((Q, blocks, cells), F32),
-            sides,
             pltpu.VMEM((blocks, cells), I32),
             pltpu.VMEM((blocks, LANES), F32),
             pltpu.VMEM((tiles + 1, 256, LANES), BF16),
             pltpu.VMEM((2, blocks, 2 * cap), BF16),
             payload,
+            pltpu.VMEM((9, blocks, LANES), F32),
         ),
-        scratch_shapes=[pltpu.VMEM((tiles - 2, Q, blocks, LANES), F32)],
+        scratch_shapes=[pltpu.VMEM((tiles - 2, Q, blocks, LANES), F32), sides],
         compiler_params=room,
         cost_estimate=pl.CostEstimate(flops=100_000_000, bytes_accessed=4_000_000, transcendentals=0),
         name="inner",
     )
-    cur, outer, bits, code, spread, take, sa = inner(pop, nbr, ifc, solid, ahead, abits)
+    cur, bits, code, spread, take, sa, own = inner(pop, nbr, ifc, solid, ahead, abits)
     ra = swapped(sa, 0)
     relay = swapped(rb, 0)
     state = pltpu.VMEM((Q, blocks, cells), F32)
-    layer = pltpu.VMEM((Q, blocks, LANES), F32)
+    layer = pltpu.VMEM((9, blocks, LANES), F32)
     current = pl.pallas_call(
         functools.partial(current_kernel, count=count),
-        in_specs=[dense] * 9,
+        in_specs=[dense] * 8,
         out_shape=(state, state, pltpu.VMEM((5, blocks, cells), F32), layer, pltpu.VMEM((2, blocks, LANES), F32)),
-        scratch_shapes=[pltpu.VMEM((2, 10, blocks, LANES), F32)],
+        scratch_shapes=[pltpu.VMEM((2, 8, blocks, LANES), F32)],
         compiler_params=room,
         cost_estimate=pl.CostEstimate(flops=100_000_000, bytes_accessed=4_000_000, transcendentals=0),
         name="current",
     )
-    given = [held(x) for x in (cur, outer, code, spread, take, sb, near, ra, rb)]
+    given = [held(x) for x in (cur, own, code, spread, take, near, ra, rb)]
     now, post, fine, ghost, codes = current(*given)
     out = pl.pallas_call(
         functools.partial(final_kernel, count=count),
-        in_specs=[dense] * 10,
+        in_specs=[dense] * 11,
         out_specs=away,
         out_shape=jax.ShapeDtypeStruct(pop.shape, F32),
-        scratch_shapes=[state, layer, pltpu.SemaphoreType.DMA((Q,))],
+        scratch_shapes=[state, pltpu.SemaphoreType.DMA((Q,))],
         compiler_params=room,
         name="final",
-    )(*(held(x) for x in (now, post, fine, ghost, codes, bits, spread, rb, relay)), nbr)
+    )(*(held(x) for x in (now, post, fine, ghost, codes, bits, spread, sb, rb, relay)), nbr)
     return out.transpose(1, 0, 2)
 
 

time: 13.8 us -> 13.5 us (0.978)
  waiting for transfers between devices: 2.61 us -> 2.41 us
    ppermute x4, waiting for transfers between devices: 2.61 us -> 2.41 us  [swapped(): return lax.ppermute(x, 'blk', low + [(b, a) for a, b in low])]
where the time goes in v6:
time: 13.5 us; the launch traced here: 13.4 us
  Pallas kernels  6.91 us (51%)
  starting transfers between devices  3.93 us (29%)
  waiting for transfers between devices  2.41 us (18%)
    ppermute x4, starting transfers between devices, swapped(): return lax.ppermute(x, 'blk', low + [(b, a) for a, b in low])  3.93 us
    ppermute x4, waiting for transfers between devices, swapped(): return lax.ppermute(x, 'blk', low + [(b, a) for a, b in low])  2.41 us
    pallas_call x1, Pallas kernels, body(): inner(pop, nbr, ifc, solid, ahead, abits)  2.11 us
    pallas_call x1, Pallas kernels, body(): pl.pallas_call(functools.partial(final_kernel, count=count), in_specs=[de...  1.84 us
    pallas_call x1, Pallas kernels, body(): ahead, abits, co, part = outer(pop, *small, co)  1.8 us
    pallas_call x1, Pallas kernels, body(): now, post, fine, ghost, codes = current(*given)  0.96 us
  transfers between devices with their start and end apart: 4, of which 2 were waited for; matrix products, arithmetic and copies ran while one was open for 0% of the time, Pallas kernels for 36%

profile of v6, /device:TPU:23, one launch (start us, length us, event | category | flops | bytes accessed | tf_op | source)
XLA Modules:
  0.0 13.4 jit_solution(975155132631806335)
XLA Ops:
  0.0 0.0 copy-start.2
  0.0 0.0 copy-start
  0.0 0.0 copy-start.3
  0.0 0.0 copy-start.1
  0.0 0.7 %collective-permute-start = (f32[2,19,2,64]{3,2,1,0:T(2,128)}, f32[2,19,2,64]{3,2,1,0:T(2,128)S(1)}, u32[]{:S(2)}, u32[]{:S(2)}) collective-permute-start(f32[2,19,2,64]{3,2,1,0:T(2,128)} %bitcast.12), channel_id=1, source_target_pairs={{0,1},{2,3},{4,5},{6,7},{8,9},{10,11},{12,13},{14,15},{16,17},{18,... | collective-permute-start | bytes 58376 | tf_op jit(solution)/shard_map/ppermute | solution.py:699
  0.8 1.8 %outer.1 = (f32[2,19,32,128]{3,2,1,0:T(8,128)S(1)}, s32[32,128]{1,0:T(8,128)S(1)}, f32[2,19,2,64]{3,2,1,0:T(2,128)S(1)}, f32[8,16,128]{2,1,0:T(8,128)S(1)}) custom-call(f32[19,32,512]{2,1,0:T(8,128)} %bitcast.5, s32[6,32]{1,0:T(8,128)} %bitcast.7, s32[2,32]{1,0:T(2,128)} %bitcast.10, s32[32,512]{1,0:T(8,128)} %solid_ref.1, f32[2,19,2,64]{3,2,1,0:T(2,128)} %bitcast.13), custom_call_target="tpu_custom_call" | custom-call | flops 20000000 | bytes 1000000 | tf_op jit(solution)/shard_map/outer/pallas_call | solution.py:734
  2.6 0.0 collective-permute-done.far_co_ref
  2.6 0.2 %pack.1 = (f32[9,16,128]{2,1,0:T(8,128)S(1)}, f32[16,128]{1,0:T(8,128)S(1)}) custom-call(f32[8,16,128]{2,1,0:T(8,128)S(1)} %get-tuple-element.30.part_ref, f32[2,19,2,64]{3,2,1,0:T(2,128)S(1)} %get-tuple-element.31.co_ref, f32[2,19,2,64]{3,2,1,0:T(2,128)S(1)} %collective-permute-done.far_co_ref), custom_call_target="tpu_custom_call" | custom-call | tf_op jit(solution)/shard_map/pack/pallas_call | solution.py:735
  2.8 3.1 %collective-permute-start.2 = (f32[9,16,128]{2,1,0:T(8,128)S(1)}, f32[9,16,128]{2,1,0:T(8,128)S(1)}, u32[]{:S(2)}, u32[]{:S(2)}) collective-permute-start(f32[9,16,128]{2,1,0:T(8,128)S(1)} %get-tuple-element.34.sb_ref), channel_id=1, source_target_pairs={{1,2},{3,4},{5,6},{7,8},{9,10},{11,12},{13,14},{15,16},{17,18},{19... | collective-permute-start | bytes 221192 | tf_op jit(solution)/shard_map/ppermute | solution.py:699
  5.9 0.0 copy-done.2
  5.9 0.0 copy-done
  5.9 0.0 copy-done.3
  5.9 0.0 copy-done.1
  5.9 2.1 %inner.1 = (f32[19,32,512]{2,1,0:T(8,128)S(1)}, s32[32,512]{1,0:T(8,128)S(1)}, f32[32,128]{1,0:T(8,128)S(1)}, bf16[5,256,128]{2,1,0:T(8,128)(2,1)S(1)}, bf16[2,3...) custom-call(f32[19,32,512]{2,1,0:T(8,128)S(1)} %bitcast.6, s32[6,32]{1,0:T(8,128)S(1)} %bitcast.8, ...), custom_call_target="tpu_custom_call" | custom-call | flops 100000000 | bytes 4000000 | tf_op jit(solution)/shard_map/inner/pallas_call | solution.py:761
  8.1 0.1 collective-permute-start.1
  8.1 2.1 %collective-permute-done.2.rb_ref = f32[9,16,128]{2,1,0:T(8,128)S(1)} collective-permute-done((f32[9,16,128]{2,1,0:T(8,128)S(1)}, f32[9,16,128]{2,1,0:T(8,128)S(1)}, u32[]{:S(2)}, u32[]{:S(2)}) %collective-permute-start.2) | collective-permute-done | bytes 73760 | tf_op jit(solution)/shard_map/ppermute | solution.py:699
  10.2 0.0 collective-permute-start.3
  10.2 0.0 collective-permute-done.1.ra_ref
  10.2 1.0 %current.1 = (f32[19,32,512]{2,1,0:T(8,128)S(1)}, f32[19,32,512]{2,1,0:T(8,128)S(1)}, f32[5,32,512]{2,1,0:T(8,128)S(1)}, f32[9,32,128]{2,1,0:T(8,128)S(1)}, f32[2,32,128]{2,1,0:T(8,128)S(1)}) custom-call(f32[19,32,512]{2,1,0:T(8,128)S(1)} %get-tuple-element.25.cur_ref, f32[9,32,128]{2,1,0:T(8,128)S(1)} %get-tuple-element.26.own_ref, ...), custom_call_target="tpu_custom_call" | custom-call | flops 100000000 | bytes 4000000 | tf_op jit(solution)/shard_map/current/pallas_call | solution.py:776
  11.2 0.3 %collective-permute-done.3.relay_ref = f32[9,16,128]{2,1,0:T(8,128)S(1)} collective-permute-done((f32[9,16,128]{2,1,0:T(8,128)S(1)}, f32[9,16,128]{2,1,0:T(8,128)S(1)}, u32[]{:S(2)}, u32[]{:S(2)}) %collective-permute-start.3) | collective-permute-done | bytes 73760 | tf_op jit(solution)/shard_map/ppermute | solution.py:699
  11.5 1.8 %final.1 = f32[19,32,512]{2,1,0:T(8,128)} custom-call(f32[19,32,512]{2,1,0:T(8,128)S(1)} %get-tuple-element.35.now_ref, f32[19,32,512]{2,1,0:T(8,128)S(1)} %get-tuple-element.36.post_ref, f32[5,32,512]{2,1,0:T(8,128)S(1)} %get-tuple-element.37.fine_ref, f32[9,32,128]{2,1,0:T(8,128)S(1)} %get-tuple-element.38.half_ref, ...), custom_call_target="tpu_custom_call" | custom-call | tf_op jit(solution)/shard_map/final/pallas_call | solution.py:777
Async XLA Ops:
  0.0 5.9 %copy-start.2 = (s32[32,6]{0,1:T(8,128)S(1)}, s32[32,6]{0,1:T(8,128)}, u32[]{:S(2)}) copy-start(s32[32,6]{0,1:T(8,128)} %param.7) | copy-start | bytes 2308
  0.0 5.9 %copy-start = (f32[32,19,512]{2,0,1:T(8,128)S(1)}, f32[32,19,512]{2,0,1:T(8,128)}, u32[]{:S(2)}) copy-start(f32[32,19,512]{2,0,1:T(8,128)} %param.5) | copy-start | bytes 3735556
  0.0 5.9 %copy-start.3 = (s32[32,2]{0,1:T(2,128)S(1)}, s32[32,2]{0,1:T(2,128)}, u32[]{:S(2)}) copy-start(s32[32,2]{0,1:T(2,128)} %param.8) | copy-start | bytes 772
  0.0 5.9 %copy-start.1 = (s32[32,512]{1,0:T(8,128)S(1)}, s32[32,512]{1,0:T(8,128)}, u32[]{:S(2)}) copy-start(s32[32,512]{1,0:T(8,128)} %solid_ref.1) | copy-start | bytes 196612
  0.0 2.5 %collective-permute-start = (f32[2,19,2,64]{3,2,1,0:T(2,128)}, f32[2,19,2,64]{3,2,1,0:T(2,128)S(1)}, u32[]{:S(2)}, u32[]{:S(2)}) collective-permute-start(f32[2,19,2,64]{3,2,1,0:T(2,128)} %bitcast.12), channel_id=1, source_target_pairs={{0,1},{2,3},{4,5},{6,7},{8,9},{10,11},{12,13},{14,15},{16,17},{18,... | collective-permute-start | bytes 58376 | tf_op jit(solution)/shard_map/ppermute | solution.py:699
  2.8 7.5 %collective-permute-start.2 = (f32[9,16,128]{2,1,0:T(8,128)S(1)}, f32[9,16,128]{2,1,0:T(8,128)S(1)}, u32[]{:S(2)}, u32[]{:S(2)}) collective-permute-start(f32[9,16,128]{2,1,0:T(8,128)S(1)} %get-tuple-element.34.sb_ref), channel_id=1, source_target_pairs={{1,2},{3,4},{5,6},{7,8},{9,10},{11,12},{13,14},{15,16},{17,18},{19... | collective-permute-start | bytes 221192 | tf_op jit(solution)/shard_map/ppermute | solution.py:699
  8.1 2.2 %collective-permute-start.1 = (f32[8,16,128]{2,1,0:T(8,128)S(1)}, f32[8,16,128]{2,1,0:T(8,128)S(1)}, u32[]{:S(2)}, u32[]{:S(2)}) collective-permute-start(f32[8,16,128]{2,1,0:T(8,128)S(1)} %get-tuple-element.33), channel_id=1, source_target_pairs={{0,1},{2,3},{4,5},{6,7},{8,9},{10,11},{12,13},{14,15},{16,17},{18,... | collective-permute-start | bytes 196616 | tf_op jit(solution)/shard_map/ppermute | solution.py:699
  10.2 1.3 %collective-permute-start.3 = (f32[9,16,128]{2,1,0:T(8,128)S(1)}, f32[9,16,128]{2,1,0:T(8,128)S(1)}, u32[]{:S(2)}, u32[]{:S(2)}) collective-permute-start(f32[9,16,128]{2,1,0:T(8,128)S(1)} %collective-permute-done.2.rb_ref), channel_id=1, source_target_pairs={{0,1},{2,3},{4,5},{6,7},{8,9},{10,11},{12,13},{14,15},{16,17},{18,... | collective-permute-start | bytes 221192 | tf_op jit(solution)/shard_map/ppermute | solution.py:699

commit v7 on v6

--- a/solution.py
+++ b/solution.py
@@ -51,6 +51,11 @@
     w = 1.0 / 0.6
     relax = np.array([0, 1.19, 1.4, 0, 1.2, 0, 1.2, 0, 1.2, w, 1.4, w, 1.4, w, w, w, 1.98, 1.98, 1.98])
     return [float(c) for c in relax / norms]
+
+
+def kept(f, wall):
+    out = collide(f)
+    return [jnp.where(wall, f[OPP[q]], out[q]) for q in range(Q)]
 
 
 def linear(p, items):
@@ -247,7 +252,7 @@
 
 def bounce_bits(t, solid, absent):
     half, j, k = lanes(solid[0].shape[0])
-    acc = jnp.where(solid[t] != 0, 1, 0)
+    acc = jnp.where(solid[t] != 0, (1 << Q) - 1, 0)
     for q in range(1, Q):
         ex, ey, ez = VEL[q]
         v = roll(sources(q, t, solid, solid[t], half), 64 * abs(ex) + 8 * ey + ez)
@@ -383,9 +388,9 @@
     return [g[b * s : b * (s + 1)] for s in range(5)]
 
 
-def pull(q, t, x, parts, gx, bits, bounced, init):
+def pull(q, t, x, parts, gx, bits, bounced):
     if q == 0:
-        return jnp.where((bits & 1) != 0, init, x[t])
+        return x[t]
     half, j, k = lanes(bits.shape[0])
     ex, ey, ez = VEL[q]
     turn = 64 * abs(ex)
@@ -397,8 +402,7 @@
     if ez:
         g = parts[2]
         out = jnp.where(cz, roll(sources(q, t, g, g[t], half), turn + 8 * ey - 7 * ez), out)
-    out = jnp.where((bits & (1 << q)) != 0, bounced, out)
-    return jnp.where((bits & 1) != 0, init, out)
+    return jnp.where((bits & (1 << q)) != 0, bounced, out)
 
 
 def gathers(q, x, hot, fine, remote):
@@ -440,7 +444,7 @@
         ready()
 
     for r in groups(blocks):
-        out = collide([load(q, r, t) for q in range(Q)])
+        out = kept([load(q, r, t) for q in range(Q)], solid[t][r] != 0)
         for q in range(Q):
             post_ref[side, q, r, :] = out[q]
     to = send_rows(nbr_ref[side : side + 1, :], first + (blocks if side == 0 else -blocks), blocks, send_ref.shape[1])
@@ -506,7 +510,7 @@
             prepare_side(side, load, nbr_ref, solid, put, post_ref, send_ref, hot, absent, code, first, copies[0].wait)
 
 
-def inner_kernel(pop_ref, nbr_ref, ifc_ref, solid_ref, ahead_ref, abits_ref, cur_ref, bits_ref, code_ref, spread_ref, take_ref, send_ref, own_ref, mid_ref, outer_ref, *, count):
+def inner_kernel(pop_ref, nbr_ref, ifc_ref, solid_ref, ahead_ref, abits_ref, cur_ref, bits_ref, code_ref, spread_ref, take_ref, send_ref, own_ref, hot_ref, mid_ref, outer_ref, *, count):
     position = lax.axis_index("blk")
     blocks = solid_ref.shape[0]
     tiles = solid_ref.shape[1] // LANES
@@ -541,10 +545,12 @@
 
     for t in range(1, tiles - 1):
         for r in groups(blocks):
-            out = collide([pop_ref[q, r, span[t]] for q in range(Q)])
+            out = kept([pop_ref[q, r, span[t]] for q in range(Q)], solid[t][r] != 0)
             for q in range(Q):
                 mid_ref[t - 1, q, r, :] = out[q]
 
+    for d in range(6):
+        hot_ref[d] = hot[d]
     half, j, k = lanes(blocks)
     items = []
     for q in range(Q):
@@ -566,11 +572,11 @@
         ghosts = gathers(q, x, hot, None, None)
         for t in range(tiles):
             cur_ref[q, :, span[t]] = pull(
-                q, t, x, ghosts, ghosts[0], bits_ref[:, span[t]], post(OPP[q], t), pop_ref[q, :, span[t]]
+                q, t, x, ghosts, ghosts[0], bits_ref[:, span[t]], post(OPP[q], t)
             )
 
 
-def current_kernel(cur_ref, own_ref, code_ref, spread_ref, take_ref, near_ref, ra_ref, rb_ref, now_ref, post_ref, fine_ref, ghost_ref, codes_ref, got_ref, *, count):
+def current_kernel(cur_ref, own_ref, code_ref, spread_ref, take_ref, near_ref, bits_ref, ra_ref, rb_ref, post_ref, fine_ref, ghost_ref, codes_ref, got_ref, now_ref, *, count):
     position = lax.axis_index("blk")
     blocks, cells = cur_ref.shape[1:]
     tiles = cells // LANES
@@ -629,7 +635,7 @@
 
     for t in range(tiles):
         for r in groups(blocks):
-            out = collide([now_ref[q, r, span[t]] for q in range(Q)])
+            out = kept([now_ref[q, r, span[t]] for q in range(Q)], (bits_ref[r, span[t]] & 1) != 0)
             for q in range(Q):
                 post_ref[q, r, span[t]] = out[q]
 
@@ -639,14 +645,13 @@
             fine_ref[s, :, span[t]] = v
 
 
-def final_kernel(now_ref, post_ref, fine_ref, half_ref, codes_ref, bits_ref, spread_ref, sb_ref, rb_ref, relay_ref, nbr_ref, out_ref, buf_ref, sem, *, count):
+def final_kernel(post_ref, fine_ref, half_ref, codes_ref, bits_ref, spread_ref, sb_ref, rb_ref, relay_ref, hot_ref, out_ref, buf_ref, sem, *, count):
     position = lax.axis_index("blk")
     blocks, cells = bits_ref.shape
     tiles = cells // LANES
-    first = position * blocks
     half, j, k = lanes(blocks)
     span = [slice(LANES * t, LANES * (t + 1)) for t in range(tiles)]
-    hot = local_hots(nbr_ref, first)
+    hot = [hot_ref[d] for d in range(6)]
     copies = []
 
     def emit(q, remote):
@@ -654,7 +659,7 @@
         ghosts = gathers(q, x, hot, lambda s, t: fine_ref[s, :, span[t]], remote)
         for t in range(tiles):
             buf_ref[q, :, span[t]] = pull(
-                q, t, x, ghosts, ghosts[0], bits_ref[:, span[t]], post_ref[OPP[q], :, span[t]], now_ref[q, :, span[t]]
+                q, t, x, ghosts, ghosts[0], bits_ref[:, span[t]], post_ref[OPP[q], :, span[t]]
             )
         copy = pltpu.make_async_copy(buf_ref.at[q], out_ref.at[q], sem.at[q])
         copy.start()
@@ -664,7 +669,7 @@
         if VEL[q][0] == 0:
             emit(q, None)
     n = rb_ref.shape[0] - 1
-    handed = rows_of(both_halves(relay_ref[n], False))
+    handed = rows_of(both_halves(relay_ref[0], False))
     direct = [both_halves(rb_ref[n], u) for u in (False, True)]
 
     def far(c, s):
@@ -752,37 +757,38 @@
             pltpu.VMEM((2, blocks, 2 * cap), BF16),
             payload,
             pltpu.VMEM((9, blocks, LANES), F32),
+            pltpu.VMEM((6, blocks, 2 * blocks), BF16),
         ),
         scratch_shapes=[pltpu.VMEM((tiles - 2, Q, blocks, LANES), F32), sides],
         compiler_params=room,
         cost_estimate=pl.CostEstimate(flops=100_000_000, bytes_accessed=4_000_000, transcendentals=0),
         name="inner",
     )
-    cur, bits, code, spread, take, sa, own = inner(pop, nbr, ifc, solid, ahead, abits)
+    cur, bits, code, spread, take, sa, own, hots = inner(pop, nbr, ifc, solid, ahead, abits)
     ra = swapped(sa, 0)
-    relay = swapped(rb, 0)
+    relay = swapped(rb[-1:], 0)
     state = pltpu.VMEM((Q, blocks, cells), F32)
     layer = pltpu.VMEM((9, blocks, LANES), F32)
     current = pl.pallas_call(
         functools.partial(current_kernel, count=count),
-        in_specs=[dense] * 8,
-        out_shape=(state, state, pltpu.VMEM((5, blocks, cells), F32), layer, pltpu.VMEM((2, blocks, LANES), F32)),
-        scratch_shapes=[pltpu.VMEM((2, 8, blocks, LANES), F32)],
+        in_specs=[dense] * 9,
+        out_shape=(state, pltpu.VMEM((5, blocks, cells), F32), layer, pltpu.VMEM((2, blocks, LANES), F32)),
+        scratch_shapes=[pltpu.VMEM((2, 8, blocks, LANES), F32), state],
         compiler_params=room,
         cost_estimate=pl.CostEstimate(flops=100_000_000, bytes_accessed=4_000_000, transcendentals=0),
         name="current",
     )
-    given = [held(x) for x in (cur, own, code, spread, take, near, ra, rb)]
-    now, post, fine, ghost, codes = current(*given)
+    given = [held(x) for x in (cur, own, code, spread, take, near, bits, ra, rb)]
+    post, fine, ghost, codes = current(*given)
     out = pl.pallas_call(
         functools.partial(final_kernel, count=count),
-        in_specs=[dense] * 11,
+        in_specs=[dense] * 10,
         out_specs=away,
         out_shape=jax.ShapeDtypeStruct(pop.shape, F32),
         scratch_shapes=[state, pltpu.SemaphoreType.DMA((Q,))],
         compiler_params=room,
         name="final",
-    )(*(held(x) for x in (now, post, fine, ghost, codes, bits, spread, sb, rb, relay)), nbr)
+    )(*(held(x) for x in (post, fine, ghost, codes, bits, spread, sb, rb, relay, hots)))
     return out.transpose(1, 0, 2)
 
 

time: 13.5 us -> 13.3 us (0.985)
  transfers between devices with their start and end apart: 4 -> 4, of which waited for: 2 -> 2; matrix products, arithmetic and copies ran while one was open for 0% -> 0% of each run, Pallas kernels for 36% -> 37%
where the time goes in v7:
time: 13.3 us; the launch traced here: 13.2 us
  Pallas kernels  6.81 us (51%)
  starting transfers between devices  3.92 us (29%)
  waiting for transfers between devices  2.32 us (17%)
    ppermute x4, starting transfers between devices, swapped(): return lax.ppermute(x, 'blk', low + [(b, a) for a, b in low])  3.92 us
    ppermute x4, waiting for transfers between devices, swapped(): return lax.ppermute(x, 'blk', low + [(b, a) for a, b in low])  2.32 us
    pallas_call x1, Pallas kernels, body(): inner(pop, nbr, ifc, solid, ahead, abits)  2.09 us
    pallas_call x1, Pallas kernels, body(): ahead, abits, co, part = outer(pop, *small, co)  1.8 us
    pallas_call x1, Pallas kernels, body(): pl.pallas_call(functools.partial(final_kernel, count=count), in_specs=[de...  1.75 us
    pallas_call x1, Pallas kernels, body(): post, fine, ghost, codes = current(*given)  0.98 us
  transfers between devices with their start and end apart: 4, of which 2 were waited for; matrix products, arithmetic and copies ran while one was open for 0% of the time, Pallas kernels for 37%

profile of v7, /device:TPU:23, one launch (start us, length us, event | category | flops | bytes accessed | tf_op | source)
XLA Modules:
  0.0 13.2 jit_solution(5689134411453607971)
XLA Ops:
  0.0 0.0 copy-start
  0.0 0.0 copy-start.2
  0.0 0.0 copy-start.3
  0.0 0.0 copy-start.1
  0.0 0.7 %collective-permute-start = (f32[2,19,2,64]{3,2,1,0:T(2,128)}, f32[2,19,2,64]{3,2,1,0:T(2,128)S(1)}, u32[]{:S(2)}, u32[]{:S(2)}) collective-permute-start(f32[2,19,2,64]{3,2,1,0:T(2,128)} %bitcast.11), channel_id=1, source_target_pairs={{0,1},{2,3},{4,5},{6,7},{8,9},{10,11},{12,13},{14,15},{16,17},{18,... | collective-permute-start | bytes 58376 | tf_op jit(solution)/shard_map/ppermute | solution.py:704
  0.8 1.8 %outer.1 = (f32[2,19,32,128]{3,2,1,0:T(8,128)S(1)}, s32[32,128]{1,0:T(8,128)S(1)}, f32[2,19,2,64]{3,2,1,0:T(2,128)S(1)}, f32[8,16,128]{2,1,0:T(8,128)S(1)}) custom-call(f32[19,32,512]{2,1,0:T(8,128)} %bitcast.5, s32[6,32]{1,0:T(8,128)} %bitcast.7, s32[2,32]{1,0:T(2,128)} %bitcast.9, s32[32,512]{1,0:T(8,128)} %solid_ref.1, f32[2,19,2,64]{3,2,1,0:T(2,128)} %bitcast.12), custom_call_target="tpu_custom_call" | custom-call | flops 20000000 | bytes 1000000 | tf_op jit(solution)/shard_map/outer/pallas_call | solution.py:739
  2.6 0.0 collective-permute-done.far_co_ref
  2.6 0.2 %pack.1 = (f32[9,16,128]{2,1,0:T(8,128)S(1)}, f32[16,128]{1,0:T(8,128)S(1)}) custom-call(f32[8,16,128]{2,1,0:T(8,128)S(1)} %get-tuple-element.30.part_ref, f32[2,19,2,64]{3,2,1,0:T(2,128)S(1)} %get-tuple-element.31.co_ref, f32[2,19,2,64]{3,2,1,0:T(2,128)S(1)} %collective-permute-done.far_co_ref), custom_call_target="tpu_custom_call" | custom-call | tf_op jit(solution)/shard_map/pack/pallas_call | solution.py:740
  2.8 3.1 %collective-permute-start.2 = (f32[9,16,128]{2,1,0:T(8,128)S(1)}, f32[9,16,128]{2,1,0:T(8,128)S(1)}, u32[]{:S(2)}, u32[]{:S(2)}) collective-permute-start(f32[9,16,128]{2,1,0:T(8,128)S(1)} %get-tuple-element.35.sb_ref), channel_id=1, source_target_pairs={{1,2},{3,4},{5,6},{7,8},{9,10},{11,12},{13,14},{15,16},{17,18},{19... | collective-permute-start | bytes 221192 | tf_op jit(solution)/shard_map/ppermute | solution.py:704
  5.9 0.0 copy-done
  5.9 0.0 copy-done.2
  5.9 0.0 copy-done.3
  5.9 0.0 copy-done.1
  5.9 2.1 %inner.1 = (f32[19,32,512]{2,1,0:T(8,128)S(1)}, s32[32,512]{1,0:T(8,128)S(1)}, f32[32,128]{1,0:T(8,128)S(1)}, bf16[5,256,128]{2,1,0:T(8,128)(2,1)S(1)}, bf16[2,3...) custom-call(f32[19,32,512]{2,1,0:T(8,128)S(1)} %bitcast.6, ...), custom_call_target="tpu_custom_call" | custom-call | flops 100000000 | bytes 4000000 | tf_op jit(solution)/shard_map/inner/pallas_call | solution.py:767
  8.0 0.1 collective-permute-start.1
  8.1 2.1 %collective-permute-done.2.rb_ref = f32[9,16,128]{2,1,0:T(8,128)S(1)} collective-permute-done((f32[9,16,128]{2,1,0:T(8,128)S(1)}, f32[9,16,128]{2,1,0:T(8,128)S(1)}, u32[]{:S(2)}, u32[]{:S(2)}) %collective-permute-start.2) | collective-permute-done | bytes 73760 | tf_op jit(solution)/shard_map/ppermute | solution.py:704
  10.2 0.0 collective-permute-start.3
  10.3 0.0 collective-permute-done.1.ra_ref
  10.3 1.0 %current.1 = (f32[19,32,512]{2,1,0:T(8,128)S(1)}, f32[5,32,512]{2,1,0:T(8,128)S(1)}, f32[9,32,128]{2,1,0:T(8,128)S(1)}, f32[2,32,128]{2,1,0:T(8,128)S(1)}) custom-call(f32[19,32,512]{2,1,0:T(8,128)S(1)} %get-tuple-element.25.cur_ref, f32[9,32,128]{2,1,0:T(8,128)S(1)} %get-tuple-element.26.own_ref, f32[32,128]{1,0:T(8,128)S(1)} %get-tuple-element.27.code_ref, ...), custom_call_target="tpu_custom_call" | custom-call | flops 100000000 | bytes 4000000 | tf_op jit(solution)/shard_map/current/pallas_call | solution.py:782
  11.2 0.2 %collective-permute-done.3.relay_ref = f32[1,16,128]{2,1,0:T(8,128)S(1)} collective-permute-done((f32[1,16,128]{2,1,0:T(8,128)S(1)}, f32[1,16,128]{2,1,0:T(8,128)S(1)}, u32[]{:S(2)}, u32[]{:S(2)}) %collective-permute-start.3) | collective-permute-done | bytes 8224 | tf_op jit(solution)/shard_map/ppermute | solution.py:704
  11.4 1.7 %final.1 = f32[19,32,512]{2,1,0:T(8,128)} custom-call(f32[19,32,512]{2,1,0:T(8,128)S(1)} %get-tuple-element.36.post_ref, f32[5,32,512]{2,1,0:T(8,128)S(1)} %get-tuple-element.37.fine_ref, f32[9,32,128]{2,1,0:T(8,128)S(1)} %get-tuple-element.38.half_ref, f32[2,32,128]{2,1,0:T(8,128)S(1)} %get-tuple-element.39.codes_ref, ...), custom_call_target="tpu_custom_call" | custom-call | tf_op jit(solution)/shard_map/final/pallas_call | solution.py:783
  (1 shorter events, 0.0 us)
Async XLA Ops:
  0.0 5.9 %copy-start = (f32[32,19,512]{2,0,1:T(8,128)S(1)}, f32[32,19,512]{2,0,1:T(8,128)}, u32[]{:S(2)}) copy-start(f32[32,19,512]{2,0,1:T(8,128)} %param.5) | copy-start | bytes 3735556
  0.0 5.9 %copy-start.2 = (s32[32,6]{0,1:T(8,128)S(1)}, s32[32,6]{0,1:T(8,128)}, u32[]{:S(2)}) copy-start(s32[32,6]{0,1:T(8,128)} %param.7) | copy-start | bytes 2308
  0.0 5.9 %copy-start.3 = (s32[32,2]{0,1:T(2,128)S(1)}, s32[32,2]{0,1:T(2,128)}, u32[]{:S(2)}) copy-start(s32[32,2]{0,1:T(2,128)} %param.8) | copy-start | bytes 772
  0.0 5.9 %copy-start.1 = (s32[32,512]{1,0:T(8,128)S(1)}, s32[32,512]{1,0:T(8,128)}, u32[]{:S(2)}) copy-start(s32[32,512]{1,0:T(8,128)} %solid_ref.1) | copy-start | bytes 196612
  0.0 2.6 %collective-permute-start = (f32[2,19,2,64]{3,2,1,0:T(2,128)}, f32[2,19,2,64]{3,2,1,0:T(2,128)S(1)}, u32[]{:S(2)}, u32[]{:S(2)}) collective-permute-start(f32[2,19,2,64]{3,2,1,0:T(2,128)} %bitcast.11), channel_id=1, source_target_pairs={{0,1},{2,3},{4,5},{6,7},{8,9},{10,11},{12,13},{14,15},{16,17},{18,... | collective-permute-start | bytes 58376 | tf_op jit(solution)/shard_map/ppermute | solution.py:704
  2.8 7.5 %collective-permute-start.2 = (f32[9,16,128]{2,1,0:T(8,128)S(1)}, f32[9,16,128]{2,1,0:T(8,128)S(1)}, u32[]{:S(2)}, u32[]{:S(2)}) collective-permute-start(f32[9,16,128]{2,1,0:T(8,128)S(1)} %get-tuple-element.35.sb_ref), channel_id=1, source_target_pairs={{1,2},{3,4},{5,6},{7,8},{9,10},{11,12},{13,14},{15,16},{17,18},{19... | collective-permute-start | bytes 221192 | tf_op jit(solution)/shard_map/ppermute | solution.py:704
  8.0 2.2 %collective-permute-start.1 = (f32[8,16,128]{2,1,0:T(8,128)S(1)}, f32[8,16,128]{2,1,0:T(8,128)S(1)}, u32[]{:S(2)}, u32[]{:S(2)}) collective-permute-start(f32[8,16,128]{2,1,0:T(8,128)S(1)} %get-tuple-element.34), channel_id=1, source_target_pairs={{0,1},{2,3},{4,5},{6,7},{8,9},{10,11},{12,13},{14,15},{16,17},{18,... | collective-permute-start | bytes 196616 | tf_op jit(solution)/shard_map/ppermute | solution.py:704
  10.2 1.2 %collective-permute-start.3 = (f32[1,16,128]{2,1,0:T(8,128)S(1)}, f32[1,16,128]{2,1,0:T(8,128)S(1)}, u32[]{:S(2)}, u32[]{:S(2)}) collective-permute-start(f32[1,16,128]{2,1,0:T(8,128)S(1)} %slice.4), channel_id=1, source_target_pairs={{0,1},{2,3},{4,5},{6,7},{8,9},{10,11},{12,13},{14,15},{16,17},{18,... | collective-permute-start | bytes 24584 | tf_op jit(solution)/shard_map/ppermute | solution.py:704

commit v8 on v7

--- a/solution.py
+++ b/solution.py
@@ -28,6 +28,7 @@
 MIRROR = [VEL.index((-x, y, z)) for x, y, z in VEL]
 FACE = CROSSING[0]
 LAYER = [q for q in range(Q) if VEL[q][0] <= 0]
+CODED = VEL.index((-1, -1, 0))
 MIXED = [q for q in LAYER if VEL[q][1] < 0]
 
 
@@ -169,7 +170,7 @@
     rho = h[0]
     for q in range(1, Q):
         rho = rho + h[q]
-    safe = jnp.where(rho > 0, rho, 1.0)
+    inv = 1.0 / jnp.where(rho > 0, rho, 1.0)
     u = []
     for axis in range(3):
         m = None
@@ -177,7 +178,7 @@
             if VEL[q][axis]:
                 t = h[q] if VEL[q][axis] > 0 else -h[q]
                 m = t if m is None else m + t
-        u.append(m / safe)
+        u.append(m * inv)
     sq = u[0] * u[0] + u[1] * u[1] + u[2] * u[2]
     out = {}
     for q in CROSSING[2]:
@@ -470,7 +471,9 @@
         corner = corners(c, half, j, k)
         if VEL[c][0] > 0 and corner is not None:
             streamed.append((c, jnp.where(corner, post_ref[side, OPP[actual[c]]], 0.0)))
-    slots = [post_ref[side, actual[c]] for c in FACE] + shares(streamed) + [code]
+    faces = [post_ref[side, actual[c]] for c in FACE]
+    faces[FACE.index(CODED)] = jnp.where(j == 0, code, faces[FACE.index(CODED)])
+    slots = faces + shares(streamed)
     for s in range(0, len(slots), 2):
         a, b = slots[s], slots[min(s + 1, len(slots) - 1)]
         packed = jnp.where(half, b, roll(a, 64)) if side == 0 else jnp.where(half, roll(b, 64), a)
@@ -598,8 +601,8 @@
     up = {q: from_next(s) for s, q in enumerate(FACE)}
     low = {MIRROR[q]: from_prev(s) for s, q in enumerate(FACE)}
     code = code_ref[...]
-    up_code = both_halves(from_next(14), False)
-    low_code = both_halves(from_prev(14), True)
+    up_code = jnp.broadcast_to(up[CODED][:, 0:1], code.shape)
+    low_code = jnp.broadcast_to(low[MIRROR[CODED]][:, 64:65], code.shape)
     codes_ref[0] = up_code
     codes_ref[1] = low_code
     near = jnp.where(even, near_ref[...], rb_ref[n])
@@ -720,7 +723,7 @@
     cap = blocks // 2
     room = pltpu.CompilerParams(vmem_limit_bytes=20 << 20)
     sides = pltpu.VMEM((2, Q, blocks, LANES), F32)
-    payload = pltpu.VMEM((8, cap, LANES), F32)
+    payload = pltpu.VMEM((7, cap, LANES), F32)
     small = (nbr, ifc, solid)
     far_co = swapped(co, 0)
     outer = pl.pallas_call(
@@ -740,7 +743,7 @@
     sb, near = pl.pallas_call(
         pack_kernel,
         in_specs=[dense] * 3,
-        out_shape=(pltpu.VMEM((9, cap, LANES), F32), pltpu.VMEM((cap, LANES), F32)),
+        out_shape=(pltpu.VMEM((8, cap, LANES), F32), pltpu.VMEM((cap, LANES), F32)),
         compiler_params=room,
         name="pack",
     )(held(part), held(co), held(far_co))
@@ -773,7 +776,7 @@
         functools.partial(current_kernel, count=count),
         in_specs=[dense] * 9,
         out_shape=(state, pltpu.VMEM((5, blocks, cells), F32), layer, pltpu.VMEM((2, blocks, LANES), F32)),
-        scratch_shapes=[pltpu.VMEM((2, 8, blocks, LANES), F32), state],
+        scratch_shapes=[pltpu.VMEM((2, 7, blocks, LANES), F32), state],
         compiler_params=room,
         cost_estimate=pl.CostEstimate(flops=100_000_000, bytes_accessed=4_000_000, transcendentals=0),
         name="current",

time: 13.3 us -> 13.2 us (level)
  no operation moved by 1% of the time
where the time goes in v8:
time: 13.2 us; the launch traced here: 13.1 us
  Pallas kernels  6.75 us (51%)
  starting transfers between devices  3.91 us (30%)
  waiting for transfers between devices  2.28 us (17%)
    ppermute x4, starting transfers between devices, swapped(): return lax.ppermute(x, 'blk', low + [(b, a) for a, b in low])  3.91 us
    ppermute x4, waiting for transfers between devices, swapped(): return lax.ppermute(x, 'blk', low + [(b, a) for a, b in low])  2.28 us
    pallas_call x1, Pallas kernels, body(): inner(pop, nbr, ifc, solid, ahead, abits)  2.04 us
    pallas_call x1, Pallas kernels, body(): ahead, abits, co, part = outer(pop, *small, co)  1.8 us
    pallas_call x1, Pallas kernels, body(): pl.pallas_call(functools.partial(final_kernel, count=count), in_specs=[de...  1.72 us
    pallas_call x1, Pallas kernels, body(): post, fine, ghost, codes = current(*given)  0.98 us
  transfers between devices with their start and end apart: 4, of which 2 were waited for; matrix products, arithmetic and copies ran while one was open for 0% of the time, Pallas kernels for 37%

profile of v8, /device:TPU:23, one launch (start us, length us, event | category | flops | bytes accessed | tf_op | source)
XLA Modules:
  0.0 13.1 jit_solution(3031048031842956367)
XLA Ops:
  0.0 0.0 copy-start
  0.0 0.0 copy-start.2
  0.0 0.0 copy-start.3
  0.0 0.0 copy-start.1
  0.0 0.7 %collective-permute-start = (f32[2,19,2,64]{3,2,1,0:T(2,128)}, f32[2,19,2,64]{3,2,1,0:T(2,128)S(1)}, u32[]{:S(2)}, u32[]{:S(2)}) collective-permute-start(f32[2,19,2,64]{3,2,1,0:T(2,128)} %bitcast.11), channel_id=1, source_target_pairs={{0,1},{2,3},{4,5},{6,7},{8,9},{10,11},{12,13},{14,15},{16,17},{18,... | collective-permute-start | bytes 58376 | tf_op jit(solution)/shard_map/ppermute | solution.py:707
  0.8 1.8 %outer.1 = (f32[2,19,32,128]{3,2,1,0:T(8,128)S(1)}, s32[32,128]{1,0:T(8,128)S(1)}, f32[2,19,2,64]{3,2,1,0:T(2,128)S(1)}, f32[7,16,128]{2,1,0:T(8,128)S(1)}) custom-call(f32[19,32,512]{2,1,0:T(8,128)} %bitcast.5, s32[6,32]{1,0:T(8,128)} %bitcast.7, s32[2,32]{1,0:T(2,128)} %bitcast.9, s32[32,512]{1,0:T(8,128)} %solid_ref.1, f32[2,19,2,64]{3,2,1,0:T(2,128)} %bitcast.12), custom_call_target="tpu_custom_call" | custom-call | flops 20000000 | bytes 1000000 | tf_op jit(solution)/shard_map/outer/pallas_call | solution.py:742
  2.6 0.0 collective-permute-done.far_co_ref
  2.6 0.2 %pack.1 = (f32[8,16,128]{2,1,0:T(8,128)S(1)}, f32[16,128]{1,0:T(8,128)S(1)}) custom-call(f32[7,16,128]{2,1,0:T(8,128)S(1)} %get-tuple-element.30.part_ref, f32[2,19,2,64]{3,2,1,0:T(2,128)S(1)} %get-tuple-element.31.co_ref, f32[2,19,2,64]{3,2,1,0:T(2,128)S(1)} %collective-permute-done.far_co_ref), custom_call_target="tpu_custom_call" | custom-call | tf_op jit(solution)/shard_map/pack/pallas_call | solution.py:743
  2.8 3.1 %collective-permute-start.2 = (f32[8,16,128]{2,1,0:T(8,128)S(1)}, f32[8,16,128]{2,1,0:T(8,128)S(1)}, u32[]{:S(2)}, u32[]{:S(2)}) collective-permute-start(f32[8,16,128]{2,1,0:T(8,128)S(1)} %get-tuple-element.35.sb_ref), channel_id=1, source_target_pairs={{1,2},{3,4},{5,6},{7,8},{9,10},{11,12},{13,14},{15,16},{17,18},{19... | collective-permute-start | bytes 196616 | tf_op jit(solution)/shard_map/ppermute | solution.py:707
  5.9 0.0 copy-done
  5.9 0.0 copy-done.2
  5.9 0.0 copy-done.3
  5.9 0.0 copy-done.1
  5.9 2.0 %inner.1 = (f32[19,32,512]{2,1,0:T(8,128)S(1)}, s32[32,512]{1,0:T(8,128)S(1)}, f32[32,128]{1,0:T(8,128)S(1)}, bf16[5,256,128]{2,1,0:T(8,128)(2,1)S(1)}, bf16[2,3...) custom-call(f32[19,32,512]{2,1,0:T(8,128)S(1)} %bitcast.6, ...), custom_call_target="tpu_custom_call" | custom-call | flops 100000000 | bytes 4000000 | tf_op jit(solution)/shard_map/inner/pallas_call | solution.py:770
  8.0 0.1 collective-permute-start.1
  8.1 2.1 %collective-permute-done.2.rb_ref = f32[8,16,128]{2,1,0:T(8,128)S(1)} collective-permute-done((f32[8,16,128]{2,1,0:T(8,128)S(1)}, f32[8,16,128]{2,1,0:T(8,128)S(1)}, u32[]{:S(2)}, u32[]{:S(2)}) %collective-permute-start.2) | collective-permute-done | bytes 65568 | tf_op jit(solution)/shard_map/ppermute | solution.py:707
  10.2 0.0 collective-permute-start.3
  10.2 0.0 collective-permute-done.1.ra_ref
  10.2 1.0 %current.1 = (f32[19,32,512]{2,1,0:T(8,128)S(1)}, f32[5,32,512]{2,1,0:T(8,128)S(1)}, f32[9,32,128]{2,1,0:T(8,128)S(1)}, f32[2,32,128]{2,1,0:T(8,128)S(1)}) custom-call(f32[19,32,512]{2,1,0:T(8,128)S(1)} %get-tuple-element.25.cur_ref, f32[9,32,128]{2,1,0:T(8,128)S(1)} %get-tuple-element.26.own_ref, f32[32,128]{1,0:T(8,128)S(1)} %get-tuple-element.27.code_ref, ...), custom_call_target="tpu_custom_call" | custom-call | flops 100000000 | bytes 4000000 | tf_op jit(solution)/shard_map/current/pallas_call | solution.py:785
  11.2 0.2 %collective-permute-done.3.relay_ref = f32[1,16,128]{2,1,0:T(8,128)S(1)} collective-permute-done((f32[1,16,128]{2,1,0:T(8,128)S(1)}, f32[1,16,128]{2,1,0:T(8,128)S(1)}, u32[]{:S(2)}, u32[]{:S(2)}) %collective-permute-start.3) | collective-permute-done | bytes 8224 | tf_op jit(solution)/shard_map/ppermute | solution.py:707
  11.3 1.7 %final.1 = f32[19,32,512]{2,1,0:T(8,128)} custom-call(f32[19,32,512]{2,1,0:T(8,128)S(1)} %get-tuple-element.36.post_ref, f32[5,32,512]{2,1,0:T(8,128)S(1)} %get-tuple-element.37.fine_ref, f32[9,32,128]{2,1,0:T(8,128)S(1)} %get-tuple-element.38.half_ref, f32[2,32,128]{2,1,0:T(8,128)S(1)} %get-tuple-element.39.codes_ref, ...), custom_call_target="tpu_custom_call" | custom-call | tf_op jit(solution)/shard_map/final/pallas_call | solution.py:786
  (1 shorter events, 0.0 us)
Async XLA Ops:
  0.0 5.9 %copy-start = (f32[32,19,512]{2,0,1:T(8,128)S(1)}, f32[32,19,512]{2,0,1:T(8,128)}, u32[]{:S(2)}) copy-start(f32[32,19,512]{2,0,1:T(8,128)} %param.5) | copy-start | bytes 3735556
  0.0 5.9 %copy-start.2 = (s32[32,6]{0,1:T(8,128)S(1)}, s32[32,6]{0,1:T(8,128)}, u32[]{:S(2)}) copy-start(s32[32,6]{0,1:T(8,128)} %param.7) | copy-start | bytes 2308
  0.0 5.9 %copy-start.3 = (s32[32,2]{0,1:T(2,128)S(1)}, s32[32,2]{0,1:T(2,128)}, u32[]{:S(2)}) copy-start(s32[32,2]{0,1:T(2,128)} %param.8) | copy-start | bytes 772
  0.0 5.9 %copy-start.1 = (s32[32,512]{1,0:T(8,128)S(1)}, s32[32,512]{1,0:T(8,128)}, u32[]{:S(2)}) copy-start(s32[32,512]{1,0:T(8,128)} %solid_ref.1) | copy-start | bytes 196612
  0.0 2.6 %collective-permute-start = (f32[2,19,2,64]{3,2,1,0:T(2,128)}, f32[2,19,2,64]{3,2,1,0:T(2,128)S(1)}, u32[]{:S(2)}, u32[]{:S(2)}) collective-permute-start(f32[2,19,2,64]{3,2,1,0:T(2,128)} %bitcast.11), channel_id=1, source_target_pairs={{0,1},{2,3},{4,5},{6,7},{8,9},{10,11},{12,13},{14,15},{16,17},{18,... | collective-permute-start | bytes 58376 | tf_op jit(solution)/shard_map/ppermute | solution.py:707
  2.8 7.4 %collective-permute-start.2 = (f32[8,16,128]{2,1,0:T(8,128)S(1)}, f32[8,16,128]{2,1,0:T(8,128)S(1)}, u32[]{:S(2)}, u32[]{:S(2)}) collective-permute-start(f32[8,16,128]{2,1,0:T(8,128)S(1)} %get-tuple-element.35.sb_ref), channel_id=1, source_target_pairs={{1,2},{3,4},{5,6},{7,8},{9,10},{11,12},{13,14},{15,16},{17,18},{19... | collective-permute-start | bytes 196616 | tf_op jit(solution)/shard_map/ppermute | solution.py:707
  8.0 2.2 %collective-permute-start.1 = (f32[7,16,128]{2,1,0:T(8,128)S(1)}, f32[7,16,128]{2,1,0:T(8,128)S(1)}, u32[]{:S(2)}, u32[]{:S(2)}) collective-permute-start(f32[7,16,128]{2,1,0:T(8,128)S(1)} %get-tuple-element.34), channel_id=1, source_target_pairs={{0,1},{2,3},{4,5},{6,7},{8,9},{10,11},{12,13},{14,15},{16,17},{18,... | collective-permute-start | bytes 172040 | tf_op jit(solution)/shard_map/ppermute | solution.py:707
  10.2 1.2 %collective-permute-start.3 = (f32[1,16,128]{2,1,0:T(8,128)S(1)}, f32[1,16,128]{2,1,0:T(8,128)S(1)}, u32[]{:S(2)}, u32[]{:S(2)}) collective-permute-start(f32[1,16,128]{2,1,0:T(8,128)S(1)} %slice.4), channel_id=1, source_target_pairs={{0,1},{2,3},{4,5},{6,7},{8,9},{10,11},{12,13},{14,15},{16,17},{18,... | collective-permute-start | bytes 24584 | tf_op jit(solution)/shard_map/ppermute | solution.py:707
